TPU v7x, 128 devices: a whole 4x4x4 slice. The times are simulated.
128 devices in a mesh: lon: 32 (over x_lo, y, z), lat: 4 (over x_hi, core).
Axes of the slice: x: 4 (x_hi: 2, x_lo: 2; x = x_hi * 2 + x_lo), y: 4, z: 4, core: 2. Of those that a mesh axis runs over, the one named last changes fastest.
Arguments:
- ocean_state: bfloat16 [320, 1024, 128], P('lat', 'lon'), may hold values from -6 to 6
- land_sea: int32 [320, 1024], P('lat', 'lon'), may hold values 0 or 1
- kernel: bfloat16 [7, 7, 128], replicated, may hold values from -0.875 to 0.875
- conv_bias: float32 [128], replicated, may hold values from -3 to 3
- norm_gain: float32 [128], replicated, may hold values from 0.5 to 1.5
- norm_bias: float32 [128], replicated, may hold values from -3 to 3
- w_expand: bfloat16 [128, 512], replicated, may hold values from -0.5 to 0.5
- b_expand: float32 [512], replicated, may hold values from -3 to 3
- w_reduce: bfloat16 [512, 128], replicated, may hold values from -0.25 to 0.25
- b_reduce: float32 [128], replicated, may hold values from -3 to 3
- layer_scale: float32 [128], replicated, may hold values from 0.3 to 1
- cotangent: bfloat16 [320, 1024, 128], P('lat', 'lon'), may hold values from -6 to 6
Outputs:
- result: bfloat16 [320, 1024, 128], P('lat', 'lon')
- state_grad: bfloat16 [320, 1024, 128], P('lat', 'lon')
All inputs are finite; a program needn't handle non-finite values. No bound on the sum of `land_sea` on one device may be relied on, other than what follows from the above.
Results may differ from a plain program's by a relative error of at most 0.0037.
Values may be sent and summed in bfloat16 or wider, within the bound.
A program may use at most 192 MiB of HBM per device.

v0:
```python
import jax
import jax.numpy as jnp
from jax import lax
from jax.sharding import PartitionSpec as P


def for_sending(value):
    return jax.tree.map(lambda a: a.astype(jnp.bfloat16) if a.dtype == jnp.float32 else a, value)


def shifted(block, axis, distance):
    devices = range(lax.axis_size(axis))
    route = [((i - distance) % len(devices), i) for i in devices]
    return lax.ppermute(block, axis, route)


def from_behind(value, axis, steps):
    count = lax.axis_size(axis)
    leading, last = (max(0, -steps), min(count, count - steps))
    return lax.ppermute(value, axis, [(source, source + steps) for source in range(leading, last)])


def extended_2(block, sides, width):
    for axis, dim in sides:
        count = lax.axis_size(axis)
        forward = [(i, i + 1) for i in range(count - 1)]
        forward.append((count - 1, 0))
        backward = [(target, source) for source, target in forward]
        low = lax.ppermute(
            lax.slice_in_dim(block, block.shape[dim] - width, None, axis=dim), axis, forward
        )
        high = lax.ppermute(lax.slice_in_dim(block, 0, width, axis=dim), axis, backward)
        block = jnp.concatenate([low, block, high], axis=dim)
    return block


def gelu_value(values):
    return 0.5 * values * (1.0 + lax.erf(values * 0.7071067811865476))


def gelu_slope(values):
    cumulative = 0.5 * (1.0 + lax.erf(values * 0.7071067811865476))
    return cumulative + values * jnp.exp(-0.5 * values * values) * 0.3989422804014327


def depthwise(padded, kernel, conv_bias):
    out_rows = padded.shape[0] - 6
    out_cols = padded.shape[1] - 6
    summed = jnp.zeros((out_rows, out_cols, padded.shape[2]), jnp.float32) + conv_bias
    for row_tap in range(7):
        for col_tap in range(7):
            window = padded[row_tap : row_tap + out_rows, col_tap : col_tap + out_cols]
            summed = summed + kernel[row_tap, col_tap].astype(jnp.float32) * window
    return summed


def pointwise(
    conv_out,
    ocean_state,
    keep_mask,
    cotangent,
    norm_gain,
    norm_bias,
    w_expand,
    b_expand,
    w_reduce,
    b_reduce,
    layer_scale,
):
    row_mean = jnp.mean(conv_out, axis=-1, keepdims=True)
    centered = conv_out - row_mean
    inv_std = lax.rsqrt(jnp.mean(centered * centered, axis=-1, keepdims=True) + 1e-06)
    normal_hat = centered * inv_std
    normed = (normal_hat * norm_gain + norm_bias).astype(jnp.bfloat16)
    hidden = jnp.dot(normed, w_expand, preferred_element_type=jnp.float32) + b_expand
    activated = gelu_value(hidden).astype(jnp.bfloat16)
    projected = jnp.dot(activated, w_reduce, preferred_element_type=jnp.float32) + b_reduce
    result = (keep_mask * (ocean_state.astype(jnp.float32) + layer_scale * projected)).astype(
        jnp.bfloat16
    )
    grad_out = (keep_mask * layer_scale * cotangent.astype(jnp.float32)).astype(jnp.bfloat16)
    grad_act = jnp.dot(grad_out, w_reduce.T, preferred_element_type=jnp.float32)
    grad_hidden = (grad_act * gelu_slope(hidden)).astype(jnp.bfloat16)
    grad_normed = jnp.dot(grad_hidden, w_expand.T, preferred_element_type=jnp.float32)
    grad_scaled = grad_normed * norm_gain
    conv_grad = inv_std * (
        grad_scaled
        - jnp.mean(grad_scaled, axis=-1, keepdims=True)
        - normal_hat * jnp.mean(grad_scaled * normal_hat, axis=-1, keepdims=True)
    )
    return (result, conv_grad)


def fold_forward(mirrored):
    spread = lax.all_to_all(mirrored[None], "lon", split_axis=3, concat_axis=0, tiled=True)
    collected = lax.all_to_all(spread[::-1], "lon", split_axis=0, concat_axis=3, tiled=True)
    return collected[0]


def fold_backward(mirrored):
    spread = lax.all_to_all(
        mirrored[None].astype(jnp.bfloat16), "lon", split_axis=3, concat_axis=0, tiled=True
    ).astype(jnp.float32)
    collected = lax.all_to_all(
        for_sending(spread[::-1]), "lon", split_axis=0, concat_axis=3, tiled=True
    )
    return collected[0]


def send_lon_rim(rim_piece, step_by):
    return shifted(rim_piece.astype(jnp.bfloat16), "lon", step_by).astype(rim_piece.dtype)


def send_lat_rim(rim_piece, step_by):
    return from_behind(rim_piece.astype(jnp.bfloat16), "lat", step_by).astype(rim_piece.dtype)


def body(
    ocean_state,
    land_sea,
    kernel,
    conv_bias,
    norm_gain,
    norm_bias,
    w_expand,
    b_expand,
    w_reduce,
    b_reduce,
    layer_scale,
    cotangent,
):
    band_rows, band_cols, channels = ocean_state.shape
    keep_mask = land_sea.astype(jnp.float32)[:, :, None]
    masked = (ocean_state.astype(jnp.float32) * keep_mask).astype(jnp.bfloat16)
    extended = extended_2(masked, (("lat", 0), ("lon", 1)), 3)
    band_index = lax.axis_index("lat")
    band_count = lax.axis_size("lat")
    lower_rows = jnp.where(band_index == 0, jnp.zeros_like(extended[:3]), extended[:3])
    mirrored = extended[band_rows : band_rows + 3][::-1, ::-1]
    partner_rows = fold_forward(mirrored)
    upper_rows = jnp.where(band_index == band_count - 1, partner_rows, extended[band_rows + 3 :])
    padded = jnp.concatenate([lower_rows, extended[3 : band_rows + 3], upper_rows], 0).astype(
        jnp.float32
    )

    def convolve(plane_in):
        return depthwise(plane_in, kernel, conv_bias)

    conv_out, pullback = jax.vjp(convolve, padded)
    cell_count = band_rows * band_cols
    result, conv_grad = pointwise(
        conv_out.reshape(cell_count, channels),
        ocean_state.reshape(cell_count, channels),
        keep_mask.reshape(cell_count, 1),
        cotangent.reshape(cell_count, channels),
        norm_gain,
        norm_bias,
        w_expand,
        b_expand,
        w_reduce,
        b_reduce,
        layer_scale,
    )
    padded_grad = pullback(conv_grad.reshape(band_rows, band_cols, channels))[0]
    from_right = send_lon_rim(padded_grad[:, :3], -1)
    from_left = send_lon_rim(padded_grad[:, band_cols + 3 :], 1)
    col_core = padded_grad[:, 3 : band_cols + 3]
    col_core = col_core.at[:, :3].add(from_left).at[:, band_cols - 3 :].add(from_right)
    from_below = send_lat_rim(col_core[band_rows + 3 :], 1)
    from_above = send_lat_rim(col_core[:3], -1)
    mirrored_grad = col_core[band_rows + 3 :][::-1, ::-1]
    returned = fold_backward(mirrored_grad)
    fold_term = jnp.where(band_index == band_count - 1, returned, jnp.zeros_like(returned))
    inner = col_core[3 : band_rows + 3]
    inner = inner.at[:3].add(from_below).at[band_rows - 3 :].add(from_above)
    inner = inner.at[band_rows - 3 :].add(fold_term)
    state_grad = (keep_mask * (cotangent.astype(jnp.float32) + inner)).astype(jnp.bfloat16)
    return (result.reshape(band_rows, band_cols, channels), state_grad)


def solution(mesh):
    placed = (
        P("lat", "lon", None),
        P("lat", "lon"),
        P(),
        P(),
        P(),
        P(),
        P(),
        P(),
        P(),
        P(),
        P(),
        P("lat", "lon", None),
    )
    return jax.shard_map(
        body,
        mesh=mesh,
        in_specs=placed,
        out_specs=(P("lat", "lon", None), P("lat", "lon", None)),
        check_vma=False,
    )
```

profile of v0, /device:TPU:1, one launch (start us, length us, event | category | flops | bytes accessed | tf_op | source)
XLA Modules:
  0.0 173.0 jit_solution(278286113013113201)
XLA Ops:
  1.6 1.5 multiply_convert_fusion.3
  3.1 4.2 %collective-permute-start = (bf16[3,32,128]{2,1,0:T(8,128)(2,1)S(1)}, bf16[3,32,128]{2,1,0:T(8,128)(2,1)S(1)}, u32[]{:S(2)}, u32[]{:S(2)}) collective-permute-start(bf16[3,32,128]{2,1,0:T(8,128)(2,1)S(1)} %get-tuple-element.132), channel_id=1, source_target_pairs={{0,1},{1,2},{2,3},{3,0},{4,5},{5,6},{6,7},{7,4},{8,9},{9,10},{10,1... | collective-permute-start | bytes 73736 | tf_op jit(solution)/shard_map/ppermute | solution.py:29
  7.4 1.2 fusion.60
  8.8 3.2 %collective-permute-done.1 = bf16[3,32,128]{2,1,0:T(8,128)(2,1)S(1)} collective-permute-done((bf16[3,32,128]{2,1,0:T(8,128)(2,1)S(1)}, bf16[3,32,128]{2,1,0:T(8,128)(2,1)S(1)}, u32[]{:S(2)}, u32[]{:S(2)}) %collective-permute-start.1) | collective-permute-done | bytes 24608 | tf_op jit(solution)/shard_map/ppermute | solution.py:32
  12.1 6.3 %collective-permute-start.3 = (bf16[86,3,128]{2,0,1:T(8,128)(2,1)S(1)}, bf16[86,3,128]{2,0,1:T(8,128)(2,1)S(1)}, u32[]{:S(2)}, u32[]{:S(2)}) collective-permute-start(bf16[86,3,128]{2,0,1:T(8,128)(2,1)S(1)} %copy.228), channel_id=1, source_target_pairs={{4,0},{8,4},{12,8},{16,12},{20,16},{24,20},{28,24},{32,28},{36,32}... | collective-permute-start | bytes 198152 | tf_op jit(solution)/shard_map/ppermute | solution.py:32
  18.7 1.1 collective-permute-done.3
  19.8 6.0 %collective-permute-done.2 = bf16[86,3,128]{2,0,1:T(8,128)(2,1)S(1)} collective-permute-done((bf16[86,3,128]{2,0,1:T(8,128)(2,1)S(1)}, bf16[86,3,128]{2,0,1:T(8,128)(2,1)S(1)}, u32[]{:S(2)}, u32[]{:S(2)}) %collective-permute-start.2) | collective-permute-done | bytes 66080 | tf_op jit(solution)/shard_map/ppermute | solution.py:29
  26.8 3.9 %all-to-all-start = ((bf16[32,2,228]{2,1,0:T(2,128)(2,1)}), bf16[32,2,228]{2,1,0:T(2,128)(2,1)S(1)}, u32[]{:S(2)}, u32[]{:S(2)}) async-start(bf16[32,2,228]{2,1,0:T(2,128)(2,1)} %reshape.287), calls=%async_computation | async-start | bytes 65536 | tf_op jit(solution)/shard_map/all_to_all | solution.py:95
  31.3 6.7 %all-to-all-done = bf16[32,2,228]{2,1,0:T(2,128)(2,1)S(1)} async-done(((bf16[32,2,228]{2,1,0:T(2,128)(2,1)}), bf16[32,2,228]{2,1,0:T(2,128)(2,1)S(1)}, u32[]{:S(2)}, u32[]{:S(2)}) %all-to-all-start) | async-done | bytes 29216 | tf_op jit(solution)/shard_map/all_to_all | solution.py:95
  39.0 4.0 %all-to-all-start.1 = ((bf16[32,2,228]{2,1,0:T(2,128)(2,1)}), bf16[32,2,228]{2,1,0:T(2,128)(2,1)S(1)}, u32[]{:S(2)}, u32[]{:S(2)}) async-start(bf16[32,2,228]{2,1,0:T(2,128)(2,1)} %reshape.289), calls=%async_computation.1 | async-start | bytes 65536 | tf_op jit(solution)/shard_map/all_to_all | solution.py:96
  43.5 6.4 %all-to-all-done.1 = bf16[32,2,228]{2,1,0:T(2,128)(2,1)S(1)} async-done(((bf16[32,2,228]{2,1,0:T(2,128)(2,1)}), bf16[32,2,228]{2,1,0:T(2,128)(2,1)S(1)}, u32[]{:S(2)}, u32[]{:S(2)}) %all-to-all-start.1) | async-done | bytes 29216 | tf_op jit(solution)/shard_map/all_to_all | solution.py:96
  51.0 9.5 %fusion.70 = (f32[80,32]{1,0:T(8,128)S(1)}, f32[80,32,128]{2,1,0:T(8,128)S(1)}) fusion(f32[86,38,128]{2,1,0:T(8,128)S(1)} %maximum_convert_fusion, f32[128]{0:T(128)} %get-tuple-element.181, f32[128]{0:T(128)} %get-tuple-element.182, f32[128]{0:T(128)S(1)} %get-tuple-element.135, f32[128]{0:T(128)S(1)} %get-tuple-element.136, ...), kind=kLoop, calls=%fused_computation.255 | loop fusion | flops 32437760 | bytes 65571840 | tf_op jit(solution)/shard_map/reduce_sum | solution.py:70
  61.5 1.5 add_convert_fusion
  63.0 3.2 %convolution_add_fusion = f32[2560,512]{1,0:T(8,128)} fusion(bf16[2560,128]{1,0:T(8,128)(2,1)S(1)} %add_convert_fusion, bf16[128,512]{1,0:T(8,128)(2,1)S(1)} %copy-done, f32[512]{0:T(512)S(1)} %copy-done.8), kind=kOutput, calls=%fused_computation.9 | convolution fusion | flops 336855040 | bytes 6031360 | tf_op jit(solution)/shard_map/dot_general | solution.py:75
  66.2 5.4 %fusion.68 = (f32[2560]{0:T(1024)S(1)}, f32[2560]{0:T(1024)S(1)}, f32[2560,128]{1,0:T(8,128)S(1)}) fusion(f32[2560]{0:T(1024)S(1)} %rsqrt.12, f32[2560]{0:T(1024)S(1)} %div.15, f32[80,32,128]{2,1,0:T(8,128)S(1)} %get-tuple-element.73, f32[128]{0:T(128)S(1)} %copy-done.89, bf16[128,512]{1,0:T(8,128)(2,1)S(1)} %copy-done, ...), kind=kOutput, calls=%fused_computation.253 | convolution fusion | flops 686156800 | bytes 8823296 | tf_op jit(solution)/shard_map/dot_general | solution.py:84
  71.8 2.2 %subtract_multiply_fusion = f32[2560,128]{1,0:T(8,128)S(1)} fusion(f32[2560,128]{1,0:T(8,128)S(1)} %get-tuple-element.183, f32[80,32,128]{2,1,0:T(8,128)S(1)} %get-tuple-element.73, f32[2560]{0:T(1024)S(1)} %get-tuple-element.184, f32[2560]{0:T(1024)S(1)} %get-tuple-element.185, f32[2560]{0:T(1024)S(1)} %rsqrt.12, f32[2560]{0:T(1024)S(1)} %div.15), kind=kLoop, calls=%fused_computation.121 | loop fusion | flops 1966080 | bytes 3973120 | tf_op jit(solution)/shard_map/mul | solution.py:86
  74.3 4.5 %broadcast_multiply_fusion.2 = (f32[80,32,128]{2,1,0:T(8,128)S(1)}, f32[80,32,128]{2,1,0:T(8,128)S(1)}, f32[80,32,128]{2,1,0:T(8,128)S(1)}, f32[80,32,128]{2,1,0...) fusion(f32[80,32,128]{2,1,0:T(8,128)S(1)} %bitcast.210, ...), kind=kLoop, calls=%fused_computation.130 | loop fusion | flops 4259840 | bytes 18356736 | tf_op jit(solution)/shard_map/transpose(jvp())/mul | solution.py:53
  79.1 8.8 %broadcast_multiply_fusion.1 = (f32[80,32,128]{2,1,0:T(8,128)}, f32[80,32,128]{2,1,0:T(8,128)}, f32[80,32,128]{2,1,0:T(8,128)}, f32[80,32,128]{2,1,0:T(8,128)}, ...) fusion(f32[80,32,128]{2,1,0:T(8,128)S(1)} %bitcast.211, ...), kind=kLoop, calls=%fused_computation.129 | loop fusion | flops 5898240 | bytes 24912896 | tf_op jit(solution)/shard_map/transpose(jvp())/mul | solution.py:53
  87.9 8.6 %broadcast_multiply_fusion = (f32[80,32,128]{2,1,0:T(8,128)}, f32[80,32,128]{2,1,0:T(8,128)}, f32[80,32,128]{2,1,0:T(8,128)}, f32[80,32,128]{2,1,0:T(8,128)}, f3...) fusion(f32[80,32,128]{2,1,0:T(8,128)S(1)} %bitcast.212, ...), kind=kLoop, calls=%fused_computation.128 | loop fusion | flops 5898240 | bytes 24912896 | tf_op jit(solution)/shard_map/transpose(jvp())/mul | solution.py:53
  96.6 21.0 %fusion.69 = (bf16[86,38,128]{2,1,0:T(8,128)(2,1)S(1)}, f32[86,38,128]{2,1,0:T(8,128)S(1)}) fusion(f32[80,32,128]{2,1,0:T(8,128)} %get-tuple-element.78, f32[80,32,128]{2,1,0:T(8,128)} %get-tuple-element.79, f32[80,32,128]{2,1,0:T(8,128)} %get-tuple-element.80, f32[80,32,128]{2,1,0:T(8,128)} %get-tuple-element.81, f32[80,32,128]{2,1,0:T(8,128)} %get-tuple-element.82, ...), kind=kLoop, calls=%fused_computation.254 | loop fusion | flops 20496896 | bytes 66735104 | tf_op jit(solution)/shard_map/convert.59
  118.1 5.4 %collective-permute-start.5 = (bf16[86,3,128]{2,0,1:T(8,128)(2,1)S(1)}, bf16[86,3,128]{2,0,1:T(8,128)(2,1)S(1)}, u32[]{:S(2)}, u32[]{:S(2)}) collective-permute-start(bf16[86,3,128]{2,0,1:T(8,128)(2,1)S(1)} %copy.238), channel_id=1, source_target_pairs={{4,0},{8,4},{12,8},{16,12},{20,16},{24,20},{28,24},{32,28},{36,32}... | collective-permute-start | bytes 198152 | tf_op jit(solution)/shard_map/ppermute | solution.py:14
  123.8 1.3 collective-permute-done.4
  125.1 4.9 %scatter-add.16 = f32[86,32,128]{2,1,0:T(8,128)S(1)} dynamic-update-slice(f32[86,32,128]{2,1,0:T(8,128)S(1)} %slice.628, f32[86,3,128]{2,1,0:T(4,128)S(1)} %slice_add_fusion.1, s32[]{:T(128)} %constant.145.clone.1, s32[]{:T(128)} %constant.145.clone.1, s32[]{:T(128)} %constant.145.clone.1) | dynamic-update-slice | bytes 264196 | tf_op jit(solution)/shard_map/scatter-add | solution.py:168
  130.2 3.9 %scatter-add.19 = f32[86,32,128]{2,1,0:T(8,128)S(1)} dynamic-update-slice(f32[86,32,128]{2,1,0:T(8,128)S(1)} %scatter-add.16, f32[86,3,128]{2,1,0:T(4,128)S(1)} %slice_add_fusion, s32[]{:T(128)} %constant.145.clone.1, s32[]{:T(128)} %constant.156.clone.1, s32[]{:T(128)} %constant.145.clone.1) | dynamic-update-slice | bytes 264196 | tf_op jit(solution)/shard_map/scatter-add | solution.py:168
  135.6 4.1 %all-to-all-start.2 = ((bf16[32,2,192]{2,1,0:T(2,128)(2,1)}), bf16[32,2,192]{2,1,0:T(2,128)(2,1)S(1)}, u32[]{:S(2)}, u32[]{:S(2)}) async-start(bf16[32,2,192]{2,1,0:T(2,128)(2,1)} %reshape.291), calls=%async_computation.2 | async-start | bytes 65536 | tf_op jit(solution)/shard_map/all_to_all | solution.py:101
  139.7 4.0 %fusion.9 = bf16[2560,128]{1,0:T(8,128)(2,1)} fusion(bf16[512,128]{1,0:T(8,128)(2,1)S(1)} %copy-done.93, f32[2560,512]{1,0:T(8,128)} %convolution_add_fusion, f32[128]{0:T(128)S(1)} %copy-done.94, f32[128]{0:T(128)S(1)} %copy-done.91, f32[2560]{0:T(1024)S(1)} %copy-done.6, bf16[2560,128]{1,0:T(8,128)(2,1)S(1)} %bitcast.214), kind=kOutput, calls=%fused_computation.15 | convolution fusion | flops 344064000 | bytes 6695936 | tf_op jit(solution)/shard_map/dot_general | solution.py:77
  143.9 7.9 %collective-permute-start.6 = (bf16[3,32,128]{2,1,0:T(8,128)(2,1)S(1)}, bf16[3,32,128]{2,1,0:T(8,128)(2,1)S(1)}, u32[]{:S(2)}, u32[]{:S(2)}) collective-permute-start(bf16[3,32,128]{2,1,0:T(8,128)(2,1)S(1)} %get-tuple-element.74), channel_id=1, source_target_pairs={{0,1},{1,2},{2,3},{4,5},{5,6},{6,7},{8,9},{9,10},{10,11},{12,13},{... | collective-permute-start | bytes 73736 | tf_op jit(solution)/shard_map/ppermute | solution.py:20
  151.7 1.9 %collective-permute-start.7 = (bf16[3,32,128]{2,1,0:T(8,128)(2,1)}, bf16[3,32,128]{2,1,0:T(8,128)(2,1)}, u32[]{:S(2)}, u32[]{:S(2)}) collective-permute-start(bf16[3,32,128]{2,1,0:T(8,128)(2,1)} %get-tuple-element.76), channel_id=1, source_target_pairs={{1,0},{2,1},{3,2},{5,4},{6,5},{7,6},{9,8},{10,9},{11,10},{13,12},{... | collective-permute-start | bytes 73736 | tf_op jit(solution)/shard_map/ppermute | solution.py:20
  154.6 7.2 %all-to-all-start.3 = ((bf16[32,2,192]{2,1,0:T(2,128)(2,1)}), bf16[32,2,192]{2,1,0:T(2,128)(2,1)S(1)}, u32[]{:S(2)}, u32[]{:S(2)}) async-start(bf16[32,2,192]{2,1,0:T(2,128)(2,1)} %reshape.293), calls=%async_computation.3 | async-start | bytes 65536 | tf_op jit(solution)/shard_map/all_to_all | solution.py:104
  162.8 6.2 %all-to-all-done.3 = bf16[32,2,192]{2,1,0:T(2,128)(2,1)S(1)} async-done(((bf16[32,2,192]{2,1,0:T(2,128)(2,1)}), bf16[32,2,192]{2,1,0:T(2,128)(2,1)S(1)}, u32[]{:S(2)}, u32[]{:S(2)}) %all-to-all-start.3) | async-done | bytes 24608 | tf_op jit(solution)/shard_map/all_to_all | solution.py:104
  169.9 1.0 copy.244
  171.7 1.2 multiply_convert_fusion.2
  (254 shorter events, 12.2 us)
Async XLA Ops:
  0.6 62.4 %copy-start = (bf16[128,512]{1,0:T(8,128)(2,1)S(1)}, bf16[128,512]{1,0:T(8,128)(2,1)}, u32[]{:S(2)}) copy-start(bf16[128,512]{1,0:T(8,128)(2,1)} %param.28) | copy-start | bytes 393220
  3.1 5.7 %collective-permute-start = (bf16[3,32,128]{2,1,0:T(8,128)(2,1)S(1)}, bf16[3,32,128]{2,1,0:T(8,128)(2,1)S(1)}, u32[]{:S(2)}, u32[]{:S(2)}) collective-permute-start(bf16[3,32,128]{2,1,0:T(8,128)(2,1)S(1)} %get-tuple-element.132), channel_id=1, source_target_pairs={{0,1},{1,2},{2,3},{3,0},{4,5},{5,6},{6,7},{7,4},{8,9},{9,10},{10,1... | collective-permute-start | bytes 73736 | tf_op jit(solution)/shard_map/ppermute | solution.py:29
  7.3 4.8 %collective-permute-start.1 = (bf16[3,32,128]{2,1,0:T(8,128)(2,1)S(1)}, bf16[3,32,128]{2,1,0:T(8,128)(2,1)S(1)}, u32[]{:S(2)}, u32[]{:S(2)}) collective-permute-start(bf16[3,32,128]{2,1,0:T(8,128)(2,1)S(1)} %get-tuple-element.133), channel_id=1, source_target_pairs={{1,0},{2,1},{3,2},{0,3},{5,4},{6,5},{7,6},{4,7},{9,8},{10,9},{11,1... | collective-permute-start | bytes 73736 | tf_op jit(solution)/shard_map/ppermute | solution.py:32
  8.6 41.9 %copy-start.9 = (f32[128]{0:T(128)}, f32[128]{0:T(128)S(1)}, u32[]{:S(2)}) copy-start(f32[128]{0:T(128)S(1)} %get-tuple-element.135) | copy-start | bytes 1540
  8.6 41.9 %copy-start.11 = (f32[128]{0:T(128)}, f32[128]{0:T(128)S(1)}, u32[]{:S(2)}) copy-start(f32[128]{0:T(128)S(1)} %get-tuple-element.136) | copy-start | bytes 1540
  8.7 41.9 %copy-start.13 = (f32[128]{0:T(128)}, f32[128]{0:T(128)S(1)}, u32[]{:S(2)}) copy-start(f32[128]{0:T(128)S(1)} %get-tuple-element.137) | copy-start | bytes 1540
  8.7 41.9 %copy-start.15 = (f32[128]{0:T(128)}, f32[128]{0:T(128)S(1)}, u32[]{:S(2)}) copy-start(f32[128]{0:T(128)S(1)} %get-tuple-element.138) | copy-start | bytes 1540
  8.7 41.9 %copy-start.17 = (f32[128]{0:T(128)}, f32[128]{0:T(128)S(1)}, u32[]{:S(2)}) copy-start(f32[128]{0:T(128)S(1)} %get-tuple-element.139) | copy-start | bytes 1540
  8.7 41.9 %copy-start.19 = (f32[128]{0:T(128)}, f32[128]{0:T(128)S(1)}, u32[]{:S(2)}) copy-start(f32[128]{0:T(128)S(1)} %get-tuple-element.140) | copy-start | bytes 1540
  8.7 41.9 %copy-start.21 = (f32[128]{0:T(128)}, f32[128]{0:T(128)S(1)}, u32[]{:S(2)}) copy-start(f32[128]{0:T(128)S(1)} %get-tuple-element.141) | copy-start | bytes 1540
  8.7 41.9 %copy-start.23 = (f32[128]{0:T(128)}, f32[128]{0:T(128)S(1)}, u32[]{:S(2)}) copy-start(f32[128]{0:T(128)S(1)} %get-tuple-element.142) | copy-start | bytes 1540
  8.7 41.9 %copy-start.25 = (f32[128]{0:T(128)}, f32[128]{0:T(128)S(1)}, u32[]{:S(2)}) copy-start(f32[128]{0:T(128)S(1)} %get-tuple-element.143) | copy-start | bytes 1540
  8.7 41.9 %copy-start.27 = (f32[128]{0:T(128)}, f32[128]{0:T(128)S(1)}, u32[]{:S(2)}) copy-start(f32[128]{0:T(128)S(1)} %get-tuple-element.144) | copy-start | bytes 1540
  8.7 41.9 %copy-start.29 = (f32[128]{0:T(128)}, f32[128]{0:T(128)S(1)}, u32[]{:S(2)}) copy-start(f32[128]{0:T(128)S(1)} %get-tuple-element.145) | copy-start | bytes 1540
  8.7 41.9 %copy-start.31 = (f32[128]{0:T(128)}, f32[128]{0:T(128)S(1)}, u32[]{:S(2)}) copy-start(f32[128]{0:T(128)S(1)} %get-tuple-element.146) | copy-start | bytes 1540
  8.8 41.9 %copy-start.33 = (f32[128]{0:T(128)}, f32[128]{0:T(128)S(1)}, u32[]{:S(2)}) copy-start(f32[128]{0:T(128)S(1)} %get-tuple-element.147) | copy-start | bytes 1540
  8.8 41.9 %copy-start.35 = (f32[128]{0:T(128)}, f32[128]{0:T(128)S(1)}, u32[]{:S(2)}) copy-start(f32[128]{0:T(128)S(1)} %get-tuple-element.134) | copy-start | bytes 1540
  8.8 41.9 %copy-start.37 = (f32[128]{0:T(128)}, f32[128]{0:T(128)S(1)}, u32[]{:S(2)}) copy-start(f32[128]{0:T(128)S(1)} %get-tuple-element.148) | copy-start | bytes 1540
  8.8 41.9 %copy-start.39 = (f32[128]{0:T(128)}, f32[128]{0:T(128)S(1)}, u32[]{:S(2)}) copy-start(f32[128]{0:T(128)S(1)} %get-tuple-element.149) | copy-start | bytes 1540
  8.8 41.9 %copy-start.41 = (f32[128]{0:T(128)}, f32[128]{0:T(128)S(1)}, u32[]{:S(2)}) copy-start(f32[128]{0:T(128)S(1)} %get-tuple-element.150) | copy-start | bytes 1540
  8.8 41.9 %copy-start.43 = (f32[128]{0:T(128)}, f32[128]{0:T(128)S(1)}, u32[]{:S(2)}) copy-start(f32[128]{0:T(128)S(1)} %get-tuple-element.151) | copy-start | bytes 1540
  8.8 41.9 %copy-start.45 = (f32[128]{0:T(128)}, f32[128]{0:T(128)S(1)}, u32[]{:S(2)}) copy-start(f32[128]{0:T(128)S(1)} %get-tuple-element.152) | copy-start | bytes 1540
  12.1 7.7 %collective-permute-start.3 = (bf16[86,3,128]{2,0,1:T(8,128)(2,1)S(1)}, bf16[86,3,128]{2,0,1:T(8,128)(2,1)S(1)}, u32[]{:S(2)}, u32[]{:S(2)}) collective-permute-start(bf16[86,3,128]{2,0,1:T(8,128)(2,1)S(1)} %copy.228), channel_id=1, source_target_pairs={{4,0},{8,4},{12,8},{16,12},{20,16},{24,20},{28,24},{32,28},{36,32}... | collective-permute-start | bytes 198152 | tf_op jit(solution)/shard_map/ppermute | solution.py:32
  18.4 7.4 %collective-permute-start.2 = (bf16[86,3,128]{2,0,1:T(8,128)(2,1)S(1)}, bf16[86,3,128]{2,0,1:T(8,128)(2,1)S(1)}, u32[]{:S(2)}, u32[]{:S(2)}) collective-permute-start(bf16[86,3,128]{2,0,1:T(8,128)(2,1)S(1)} %copy.227), channel_id=1, source_target_pairs={{0,4},{4,8},{8,12},{12,16},{16,20},{20,24},{24,28},{28,32},{32,36}... | collective-permute-start | bytes 198152 | tf_op jit(solution)/shard_map/ppermute | solution.py:29
  26.8 11.1 %all-to-all-start = ((bf16[32,2,228]{2,1,0:T(2,128)(2,1)}), bf16[32,2,228]{2,1,0:T(2,128)(2,1)S(1)}, u32[]{:S(2)}, u32[]{:S(2)}) async-start(bf16[32,2,228]{2,1,0:T(2,128)(2,1)} %reshape.287), calls=%async_computation | async-start | bytes 65536 | tf_op jit(solution)/shard_map/all_to_all | solution.py:95
  39.0 11.0 %all-to-all-start.1 = ((bf16[32,2,228]{2,1,0:T(2,128)(2,1)}), bf16[32,2,228]{2,1,0:T(2,128)(2,1)S(1)}, u32[]{:S(2)}, u32[]{:S(2)}) async-start(bf16[32,2,228]{2,1,0:T(2,128)(2,1)} %reshape.289), calls=%async_computation.1 | async-start | bytes 65536 | tf_op jit(solution)/shard_map/all_to_all | solution.py:96
  117.7 7.4 %collective-permute-start.4 = (bf16[86,3,128]{2,0,1:T(8,128)(2,1)S(1)}, bf16[86,3,128]{2,0,1:T(8,128)(2,1)S(1)}, u32[]{:S(2)}, u32[]{:S(2)}) collective-permute-start(bf16[86,3,128]{2,0,1:T(8,128)(2,1)S(1)} %copy.236), channel_id=1, source_target_pairs={{124,0},{0,4},{4,8},{8,12},{12,16},{16,20},{20,24},{24,28},{28,32}... | collective-permute-start | bytes 198152 | tf_op jit(solution)/shard_map/ppermute | solution.py:14
  118.1 12.0 %collective-permute-start.5 = (bf16[86,3,128]{2,0,1:T(8,128)(2,1)S(1)}, bf16[86,3,128]{2,0,1:T(8,128)(2,1)S(1)}, u32[]{:S(2)}, u32[]{:S(2)}) collective-permute-start(bf16[86,3,128]{2,0,1:T(8,128)(2,1)S(1)} %copy.238), channel_id=1, source_target_pairs={{4,0},{8,4},{12,8},{16,12},{20,16},{24,20},{28,24},{32,28},{36,32}... | collective-permute-start | bytes 198152 | tf_op jit(solution)/shard_map/ppermute | solution.py:14
  135.6 18.1 %all-to-all-start.2 = ((bf16[32,2,192]{2,1,0:T(2,128)(2,1)}), bf16[32,2,192]{2,1,0:T(2,128)(2,1)S(1)}, u32[]{:S(2)}, u32[]{:S(2)}) async-start(bf16[32,2,192]{2,1,0:T(2,128)(2,1)} %reshape.291), calls=%async_computation.2 | async-start | bytes 65536 | tf_op jit(solution)/shard_map/all_to_all | solution.py:101
  143.9 18.0 %collective-permute-start.6 = (bf16[3,32,128]{2,1,0:T(8,128)(2,1)S(1)}, bf16[3,32,128]{2,1,0:T(8,128)(2,1)S(1)}, u32[]{:S(2)}, u32[]{:S(2)}) collective-permute-start(bf16[3,32,128]{2,1,0:T(8,128)(2,1)S(1)} %get-tuple-element.74), channel_id=1, source_target_pairs={{0,1},{1,2},{2,3},{4,5},{5,6},{6,7},{8,9},{9,10},{10,11},{12,13},{... | collective-permute-start | bytes 73736 | tf_op jit(solution)/shard_map/ppermute | solution.py:20
  151.7 10.2 %collective-permute-start.7 = (bf16[3,32,128]{2,1,0:T(8,128)(2,1)}, bf16[3,32,128]{2,1,0:T(8,128)(2,1)}, u32[]{:S(2)}, u32[]{:S(2)}) collective-permute-start(bf16[3,32,128]{2,1,0:T(8,128)(2,1)} %get-tuple-element.76), channel_id=1, source_target_pairs={{1,0},{2,1},{3,2},{5,4},{6,5},{7,6},{9,8},{10,9},{11,10},{13,12},{... | collective-permute-start | bytes 73736 | tf_op jit(solution)/shard_map/ppermute | solution.py:20
  154.6 14.4 %all-to-all-start.3 = ((bf16[32,2,192]{2,1,0:T(2,128)(2,1)}), bf16[32,2,192]{2,1,0:T(2,128)(2,1)S(1)}, u32[]{:S(2)}, u32[]{:S(2)}) async-start(bf16[32,2,192]{2,1,0:T(2,128)(2,1)} %reshape.293), calls=%async_computation.3 | async-start | bytes 65536 | tf_op jit(solution)/shard_map/all_to_all | solution.py:104
  (75 other events, 955.3 us)
where the time goes:
time: 175 us; the launch traced here: 173 us
  other arithmetic  64.9 us (37%)
  starting transfers between devices  45.3 us (26%)
  waiting for transfers between devices  30.9 us (18%)
  local copies, waits for them, and re-layouts  16.8 us (10%)
  matrix products  12.6 us (7%)
  between operations  2.43 us (1%)
    mul x6, other arithmetic, depthwise(): summed = summed + kernel[row_tap, col_tap].astype(jnp.float32) * window  22.6 us
    another operation x1, other arithmetic  21 us
    ppermute x2, starting transfers between devices, from_behind(): lax.ppermute(value, axis, [(source, source + steps) for source in range(l...  9.8 us
    reduce_sum x1, other arithmetic, pointwise(): row_mean = jnp.mean(conv_out, axis=-1, keepdims=True)  9.49 us
    scatter-add x2, local copies, waits for them, and re-layouts, body(): col_core.at[:, :3].add(from_left).at[:, band_cols - 3:].add(from_right)  8.8 us
    all_to_all x1, starting transfers between devices, fold_backward(): lax.all_to_all(for_sending(spread[::-1]), 'lon', split_axis=0, concat_axi...  7.18 us
    all_to_all x1, waiting for transfers between devices, fold_forward(): lax.all_to_all(mirrored[None], 'lon', split_axis=3, concat_axis=0, tiled=...  6.66 us
    all_to_all x1, waiting for transfers between devices, fold_forward(): lax.all_to_all(spread[::-1], 'lon', split_axis=0, concat_axis=3, tiled=True)  6.44 us
  transfers between devices with their start and end apart: 12, of which 7 were waited for; matrix products, arithmetic and copies ran while one was open for 8% of the time, Pallas kernels for 0%

commit v1 on v0

v1 whole, which is shorter than its diff:
```python
import jax
import jax.numpy as jnp
from jax import lax
from jax.sharding import PartitionSpec as P


def shifted(block, axis, distance):
    devices = range(lax.axis_size(axis))
    route = [((i - distance) % len(devices), i) for i in devices]
    return lax.ppermute(block, axis, route)


def from_behind(value, axis, steps):
    count = lax.axis_size(axis)
    leading, last = (max(0, -steps), min(count, count - steps))
    return lax.ppermute(value, axis, [(source, source + steps) for source in range(leading, last)])


def mirrored(value, axis):
    count = lax.axis_size(axis)
    return lax.ppermute(value[::-1, ::-1], axis, [(i, count - 1 - i) for i in range(count)])


def with_col_halo(block, width):
    left = shifted(block[:, block.shape[1] - width :], "lon", 1)
    right = shifted(block[:, :width], "lon", -1)
    return jnp.concatenate([left, block, right], axis=1)


def gelu_value(values):
    return 0.5 * values * (1.0 + lax.erf(values * 0.7071067811865476))


def gelu_slope(values):
    cumulative = 0.5 * (1.0 + lax.erf(values * 0.7071067811865476))
    return cumulative + values * jnp.exp(-0.5 * values * values) * 0.3989422804014327


def correlate(padded, kernel, start):
    out_rows = padded.shape[0] - 6
    out_cols = padded.shape[1] - 6
    summed = start
    for row_tap in range(7):
        for col_tap in range(7):
            window = padded[row_tap : row_tap + out_rows, col_tap : col_tap + out_cols]
            summed = summed + kernel[row_tap, col_tap].astype(jnp.float32) * window
    return summed


def pointwise(
    conv_out,
    ocean_state,
    keep_mask,
    cotangent,
    norm_gain,
    norm_bias,
    w_expand,
    b_expand,
    w_reduce,
    b_reduce,
    layer_scale,
):
    row_mean = jnp.mean(conv_out, axis=-1, keepdims=True)
    centered = conv_out - row_mean
    inv_std = lax.rsqrt(jnp.mean(centered * centered, axis=-1, keepdims=True) + 1e-06)
    normal_hat = centered * inv_std
    normed = (normal_hat * norm_gain + norm_bias).astype(jnp.bfloat16)
    hidden = jnp.dot(normed, w_expand, preferred_element_type=jnp.float32) + b_expand
    activated = gelu_value(hidden).astype(jnp.bfloat16)
    projected = jnp.dot(activated, w_reduce, preferred_element_type=jnp.float32) + b_reduce
    result = (keep_mask * (ocean_state.astype(jnp.float32) + layer_scale * projected)).astype(
        jnp.bfloat16
    )
    grad_out = (keep_mask * layer_scale * cotangent.astype(jnp.float32)).astype(jnp.bfloat16)
    grad_act = jnp.dot(grad_out, w_reduce.T, preferred_element_type=jnp.float32)
    grad_hidden = (grad_act * gelu_slope(hidden)).astype(jnp.bfloat16)
    grad_normed = jnp.dot(grad_hidden, w_expand.T, preferred_element_type=jnp.float32)
    grad_scaled = grad_normed * norm_gain
    conv_grad = inv_std * (
        grad_scaled
        - jnp.mean(grad_scaled, axis=-1, keepdims=True)
        - normal_hat * jnp.mean(grad_scaled * normal_hat, axis=-1, keepdims=True)
    )
    return (result, conv_grad)


def body(
    ocean_state,
    land_sea,
    kernel,
    conv_bias,
    norm_gain,
    norm_bias,
    w_expand,
    b_expand,
    w_reduce,
    b_reduce,
    layer_scale,
    cotangent,
):
    band_rows, band_cols, channels = ocean_state.shape
    top_band = lax.axis_index("lat") == lax.axis_size("lat") - 1
    keep_mask = land_sea.astype(jnp.float32)[:, :, None]
    masked = (ocean_state.astype(jnp.float32) * keep_mask).astype(jnp.bfloat16)

    below = from_behind(masked[band_rows - 3 :], "lat", 1)
    above = from_behind(masked[:3], "lat", -1)
    fold_rows = mirrored(masked[band_rows - 3 :], "lon")
    upper = jnp.where(top_band, fold_rows, above)
    tall = jnp.concatenate([below, masked, upper], axis=0)
    padded = with_col_halo(tall, 3).astype(jnp.float32)

    start = jnp.zeros((band_rows, band_cols, channels), jnp.float32) + conv_bias
    conv_out = correlate(padded, kernel, start)
    cell_count = band_rows * band_cols
    result, conv_grad = pointwise(
        conv_out.reshape(cell_count, channels),
        ocean_state.reshape(cell_count, channels),
        keep_mask.reshape(cell_count, 1),
        cotangent.reshape(cell_count, channels),
        norm_gain,
        norm_bias,
        w_expand,
        b_expand,
        w_reduce,
        b_reduce,
        layer_scale,
    )
    conv_grad = conv_grad.reshape(band_rows, band_cols, channels)

    grad_below = from_behind(conv_grad[band_rows - 3 :], "lat", 1)
    grad_above = from_behind(conv_grad[:3], "lat", -1)
    grad_tall = jnp.concatenate(
        [grad_below, conv_grad, grad_above, jnp.zeros_like(grad_above)], axis=0
    )
    grad_wide = with_col_halo(grad_tall, 3)
    flipped = kernel[::-1, ::-1]
    spread = correlate(
        grad_wide, flipped, jnp.zeros((band_rows + 3, band_cols, channels), jnp.float32)
    )
    fold_grad = mirrored(spread[band_rows:], "lon")
    fold_term = jnp.where(top_band, fold_grad, jnp.zeros_like(fold_grad))
    masked_grad = spread[:band_rows] + jnp.pad(fold_term, ((band_rows - 3, 0), (0, 0), (0, 0)))
    state_grad = (keep_mask * (cotangent.astype(jnp.float32) + masked_grad)).astype(jnp.bfloat16)
    return (result.reshape(band_rows, band_cols, channels), state_grad)


def solution(mesh):
    placed = (
        P("lat", "lon", None),
        P("lat", "lon"),
        P(),
        P(),
        P(),
        P(),
        P(),
        P(),
        P(),
        P(),
        P(),
        P("lat", "lon", None),
    )
    return jax.shard_map(
        body,
        mesh=mesh,
        in_specs=placed,
        out_specs=(P("lat", "lon", None), P("lat", "lon", None)),
        check_vma=False,
    )
```

time: 175 us -> 117 us (0.67)
  waiting for transfers between devices: 30.9 us -> 6.87 us
  local copies, waits for them, and re-layouts: 16.8 us -> 1.3 us
  other arithmetic: 64.9 us -> 51.8 us
  starting transfers between devices: 45.3 us -> 39.5 us
    add x2 -> x1, other arithmetic: 0.12 us -> 27.7 us  [correlate(): summed = summed + kernel[row_tap, col_tap].astype(jnp.float32) * window]
    mul x6 -> x3, other arithmetic: 22.6 us -> 0.03 us  [correlate(): summed = summed + kernel[row_tap, col_tap].astype(jnp.float32) * window]
    another operation x1 -> x0, other arithmetic: 21 us -> none
    all_to_all x4 -> x0, waiting for transfers between devices: 19.3 us -> none  [the longest x1 6.66 us: fold_forward(): lax.all_to_all(mirrored[None], 'lon', split_axis=3, concat_axis=0, tiled=...]
    all_to_all x4 -> x0, starting transfers between devices: 19.2 us -> none  [the longest x1 7.18 us: fold_backward(): lax.all_to_all(for_sending(spread[::-1]), 'lon', split_axis=0, concat_axi...]
    ppermute x4 -> x2, waiting for transfers between devices: 10.3 us -> 0.01 us  [mirrored(): lax.ppermute(value[::-1, ::-1], axis, [(i, count - 1 - i) for i in range(...]
    scatter-add x2 -> x0, local copies, waits for them, and re-layouts: 8.8 us -> none  [body(): col_core.at[:, :3].add(from_left).at[:, band_cols - 3:].add(from_right)]
    ppermute x2 -> x4, starting transfers between devices: 5.82 us -> 12.1 us  [shifted(): return lax.ppermute(block, axis, route)]
  transfers between devices with their start and end apart: 12 -> 10, of which waited for: 7 -> 4; matrix products, arithmetic and copies ran while one was open for 8% -> 7% of each run, Pallas kernels for 0% -> 0%
where the time goes in v1:
time: 117 us; the launch traced here: 114 us
  other arithmetic  51.8 us (44%)
  starting transfers between devices  39.5 us (34%)
  matrix products  13.6 us (12%)
  waiting for transfers between devices  6.87 us (6%)
  local copies, waits for them, and re-layouts  1.3 us (1%)
  between operations  1.18 us (1%)
    add x1, other arithmetic, correlate(): summed = summed + kernel[row_tap, col_tap].astype(jnp.float32) * window  27.7 us
    ppermute x4, starting transfers between devices, from_behind(): lax.ppermute(value, axis, [(source, source + steps) for source in range(l...  15 us
    ppermute x2, starting transfers between devices, mirrored(): lax.ppermute(value[::-1, ::-1], axis, [(i, count - 1 - i) for i in range(...  12.3 us
    ppermute x4, starting transfers between devices, shifted(): return lax.ppermute(block, axis, route)  12.1 us
    reduce_sum x1, other arithmetic, pointwise(): row_mean = jnp.mean(conv_out, axis=-1, keepdims=True)  9.48 us
    dot_general x1, matrix products, pointwise(): jnp.dot(grad_hidden, w_expand.T, preferred_element_type=jnp.float32)  6.14 us
    ppermute x4, waiting for transfers between devices, from_behind(): lax.ppermute(value, axis, [(source, source + steps) for source in range(l...  4.44 us
    dot_general x1, matrix products, pointwise(): jnp.dot(activated, w_reduce, preferred_element_type=jnp.float32) + b_reduce  4.32 us
  transfers between devices with their start and end apart: 10, of which 4 were waited for; matrix products, arithmetic and copies ran while one was open for 7% of the time, Pallas kernels for 0%

profile of v1, /device:TPU:1, one launch (start us, length us, event | category | flops | bytes accessed | tf_op | source)
XLA Modules:
  0.0 114.3 jit_solution(416958502038917610)
XLA Ops:
  0.7 0.8 convert_element_type.243
  1.5 0.1 copy.15
  1.6 1.5 %multiply_convert_fusion.2 = bf16[80,32,128]{2,1,0:T(8,128)(2,1)S(1)} fusion(f32[80,32]{1,0:T(8,128)S(1)} %copy.15, bf16[80,32,128]{2,1,0:T(8,128)(2,1)} %param.12), kind=kLoop, calls=%fused_computation.228 | loop fusion | flops 983040 | bytes 1320960 | tf_op jit(solution)/shard_map/convert_element_type | solution.py:104
  3.1 6.0 %collective-permute-start = (bf16[3,32,128]{2,1,0:T(8,128)(2,1)S(1)}, bf16[3,32,128]{2,1,0:T(8,128)(2,1)S(1)}, u32[]{:S(2)}, u32[]{:S(2)}) collective-permute-start(bf16[3,32,128]{2,1,0:T(8,128)(2,1)S(1)} %get-tuple-element.17), channel_id=1, source_target_pairs={{0,1},{1,2},{2,3},{4,5},{5,6},{6,7},{8,9},{9,10},{10,11},{12,13},{... | collective-permute-start | bytes 73736 | tf_op jit(solution)/shard_map/ppermute | solution.py:16
  9.1 6.3 %collective-permute-start.1 = (bf16[3,32,128]{2,1,0:T(8,128)(2,1)S(1)}, bf16[3,32,128]{2,1,0:T(8,128)(2,1)S(1)}, u32[]{:S(2)}, u32[]{:S(2)}) collective-permute-start(bf16[3,32,128]{2,1,0:T(8,128)(2,1)S(1)} %rev.7), channel_id=1, source_target_pairs={{0,124},{4,120},{8,116},{12,112},{16,108},{20,104},{24,100},{28,96... | collective-permute-start | bytes 73736 | tf_op jit(solution)/shard_map/ppermute | solution.py:21
  15.5 1.9 %collective-permute-start.2 = (bf16[3,32,128]{2,1,0:T(8,128)(2,1)S(1)}, bf16[3,32,128]{2,1,0:T(8,128)(2,1)S(1)}, u32[]{:S(2)}, u32[]{:S(2)}) collective-permute-start(bf16[3,32,128]{2,1,0:T(8,128)(2,1)S(1)} %get-tuple-element.16), channel_id=1, source_target_pairs={{1,0},{2,1},{3,2},{5,4},{6,5},{7,6},{9,8},{10,9},{11,10},{13,12},{... | collective-permute-start | bytes 73736 | tf_op jit(solution)/shard_map/ppermute | solution.py:16
  17.4 0.1 mul.1150
  17.5 1.2 %fusion.111 = bf16[2560,128]{1,0:T(8,128)(2,1)} fusion(f32[128]{0:T(128)S(1)} %copy-done.25, f32[2560]{0:T(1024)S(1)} %mul.1150, bf16[80,32,128]{2,1,0:T(8,128)(2,1)S(1)} %copy-done.2), kind=kLoop, calls=%fused_computation.221 | loop fusion | flops 1310720 | bytes 1321472 | tf_op jit(solution)/shard_map/convert_element_type | solution.py:74
  18.8 3.3 %collective-permute-done.2 = bf16[3,32,128]{2,1,0:T(8,128)(2,1)S(1)} collective-permute-done((bf16[3,32,128]{2,1,0:T(8,128)(2,1)S(1)}, bf16[3,32,128]{2,1,0:T(8,128)(2,1)S(1)}, u32[]{:S(2)}, u32[]{:S(2)}) %collective-permute-start.2) | collective-permute-done | bytes 24608 | tf_op jit(solution)/shard_map/ppermute | solution.py:16
  22.2 0.1 collective-permute-start.3
  22.3 5.7 %collective-permute-start.4 = (bf16[86,3,128]{2,1,0:T(4,128)(2,1)S(1)}, bf16[86,3,128]{2,1,0:T(4,128)(2,1)S(1)}, u32[]{:S(2)}, u32[]{:S(2)}) collective-permute-start(bf16[86,3,128]{2,1,0:T(4,128)(2,1)S(1)} %get-tuple-element.15), channel_id=1, source_target_pairs={{4,0},{8,4},{12,8},{16,12},{20,16},{24,20},{28,24},{32,28},{36,32}... | collective-permute-start | bytes 198152 | tf_op jit(solution)/shard_map/ppermute | solution.py:10
  28.1 1.8 %collective-permute-done.3 = bf16[86,3,128]{2,1,0:T(4,128)(2,1)S(1)} collective-permute-done((bf16[86,3,128]{2,1,0:T(4,128)(2,1)S(1)}, bf16[86,3,128]{2,1,0:T(4,128)(2,1)S(1)}, u32[]{:S(2)}, u32[]{:S(2)}) %collective-permute-start.3) | collective-permute-done | bytes 66080 | tf_op jit(solution)/shard_map/ppermute | solution.py:10
  29.8 0.4 maximum_convert_fusion
  30.4 9.5 %fusion.118 = (f32[80,32]{1,0:T(8,128)S(1)}, f32[80,32,128]{2,1,0:T(8,128)S(1)}) fusion(f32[86,38,128]{2,1,0:T(8,128)S(1)} %maximum_convert_fusion, f32[128]{0:T(128)S(1)} %get-tuple-element.65, f32[128]{0:T(128)S(1)} %get-tuple-element.66, f32[128]{0:T(128)S(1)} %get-tuple-element.19, f32[128]{0:T(128)S(1)} %get-tuple-element.20, ...), kind=kLoop, calls=%fused_computation.297 | loop fusion | flops 32437760 | bytes 65571840 | tf_op jit(solution)/shard_map/reduce_sum | solution.py:63
  40.0 0.8 multiply_reduce_fusion.1
  40.9 1.5 %add_convert_fusion = bf16[2560,128]{1,0:T(8,128)(2,1)S(1)} fusion(f32[80,32,128]{2,1,0:T(8,128)S(1)} %get-tuple-element.5, f32[128]{0:T(128)S(1)} %copy-done.23, f32[128]{0:T(128)S(1)} %copy-done.24, f32[2560]{0:T(1024)S(1)} %rsqrt.12, f32[2560]{0:T(1024)S(1)} %div.15), kind=kLoop, calls=%fused_computation.226 | loop fusion | flops 1638400 | bytes 1987584 | tf_op jit(solution)/shard_map/convert_element_type | solution.py:67
  42.4 3.2 %convolution_add_fusion = f32[2560,512]{1,0:T(8,128)} fusion(bf16[2560,128]{1,0:T(8,128)(2,1)S(1)} %add_convert_fusion, bf16[128,512]{1,0:T(8,128)(2,1)S(1)} %copy-done, f32[512]{0:T(512)S(1)} %copy-done.6), kind=kOutput, calls=%fused_computation.9 | convolution fusion | flops 336855040 | bytes 6031360 | tf_op jit(solution)/shard_map/dot_general | solution.py:68
  45.6 6.1 %fusion.117 = (f32[2560]{0:T(1024)S(1)}, f32[2560]{0:T(1024)S(1)}, f32[2560,128]{1,0:T(8,128)}) fusion(f32[2560]{0:T(1024)S(1)} %rsqrt.12, f32[2560]{0:T(1024)S(1)} %div.15, f32[80,32,128]{2,1,0:T(8,128)S(1)} %get-tuple-element.5, f32[128]{0:T(128)S(1)} %copy-done.24, bf16[128,512]{1,0:T(8,128)(2,1)S(1)} %copy-done, f32[2560,512]{1,0:T(8,128)} %convolution_add_fusion, ...), kind=kOutput, calls=%fused_computation.296 | convolution fusion | flops 686156800 | bytes 8823296 | tf_op jit(solution)/shard_map/dot_general | solution.py:77
  51.7 3.5 %subtract_multiply_fusion = f32[2560,128]{1,0:T(8,128)S(1)} fusion(f32[2560,128]{1,0:T(8,128)} %get-tuple-element.67, f32[80,32,128]{2,1,0:T(8,128)S(1)} %get-tuple-element.5, f32[2560]{0:T(1024)S(1)} %get-tuple-element.68, f32[2560]{0:T(1024)S(1)} %get-tuple-element.69, f32[2560]{0:T(1024)S(1)} %rsqrt.12, f32[2560]{0:T(1024)S(1)} %div.15), kind=kLoop, calls=%fused_computation.224 | loop fusion | flops 1966080 | bytes 3973120 | tf_op jit(solution)/shard_map/mul | solution.py:79
  55.2 1.9 %collective-permute-start.6 = (f32[3,32,128]{2,1,0:T(8,128)S(1)}, f32[3,32,128]{2,1,0:T(8,128)S(1)}, u32[]{:S(2)}, u32[]{:S(2)}) collective-permute-start(f32[3,32,128]{2,1,0:T(8,128)S(1)} %bitcast.179), channel_id=1, source_target_pairs={{1,0},{2,1},{3,2},{5,4},{6,5},{7,6},{9,8},{10,9},{11,10},{13,12},{... | collective-permute-start | bytes 147464 | tf_op jit(solution)/shard_map/ppermute | solution.py:16
  57.1 5.1 %collective-permute-start.5 = (f32[3,32,128]{2,1,0:T(8,128)S(1)}, f32[3,32,128]{2,1,0:T(8,128)S(1)}, u32[]{:S(2)}, u32[]{:S(2)}) collective-permute-start(f32[3,32,128]{2,1,0:T(8,128)S(1)} %bitcast.178), channel_id=1, source_target_pairs={{0,1},{1,2},{2,3},{4,5},{5,6},{6,7},{8,9},{9,10},{10,11},{12,13},{... | collective-permute-start | bytes 147464 | tf_op jit(solution)/shard_map/ppermute | solution.py:16
  62.3 1.1 %collective-permute-done.5 = f32[3,32,128]{2,1,0:T(8,128)S(1)} collective-permute-done((f32[3,32,128]{2,1,0:T(8,128)S(1)}, f32[3,32,128]{2,1,0:T(8,128)S(1)}, u32[]{:S(2)}, u32[]{:S(2)}) %collective-permute-start.5) | collective-permute-done | bytes 49184 | tf_op jit(solution)/shard_map/ppermute | solution.py:16
  63.5 0.1 collective-permute-start.7
  63.6 6.3 %collective-permute-start.8 = (f32[89,3,128]{2,1,0:T(4,128)S(1)}, f32[89,3,128]{2,1,0:T(4,128)S(1)}, u32[]{:S(2)}, u32[]{:S(2)}) collective-permute-start(f32[89,3,128]{2,1,0:T(4,128)S(1)} %get-tuple-element.9), channel_id=1, source_target_pairs={{4,0},{8,4},{12,8},{16,12},{20,16},{24,20},{28,24},{32,28},{36,32}... | collective-permute-start | bytes 410120 | tf_op jit(solution)/shard_map/ppermute | solution.py:10
  69.9 2.0 %pad_maximum_fusion.1 = (f32[86,32,128]{2,1,0:T(8,128)}, f32[86,32,128]{2,1,0:T(8,128)}) fusion(f32[3,32,128]{2,1,0:T(8,128)S(1)} %collective-permute-done.6, f32[80,32,128]{2,1,0:T(8,128)S(1)} %bitcast.174, f32[3,32,128]{2,1,0:T(8,128)S(1)} %collective-permute-done.5, f32[3,32,128]{2,1,0:T(8,128)S(1)} %broadcast.68), kind=kLoop, calls=%fused_computation.19 | loop fusion | flops 1409024 | bytes 4276224 | tf_op jit(solution)/shard_map/concatenate | solution.py:133
  71.9 0.7 collective-permute-done.7
  72.5 1.6 %maximum_maximum_fusion = (f32[89,35,128]{2,1,0:T(8,128)S(1)}, f32[89,35,128]{2,1,0:T(8,128)}) fusion(f32[3,32,128]{2,1,0:T(8,128)S(1)} %broadcast.68, f32[3,32,128]{2,1,0:T(8,128)S(1)} %collective-permute-done.6, f32[80,32,128]{2,1,0:T(8,128)S(1)} %bitcast.175, f32[3,32,128]{2,1,0:T(8,128)S(1)} %collective-permute-done.5, ...), kind=kLoop, calls=%fused_computation.17 | loop fusion | flops 3189760 | bytes 4921344 | tf_op jit(solution)/shard_map/concatenate | solution.py:27
  74.1 27.7 %fusion.11 = f32[83,32,128]{2,1,0:T(8,128)} fusion(f32[89,35,128]{2,1,0:T(8,128)} %get-tuple-element.7, f32[86,32,128]{2,1,0:T(8,128)} %get-tuple-element.11, f32[89,35,128]{2,1,0:T(8,128)S(1)} %get-tuple-element.6, f32[86,32,128]{2,1,0:T(8,128)} %get-tuple-element.10, f32[80,32,128]{2,1,0:T(8,128)S(1)} %bitcast.176, ...), kind=kLoop, calls=%fused_computation.22 | loop fusion | flops 33656832 | bytes 66707968 | tf_op jit(solution)/shard_map/add | solution.py:46
  101.8 0.8 slice.879
  102.6 6.0 %collective-permute-start.9 = (f32[3,32,128]{2,1,0:T(8,128)S(1)}, f32[3,32,128]{2,1,0:T(8,128)S(1)}, u32[]{:S(2)}, u32[]{:S(2)}) collective-permute-start(f32[3,32,128]{2,1,0:T(8,128)S(1)} %rev.8), channel_id=1, source_target_pairs={{0,124},{4,120},{8,116},{12,112},{16,108},{20,104},{24,100},{28,96... | collective-permute-start | bytes 147464 | tf_op jit(solution)/shard_map/ppermute | solution.py:21
  108.7 4.3 %fusion.9 = bf16[2560,128]{1,0:T(8,128)(2,1)} fusion(bf16[512,128]{1,0:T(8,128)(2,1)} %param.20, f32[2560,512]{1,0:T(8,128)} %convolution_add_fusion, f32[128]{0:T(128)} %param.21, f32[128]{0:T(128)} %param.22, f32[2560]{0:T(1024)S(1)} %mul.1150, bf16[2560,128]{1,0:T(8,128)(2,1)} %bitcast.177), kind=kOutput, calls=%fused_computation.15 | convolution fusion | flops 344064000 | bytes 6695936 | tf_op jit(solution)/shard_map/dot_general | solution.py:70
  113.0 1.3 %fusion.61 = bf16[80,32,128]{2,1,0:T(8,128)(2,1)} fusion(f32[83,32,128]{2,1,0:T(8,128)S(1)} %copy-done.1, f32[3,32,128]{2,1,0:T(8,128)S(1)} %broadcast_select_fusion, f32[80,32]{1,0:T(8,128)S(1)} %copy.15, bf16[80,32,128]{2,1,0:T(8,128)(2,1)S(1)} %copy-done.3), kind=kLoop, calls=%fused_computation.121 | loop fusion | flops 1638400 | bytes 2680832 | tf_op jit(solution)/shard_map/convert_element_type | solution.py:144
  (77 shorter events, 0.6 us)
Async XLA Ops:
  0.6 41.7 %copy-start = (bf16[128,512]{1,0:T(8,128)(2,1)S(1)}, bf16[128,512]{1,0:T(8,128)(2,1)}, u32[]{:S(2)}) copy-start(bf16[128,512]{1,0:T(8,128)(2,1)} %param.18) | copy-start | bytes 393220
  0.6 16.8 %copy-start.5 = (bf16[7,7,128]{2,1,0:T(8,128)(2,1)S(1)}, bf16[7,7,128]{2,1,0:T(8,128)(2,1)}, u32[]{:S(2)}) copy-start(bf16[7,7,128]{2,1,0:T(8,128)(2,1)} %param.14) | copy-start | bytes 37636
  0.7 16.8 %copy-start.2 = (bf16[80,32,128]{2,1,0:T(8,128)(2,1)S(1)}, bf16[80,32,128]{2,1,0:T(8,128)(2,1)}, u32[]{:S(2)}) copy-start(bf16[80,32,128]{2,1,0:T(8,128)(2,1)} %param.23) | copy-start | bytes 1966084
  0.7 16.8 %copy-start.25 = (f32[128]{0:T(128)S(1)}, f32[128]{0:T(128)}, u32[]{:S(2)}) copy-start(f32[128]{0:T(128)} %param.22) | copy-start | bytes 1540
  3.1 19.0 %collective-permute-start = (bf16[3,32,128]{2,1,0:T(8,128)(2,1)S(1)}, bf16[3,32,128]{2,1,0:T(8,128)(2,1)S(1)}, u32[]{:S(2)}, u32[]{:S(2)}) collective-permute-start(bf16[3,32,128]{2,1,0:T(8,128)(2,1)S(1)} %get-tuple-element.17), channel_id=1, source_target_pairs={{0,1},{1,2},{2,3},{4,5},{5,6},{6,7},{8,9},{9,10},{10,11},{12,13},{... | collective-permute-start | bytes 73736 | tf_op jit(solution)/shard_map/ppermute | solution.py:16
  9.1 9.7 %collective-permute-start.1 = (bf16[3,32,128]{2,1,0:T(8,128)(2,1)S(1)}, bf16[3,32,128]{2,1,0:T(8,128)(2,1)S(1)}, u32[]{:S(2)}, u32[]{:S(2)}) collective-permute-start(bf16[3,32,128]{2,1,0:T(8,128)(2,1)S(1)} %rev.7), channel_id=1, source_target_pairs={{0,124},{4,120},{8,116},{12,112},{16,108},{20,104},{24,100},{28,96... | collective-permute-start | bytes 73736 | tf_op jit(solution)/shard_map/ppermute | solution.py:21
  15.5 6.6 %collective-permute-start.2 = (bf16[3,32,128]{2,1,0:T(8,128)(2,1)S(1)}, bf16[3,32,128]{2,1,0:T(8,128)(2,1)S(1)}, u32[]{:S(2)}, u32[]{:S(2)}) collective-permute-start(bf16[3,32,128]{2,1,0:T(8,128)(2,1)S(1)} %get-tuple-element.16), channel_id=1, source_target_pairs={{1,0},{2,1},{3,2},{5,4},{6,5},{7,6},{9,8},{10,9},{11,10},{13,12},{... | collective-permute-start | bytes 73736 | tf_op jit(solution)/shard_map/ppermute | solution.py:16
  18.8 11.5 %copy-start.7 = (f32[128]{0:T(128)}, f32[128]{0:T(128)S(1)}, u32[]{:S(2)}) copy-start(f32[128]{0:T(128)S(1)} %get-tuple-element.52) | copy-start | bytes 1540
  18.8 11.5 %copy-start.8 = (f32[128]{0:T(128)}, f32[128]{0:T(128)S(1)}, u32[]{:S(2)}) copy-start(f32[128]{0:T(128)S(1)} %get-tuple-element.53) | copy-start | bytes 1540
  18.8 11.5 %copy-start.9 = (f32[128]{0:T(128)}, f32[128]{0:T(128)S(1)}, u32[]{:S(2)}) copy-start(f32[128]{0:T(128)S(1)} %get-tuple-element.54) | copy-start | bytes 1540
  18.8 11.5 %copy-start.10 = (f32[128]{0:T(128)}, f32[128]{0:T(128)S(1)}, u32[]{:S(2)}) copy-start(f32[128]{0:T(128)S(1)} %get-tuple-element.55) | copy-start | bytes 1540
  22.2 7.6 %collective-permute-start.3 = (bf16[86,3,128]{2,1,0:T(4,128)(2,1)S(1)}, bf16[86,3,128]{2,1,0:T(4,128)(2,1)S(1)}, u32[]{:S(2)}, u32[]{:S(2)}) collective-permute-start(bf16[86,3,128]{2,1,0:T(4,128)(2,1)S(1)} %get-tuple-element.14), channel_id=1, source_target_pairs={{124,0},{0,4},{4,8},{8,12},{12,16},{16,20},{20,24},{24,28},{28,32}... | collective-permute-start | bytes 198152 | tf_op jit(solution)/shard_map/ppermute | solution.py:10
  22.3 7.6 %collective-permute-start.4 = (bf16[86,3,128]{2,1,0:T(4,128)(2,1)S(1)}, bf16[86,3,128]{2,1,0:T(4,128)(2,1)S(1)}, u32[]{:S(2)}, u32[]{:S(2)}) collective-permute-start(bf16[86,3,128]{2,1,0:T(4,128)(2,1)S(1)} %get-tuple-element.15), channel_id=1, source_target_pairs={{4,0},{8,4},{12,8},{16,12},{20,16},{24,20},{28,24},{32,28},{36,32}... | collective-permute-start | bytes 198152 | tf_op jit(solution)/shard_map/ppermute | solution.py:10
  28.0 2.3 %copy-start.12 = (f32[128]{0:T(128)}, f32[128]{0:T(128)S(1)}, u32[]{:S(2)}) copy-start(f32[128]{0:T(128)S(1)} %get-tuple-element.57) | copy-start | bytes 1540
  28.0 2.3 %copy-start.13 = (f32[128]{0:T(128)}, f32[128]{0:T(128)S(1)}, u32[]{:S(2)}) copy-start(f32[128]{0:T(128)S(1)} %get-tuple-element.58) | copy-start | bytes 1540
  28.0 2.3 %copy-start.14 = (f32[128]{0:T(128)}, f32[128]{0:T(128)S(1)}, u32[]{:S(2)}) copy-start(f32[128]{0:T(128)S(1)} %get-tuple-element.59) | copy-start | bytes 1540
  28.0 2.3 %copy-start.15 = (f32[128]{0:T(128)}, f32[128]{0:T(128)S(1)}, u32[]{:S(2)}) copy-start(f32[128]{0:T(128)S(1)} %get-tuple-element.60) | copy-start | bytes 1540
  28.0 2.3 %copy-start.16 = (f32[128]{0:T(128)}, f32[128]{0:T(128)S(1)}, u32[]{:S(2)}) copy-start(f32[128]{0:T(128)S(1)} %get-tuple-element.61) | copy-start | bytes 1540
  28.0 2.3 %copy-start.17 = (f32[128]{0:T(128)}, f32[128]{0:T(128)S(1)}, u32[]{:S(2)}) copy-start(f32[128]{0:T(128)S(1)} %get-tuple-element.62) | copy-start | bytes 1540
  28.0 2.3 %copy-start.18 = (f32[128]{0:T(128)}, f32[128]{0:T(128)S(1)}, u32[]{:S(2)}) copy-start(f32[128]{0:T(128)S(1)} %get-tuple-element.63) | copy-start | bytes 1540
  28.0 2.3 %copy-start.19 = (f32[128]{0:T(128)}, f32[128]{0:T(128)S(1)}, u32[]{:S(2)}) copy-start(f32[128]{0:T(128)S(1)} %get-tuple-element.64) | copy-start | bytes 1540
  28.0 2.3 %copy-start.20 = (f32[128]{0:T(128)}, f32[128]{0:T(128)S(1)}, u32[]{:S(2)}) copy-start(f32[128]{0:T(128)S(1)} %get-tuple-element.65) | copy-start | bytes 1540
  28.1 2.3 %copy-start.21 = (f32[128]{0:T(128)}, f32[128]{0:T(128)S(1)}, u32[]{:S(2)}) copy-start(f32[128]{0:T(128)S(1)} %get-tuple-element.66) | copy-start | bytes 1540
  42.4 3.2 %copy-start.4 = (bf16[2560,128]{1,0:T(8,128)(2,1)S(1)}, bf16[2560,128]{1,0:T(8,128)(2,1)}, u32[]{:S(2)}) copy-start(bf16[2560,128]{1,0:T(8,128)(2,1)} %fusion.111) | copy-start | bytes 1966084
  42.4 3.2 %copy-start.26 = (bf16[512,128]{1,0:T(8,128)(2,1)S(1)}, bf16[512,128]{1,0:T(8,128)(2,1)}, u32[]{:S(2)}) copy-start(bf16[512,128]{1,0:T(8,128)(2,1)} %param.20) | copy-start | bytes 393220
  55.2 7.1 %collective-permute-start.6 = (f32[3,32,128]{2,1,0:T(8,128)S(1)}, f32[3,32,128]{2,1,0:T(8,128)S(1)}, u32[]{:S(2)}, u32[]{:S(2)}) collective-permute-start(f32[3,32,128]{2,1,0:T(8,128)S(1)} %bitcast.179), channel_id=1, source_target_pairs={{1,0},{2,1},{3,2},{5,4},{6,5},{7,6},{9,8},{10,9},{11,10},{13,12},{... | collective-permute-start | bytes 147464 | tf_op jit(solution)/shard_map/ppermute | solution.py:16
  57.1 6.3 %collective-permute-start.5 = (f32[3,32,128]{2,1,0:T(8,128)S(1)}, f32[3,32,128]{2,1,0:T(8,128)S(1)}, u32[]{:S(2)}, u32[]{:S(2)}) collective-permute-start(f32[3,32,128]{2,1,0:T(8,128)S(1)} %bitcast.178), channel_id=1, source_target_pairs={{0,1},{1,2},{2,3},{4,5},{5,6},{6,7},{8,9},{9,10},{10,11},{12,13},{... | collective-permute-start | bytes 147464 | tf_op jit(solution)/shard_map/ppermute | solution.py:16
  63.5 9.0 %collective-permute-start.7 = (f32[89,3,128]{2,1,0:T(4,128)S(1)}, f32[89,3,128]{2,1,0:T(4,128)S(1)}, u32[]{:S(2)}, u32[]{:S(2)}) collective-permute-start(f32[89,3,128]{2,1,0:T(4,128)S(1)} %get-tuple-element.8), channel_id=1, source_target_pairs={{124,0},{0,4},{4,8},{8,12},{12,16},{16,20},{20,24},{24,28},{28,32}... | collective-permute-start | bytes 410120 | tf_op jit(solution)/shard_map/ppermute | solution.py:10
  63.6 8.9 %collective-permute-start.8 = (f32[89,3,128]{2,1,0:T(4,128)S(1)}, f32[89,3,128]{2,1,0:T(4,128)S(1)}, u32[]{:S(2)}, u32[]{:S(2)}) collective-permute-start(f32[89,3,128]{2,1,0:T(4,128)S(1)} %get-tuple-element.9), channel_id=1, source_target_pairs={{4,0},{8,4},{12,8},{16,12},{20,16},{24,20},{28,24},{32,28},{36,32}... | collective-permute-start | bytes 410120 | tf_op jit(solution)/shard_map/ppermute | solution.py:10
  102.6 10.3 %collective-permute-start.9 = (f32[3,32,128]{2,1,0:T(8,128)S(1)}, f32[3,32,128]{2,1,0:T(8,128)S(1)}, u32[]{:S(2)}, u32[]{:S(2)}) collective-permute-start(f32[3,32,128]{2,1,0:T(8,128)S(1)} %rev.8), channel_id=1, source_target_pairs={{0,124},{4,120},{8,116},{12,112},{16,108},{20,104},{24,100},{28,96... | collective-permute-start | bytes 147464 | tf_op jit(solution)/shard_map/ppermute | solution.py:21
  108.7 4.3 %copy-start.1 = (f32[83,32,128]{2,1,0:T(8,128)S(1)}, f32[83,32,128]{2,1,0:T(8,128)}, u32[]{:S(2)}) copy-start(f32[83,32,128]{2,1,0:T(8,128)} %fusion.11) | copy-start | bytes 4079620
  108.7 4.4 %copy-start.3 = (bf16[80,32,128]{2,1,0:T(8,128)(2,1)S(1)}, bf16[80,32,128]{2,1,0:T(8,128)(2,1)}, u32[]{:S(2)}) copy-start(bf16[80,32,128]{2,1,0:T(8,128)(2,1)} %param.23) | copy-start | bytes 1966084
  (5 other events, 8.2 us)

commit v2 on v1

--- a/solution.py
+++ b/solution.py
@@ -2,6 +2,8 @@
 import jax.numpy as jnp
 from jax import lax
 from jax.sharding import PartitionSpec as P
+from jax.experimental import pallas as pl
+from jax.experimental.pallas import tpu as pltpu
 
 
 def shifted(block, axis, distance):
@@ -36,15 +38,31 @@
     return cumulative + values * jnp.exp(-0.5 * values * values) * 0.3989422804014327
 
 
-def correlate(padded, kernel, start):
-    out_rows = padded.shape[0] - 6
-    out_cols = padded.shape[1] - 6
-    summed = start
-    for row_tap in range(7):
-        for col_tap in range(7):
-            window = padded[row_tap : row_tap + out_rows, col_tap : col_tap + out_cols]
-            summed = summed + kernel[row_tap, col_tap].astype(jnp.float32) * window
-    return summed
+def correlate(padded, kernel, start, block=4):
+    in_rows, in_cols, chans = padded.shape
+    out_rows, out_cols = in_rows - 6, in_cols - 6
+    steps = -(-out_rows // block)
+    taps = kernel.astype(jnp.float32).reshape(49, 1, chans)
+
+    def run(x_ref, k_ref, s_ref, o_ref):
+        def step(i, carry):
+            r0 = jnp.minimum(i * block, out_rows - block)
+            acc = jnp.broadcast_to(s_ref[...], (block, out_cols, chans))
+            for row_tap in range(7):
+                for col_tap in range(7):
+                    window = x_ref[pl.ds(r0 + row_tap, block), pl.ds(col_tap, out_cols), :]
+                    acc = acc + k_ref[row_tap * 7 + col_tap] * window
+            o_ref[pl.ds(r0, block)] = acc
+            return carry
+
+        lax.fori_loop(0, steps, step, 0)
+
+    return pl.pallas_call(
+        run,
+        out_shape=jax.ShapeDtypeStruct((out_rows, out_cols, chans), jnp.float32),
+        in_specs=[pl.BlockSpec(memory_space=pltpu.VMEM)] * 3,
+        out_specs=pl.BlockSpec(memory_space=pltpu.VMEM),
+    )(padded, taps, start.reshape(1, chans))
 
 
 def pointwise(
@@ -110,8 +128,7 @@
     tall = jnp.concatenate([below, masked, upper], axis=0)
     padded = with_col_halo(tall, 3).astype(jnp.float32)
 
-    start = jnp.zeros((band_rows, band_cols, channels), jnp.float32) + conv_bias
-    conv_out = correlate(padded, kernel, start)
+    conv_out = correlate(padded, kernel, conv_bias)
     cell_count = band_rows * band_cols
     result, conv_grad = pointwise(
         conv_out.reshape(cell_count, channels),
@@ -135,9 +152,7 @@
     )
     grad_wide = with_col_halo(grad_tall, 3)
     flipped = kernel[::-1, ::-1]
-    spread = correlate(
-        grad_wide, flipped, jnp.zeros((band_rows + 3, band_cols, channels), jnp.float32)
-    )
+    spread = correlate(grad_wide, flipped, jnp.zeros((channels,), jnp.float32))
     fold_grad = mirrored(spread[band_rows:], "lon")
     fold_term = jnp.where(top_band, fold_grad, jnp.zeros_like(fold_grad))
     masked_grad = spread[:band_rows] + jnp.pad(fold_term, ((band_rows - 3, 0), (0, 0), (0, 0)))

time: 117 us -> 99.7 us (0.85); the launches traced: 114 us -> 99.2 us
  other arithmetic: 51.8 us -> 14.8 us
  Pallas kernels: 0 us -> 16.9 us
  waiting for transfers between devices: 6.87 us -> 8.84 us
  local copies, waits for them, and re-layouts: 1.3 us -> 3.06 us
  starting transfers between devices: 39.5 us -> 41.2 us
    add x1 -> x0, other arithmetic: 27.7 us -> none  [correlate(): summed = summed + kernel[row_tap, col_tap].astype(jnp.float32) * window]
    pallas_call x0 -> x2, Pallas kernels: none -> 16.9 us  [correlate(): pl.pallas_call(run, out_shape=jax.ShapeDtypeStruct((out_rows, out_cols, c...]
    reduce_sum x1, other arithmetic: 9.48 us -> 1.83 us  [pointwise(): row_mean = jnp.mean(conv_out, axis=-1, keepdims=True)]
    concatenate x1 -> x0, other arithmetic: 1.98 us -> none  [body(): jnp.concatenate([grad_below, conv_grad, grad_above, jnp.zeros_like(grad_a...]
    reshape x0 -> x3, local copies, waits for them, and re-layouts: none -> 1.8 us  [the longest x2 1.29 us: correlate(): taps = kernel.astype(jnp.float32).reshape(49, 1, chans)]
    ppermute x2, starting transfers between devices: 12.3 us -> 13.8 us  [mirrored(): lax.ppermute(value[::-1, ::-1], axis, [(i, count - 1 - i) for i in range(...]
    ppermute x4, waiting for transfers between devices: 4.44 us -> 5.79 us  [from_behind(): lax.ppermute(value, axis, [(source, source + steps) for source in range(l...]
    convert_element_type x1, other arithmetic: 0.39 us -> 1.63 us  [body(): padded = with_col_halo(tall, 3).astype(jnp.float32)]
  transfers between devices with their start and end apart: 10 -> 10, of which waited for: 4 -> 4; matrix products, arithmetic and copies ran while one was open for 7% -> 6% of each run, Pallas kernels for 0% -> 0%
where the time goes in v2:
time: 99.7 us; the launch traced here: 99.2 us
  starting transfers between devices  41.2 us (41%)
  Pallas kernels  16.9 us (17%)
  other arithmetic  14.8 us (15%)
  matrix products  13.4 us (13%)
  waiting for transfers between devices  8.84 us (9%)
  local copies, waits for them, and re-layouts  3.06 us (3%)
    pallas_call x2, Pallas kernels, correlate(): pl.pallas_call(run, out_shape=jax.ShapeDtypeStruct((out_rows, out_cols, c...  16.9 us
    ppermute x4, starting transfers between devices, from_behind(): lax.ppermute(value, axis, [(source, source + steps) for source in range(l...  15.9 us
    ppermute x2, starting transfers between devices, mirrored(): lax.ppermute(value[::-1, ::-1], axis, [(i, count - 1 - i) for i in range(...  13.8 us
    ppermute x4, starting transfers between devices, shifted(): return lax.ppermute(block, axis, route)  11.5 us
    dot_general x1, matrix products, pointwise(): jnp.dot(grad_hidden, w_expand.T, preferred_element_type=jnp.float32)  6.18 us
    ppermute x4, waiting for transfers between devices, from_behind(): lax.ppermute(value, axis, [(source, source + steps) for source in range(l...  5.79 us
    dot_general x1, matrix products, pointwise(): jnp.dot(activated, w_reduce, preferred_element_type=jnp.float32) + b_reduce  4.12 us
    mul x1, other arithmetic, pointwise(): inv_std * (grad_scaled - jnp.mean(grad_scaled, axis=-1, keepdims=True) -...  3.47 us
  transfers between devices with their start and end apart: 10, of which 4 were waited for; matrix products, arithmetic and copies ran while one was open for 6% of the time, Pallas kernels for 0%

profile of v2, /device:TPU:1, one launch (start us, length us, event | category | flops | bytes accessed | tf_op | source)
XLA Modules:
  0.0 99.2 jit_solution(11982564310141485227)
XLA Ops:
  0.7 0.8 convert_element_type.49
  1.5 0.1 copy.15
  1.5 1.5 %multiply_convert_fusion.2 = bf16[80,32,128]{2,1,0:T(8,128)(2,1)S(1)} fusion(f32[80,32]{1,0:T(8,128)S(1)} %copy.15, bf16[80,32,128]{2,1,0:T(8,128)(2,1)} %param.12), kind=kLoop, calls=%fused_computation.30 | loop fusion | flops 983040 | bytes 1320960 | tf_op jit(solution)/shard_map/convert_element_type | solution.py:122
  3.1 8.0 %collective-permute-start.1 = (bf16[3,32,128]{2,1,0:T(8,128)(2,1)S(1)}, bf16[3,32,128]{2,1,0:T(8,128)(2,1)S(1)}, u32[]{:S(2)}, u32[]{:S(2)}) collective-permute-start(bf16[3,32,128]{2,1,0:T(8,128)(2,1)S(1)} %rev.9), channel_id=1, source_target_pairs={{0,124},{4,120},{8,116},{12,112},{16,108},{20,104},{24,100},{28,96... | collective-permute-start | bytes 73736 | tf_op jit(solution)/shard_map/ppermute | solution.py:23
  11.1 2.9 %collective-permute-start.2 = (bf16[3,32,128]{2,1,0:T(8,128)(2,1)S(1)}, bf16[3,32,128]{2,1,0:T(8,128)(2,1)S(1)}, u32[]{:S(2)}, u32[]{:S(2)}) collective-permute-start(bf16[3,32,128]{2,1,0:T(8,128)(2,1)S(1)} %get-tuple-element.10), channel_id=1, source_target_pairs={{1,0},{2,1},{3,2},{5,4},{6,5},{7,6},{9,8},{10,9},{11,10},{13,12},{... | collective-permute-start | bytes 73736 | tf_op jit(solution)/shard_map/ppermute | solution.py:18
  14.0 4.3 %collective-permute-start = (bf16[3,32,128]{2,1,0:T(8,128)(2,1)S(1)}, bf16[3,32,128]{2,1,0:T(8,128)(2,1)S(1)}, u32[]{:S(2)}, u32[]{:S(2)}) collective-permute-start(bf16[3,32,128]{2,1,0:T(8,128)(2,1)S(1)} %get-tuple-element.11), channel_id=1, source_target_pairs={{0,1},{1,2},{2,3},{4,5},{5,6},{6,7},{8,9},{9,10},{10,11},{12,13},{... | collective-permute-start | bytes 73736 | tf_op jit(solution)/shard_map/ppermute | solution.py:18
  18.4 0.8 collective-permute-done
  19.3 5.7 %collective-permute-start.4 = (bf16[86,3,128]{2,1,0:T(4,128)(2,1)S(1)}, bf16[86,3,128]{2,1,0:T(4,128)(2,1)S(1)}, u32[]{:S(2)}, u32[]{:S(2)}) collective-permute-start(bf16[86,3,128]{2,1,0:T(4,128)(2,1)S(1)} %get-tuple-element.9), channel_id=1, source_target_pairs={{4,0},{8,4},{12,8},{16,12},{20,16},{24,20},{28,24},{32,28},{36,32}... | collective-permute-start | bytes 198152 | tf_op jit(solution)/shard_map/ppermute | solution.py:12
  25.0 0.4 fusion.14
  25.4 0.6 reshape.95.k_ref
  26.1 0.8 collective-permute-done.3
  26.9 1.6 %maximum_convert_fusion.x_ref = f32[86,38,128]{2,1,0:T(8,128)} fusion(bf16[86,3,128]{2,1,0:T(4,128)(2,1)S(1)} %collective-permute-done.4, bf16[3,32,128]{2,1,0:T(8,128)(2,1)S(1)} %broadcast_select_fusion.1, bf16[80,32,128]{2,1,0:T(8,128)(2,1)S(1)} %multiply_convert_fusion.2, bf16[3,32,128]{2,1,0:T(8,128)(2,1)S(1)} %collective-permute-done, ...), kind=kLoop, calls=%fused_computation.31 | loop fusion | flops 4183040 | bytes 2509824 | tf_op jit(solution)/shard_map/convert_element_type | solution.py:129
  28.5 8.2 %shard_map.131 = f32[80,32,128]{2,1,0:T(8,128)} custom-call(f32[86,38,128]{2,1,0:T(8,128)} %maximum_convert_fusion.x_ref, f32[49,1,128]{2,1,0:T(1,128)} %reshape.95.k_ref, f32[1,128]{1,0:T(1,128)} %bitcast.32), custom_call_target="tpu_custom_call" | custom-call | tf_op jit(solution)/shard_map/pallas_call | solution.py:60
  36.7 1.8 %reduce_sum.36 = f32[80,32]{1,0:T(8,128)S(1)} reduce(f32[80,32,128]{2,1,0:T(8,128)} %shard_map.131, f32[]{:T(128)} %constant.12.clone.1), dimensions={2}, to_apply=%region_0.1 | reduce | flops 325120 | bytes 1320964 | tf_op jit(solution)/shard_map/reduce_sum | solution.py:81
  38.6 0.8 multiply_reduce_fusion.1
  39.6 1.5 %add_convert_fusion = bf16[2560,128]{1,0:T(8,128)(2,1)S(1)} fusion(f32[80,32,128]{2,1,0:T(8,128)S(1)} %copy-done.1, f32[128]{0:T(128)S(1)} %copy-done.7, f32[128]{0:T(128)S(1)} %copy-done.8, f32[2560]{0:T(1024)S(1)} %rsqrt.12, f32[2560]{0:T(1024)S(1)} %div.15), kind=kLoop, calls=%fused_computation.28 | loop fusion | flops 1638400 | bytes 1987584 | tf_op jit(solution)/shard_map/convert_element_type | solution.py:85
  41.1 3.1 %convolution_add_fusion = f32[2560,512]{1,0:T(8,128)} fusion(bf16[2560,128]{1,0:T(8,128)(2,1)S(1)} %add_convert_fusion, bf16[128,512]{1,0:T(8,128)(2,1)S(1)} %copy-done, f32[512]{0:T(512)S(1)} %copy-done.6), kind=kOutput, calls=%fused_computation.9 | convolution fusion | flops 336855040 | bytes 6031360 | tf_op jit(solution)/shard_map/dot_general | solution.py:86
  44.2 6.2 %fusion.20 = (f32[2560]{0:T(1024)S(1)}, f32[2560]{0:T(1024)S(1)}, f32[2560,128]{1,0:T(8,128)}) fusion(f32[2560]{0:T(1024)S(1)} %rsqrt.12, f32[2560]{0:T(1024)S(1)} %div.15, f32[80,32,128]{2,1,0:T(8,128)S(1)} %copy-done.1, f32[128]{0:T(128)S(1)} %copy-done.8, bf16[128,512]{1,0:T(8,128)(2,1)S(1)} %copy-done, f32[2560,512]{1,0:T(8,128)} %convolution_add_fusion, ...), kind=kOutput, calls=%fused_computation.49 | convolution fusion | flops 686156800 | bytes 8823296 | tf_op jit(solution)/shard_map/dot_general | solution.py:95
  50.4 3.5 %subtract_multiply_fusion = f32[2560,128]{1,0:T(8,128)S(1)} fusion(f32[2560,128]{1,0:T(8,128)} %get-tuple-element.12, f32[80,32,128]{2,1,0:T(8,128)S(1)} %copy-done.1, f32[2560]{0:T(1024)S(1)} %get-tuple-element.13, f32[2560]{0:T(1024)S(1)} %get-tuple-element.14, f32[2560]{0:T(1024)S(1)} %rsqrt.12, f32[2560]{0:T(1024)S(1)} %div.15), kind=kLoop, calls=%fused_computation.26 | loop fusion | flops 1966080 | bytes 3973120 | tf_op jit(solution)/shard_map/mul | solution.py:97
  53.9 6.9 %collective-permute-start.5 = (f32[3,32,128]{2,1,0:T(8,128)S(1)}, f32[3,32,128]{2,1,0:T(8,128)S(1)}, u32[]{:S(2)}, u32[]{:S(2)}) collective-permute-start(f32[3,32,128]{2,1,0:T(8,128)S(1)} %bitcast.31), channel_id=1, source_target_pairs={{0,1},{1,2},{2,3},{4,5},{5,6},{6,7},{8,9},{9,10},{10,11},{12,13},{... | collective-permute-start | bytes 147464 | tf_op jit(solution)/shard_map/ppermute | solution.py:18
  60.7 1.9 %collective-permute-start.6 = (f32[3,32,128]{2,1,0:T(8,128)S(1)}, f32[3,32,128]{2,1,0:T(8,128)S(1)}, u32[]{:S(2)}, u32[]{:S(2)}) collective-permute-start(f32[3,32,128]{2,1,0:T(8,128)S(1)} %bitcast.30), channel_id=1, source_target_pairs={{1,0},{2,1},{3,2},{5,4},{6,5},{7,6},{9,8},{10,9},{11,10},{13,12},{... | collective-permute-start | bytes 147464 | tf_op jit(solution)/shard_map/ppermute | solution.py:18
  62.7 5.0 %collective-permute-done.6 = f32[3,32,128]{2,1,0:T(8,128)S(1)} collective-permute-done((f32[3,32,128]{2,1,0:T(8,128)S(1)}, f32[3,32,128]{2,1,0:T(8,128)S(1)}, u32[]{:S(2)}, u32[]{:S(2)}) %collective-permute-start.6) | collective-permute-done | bytes 49184 | tf_op jit(solution)/shard_map/ppermute | solution.py:18
  67.8 5.7 %collective-permute-start.8 = (f32[89,3,128]{2,1,0:T(4,128)S(1)}, f32[89,3,128]{2,1,0:T(4,128)S(1)}, u32[]{:S(2)}, u32[]{:S(2)}) collective-permute-start(f32[89,3,128]{2,1,0:T(4,128)S(1)} %get-tuple-element.5), channel_id=1, source_target_pairs={{4,0},{8,4},{12,8},{16,12},{20,16},{24,20},{28,24},{32,28},{36,32}... | collective-permute-start | bytes 410120 | tf_op jit(solution)/shard_map/ppermute | solution.py:12
  73.5 0.6 reshape.98.k_ref
  74.2 2.2 %collective-permute-done.7 = f32[89,3,128]{2,1,0:T(4,128)S(1)} collective-permute-done((f32[89,3,128]{2,1,0:T(4,128)S(1)}, f32[89,3,128]{2,1,0:T(4,128)S(1)}, u32[]{:S(2)}, u32[]{:S(2)}) %collective-permute-start.7) | collective-permute-done | bytes 136736 | tf_op jit(solution)/shard_map/ppermute | solution.py:12
  76.4 1.6 %pad_maximum_fusion.x_ref = f32[89,38,128]{2,1,0:T(8,128)} fusion(f32[89,3,128]{2,1,0:T(4,128)S(1)} %collective-permute-done.8, f32[3,32,128]{2,1,0:T(8,128)S(1)} %broadcast.67, f32[3,32,128]{2,1,0:T(8,128)S(1)} %collective-permute-done.6, f32[80,32,128]{2,1,0:T(8,128)S(1)} %bitcast.28, f32[3,32,128]{2,1,0:T(8,128)S(1)} %collective-permute-done.5, ...), kind=kLoop, calls=%fused_computation.17 | loop fusion | flops 2164480 | bytes 3463168 | tf_op jit(solution)/shard_map/concatenate | solution.py:29
  77.9 0.5 reshape.92.s_ref
  78.5 8.7 %shard_map.132 = f32[83,32,128]{2,1,0:T(8,128)} custom-call(f32[89,38,128]{2,1,0:T(8,128)} %pad_maximum_fusion.x_ref, f32[49,1,128]{2,1,0:T(1,128)} %reshape.98.k_ref, f32[1,128]{1,0:T(1,128)} %reshape.92.s_ref), custom_call_target="tpu_custom_call" | custom-call | tf_op jit(solution)/shard_map/pallas_call | solution.py:60
  87.2 0.8 slice.54
  88.0 5.8 %collective-permute-start.9 = (f32[3,32,128]{2,1,0:T(8,128)S(1)}, f32[3,32,128]{2,1,0:T(8,128)S(1)}, u32[]{:S(2)}, u32[]{:S(2)}) collective-permute-start(f32[3,32,128]{2,1,0:T(8,128)S(1)} %rev.11), channel_id=1, source_target_pairs={{0,124},{4,120},{8,116},{12,112},{16,108},{20,104},{24,100},{28,96... | collective-permute-start | bytes 147464 | tf_op jit(solution)/shard_map/ppermute | solution.py:23
  93.8 4.1 %fusion.9 = bf16[2560,128]{1,0:T(8,128)(2,1)} fusion(bf16[512,128]{1,0:T(8,128)(2,1)S(1)} %copy-done.11, f32[2560,512]{1,0:T(8,128)} %convolution_add_fusion, f32[128]{0:T(128)S(1)} %copy-done.12, f32[128]{0:T(128)S(1)} %copy-done.9, f32[2560]{0:T(1024)S(1)} %mul.121, bf16[2560,128]{1,0:T(8,128)(2,1)S(1)} %bitcast.29), kind=kOutput, calls=%fused_computation.15 | convolution fusion | flops 344064000 | bytes 6695936 | tf_op jit(solution)/shard_map/dot_general | solution.py:88
  97.9 1.3 %fusion.13 = bf16[80,32,128]{2,1,0:T(8,128)(2,1)} fusion(f32[83,32,128]{2,1,0:T(8,128)S(1)} %copy-done.2, f32[3,32,128]{2,1,0:T(8,128)S(1)} %broadcast_select_fusion, f32[80,32]{1,0:T(8,128)S(1)} %copy.15, bf16[80,32,128]{2,1,0:T(8,128)(2,1)S(1)} %copy-done.3), kind=kLoop, calls=%fused_computation.21 | loop fusion | flops 1638400 | bytes 2680832 | tf_op jit(solution)/shard_map/convert_element_type | solution.py:159
  (50 shorter events, 0.7 us)
Async XLA Ops:
  0.6 40.4 %copy-start = (bf16[128,512]{1,0:T(8,128)(2,1)S(1)}, bf16[128,512]{1,0:T(8,128)(2,1)}, u32[]{:S(2)}) copy-start(bf16[128,512]{1,0:T(8,128)(2,1)} %param.18) | copy-start | bytes 393220
  0.6 24.4 %copy-start.9 = (f32[128]{0:T(128)S(1)}, f32[128]{0:T(128)}, u32[]{:S(2)}) copy-start(f32[128]{0:T(128)} %param.22) | copy-start | bytes 1540
  0.7 24.4 %copy-start.3 = (bf16[80,32,128]{2,1,0:T(8,128)(2,1)S(1)}, bf16[80,32,128]{2,1,0:T(8,128)(2,1)}, u32[]{:S(2)}) copy-start(bf16[80,32,128]{2,1,0:T(8,128)(2,1)} %param.23) | copy-start | bytes 1966084
  3.0 22.4 %copy-start.5 = (bf16[7,7,128]{2,1,0:T(8,128)(2,1)S(1)}, bf16[7,7,128]{2,1,0:T(8,128)(2,1)}, u32[]{:S(2)}) copy-start(bf16[7,7,128]{2,1,0:T(8,128)(2,1)} %param.14) | copy-start | bytes 37636
  3.1 15.2 %collective-permute-start.1 = (bf16[3,32,128]{2,1,0:T(8,128)(2,1)S(1)}, bf16[3,32,128]{2,1,0:T(8,128)(2,1)S(1)}, u32[]{:S(2)}, u32[]{:S(2)}) collective-permute-start(bf16[3,32,128]{2,1,0:T(8,128)(2,1)S(1)} %rev.9), channel_id=1, source_target_pairs={{0,124},{4,120},{8,116},{12,112},{16,108},{20,104},{24,100},{28,96... | collective-permute-start | bytes 73736 | tf_op jit(solution)/shard_map/ppermute | solution.py:23
  11.1 7.2 %collective-permute-start.2 = (bf16[3,32,128]{2,1,0:T(8,128)(2,1)S(1)}, bf16[3,32,128]{2,1,0:T(8,128)(2,1)S(1)}, u32[]{:S(2)}, u32[]{:S(2)}) collective-permute-start(bf16[3,32,128]{2,1,0:T(8,128)(2,1)S(1)} %get-tuple-element.10), channel_id=1, source_target_pairs={{1,0},{2,1},{3,2},{5,4},{6,5},{7,6},{9,8},{10,9},{11,10},{13,12},{... | collective-permute-start | bytes 73736 | tf_op jit(solution)/shard_map/ppermute | solution.py:18
  14.0 5.2 %collective-permute-start = (bf16[3,32,128]{2,1,0:T(8,128)(2,1)S(1)}, bf16[3,32,128]{2,1,0:T(8,128)(2,1)S(1)}, u32[]{:S(2)}, u32[]{:S(2)}) collective-permute-start(bf16[3,32,128]{2,1,0:T(8,128)(2,1)S(1)} %get-tuple-element.11), channel_id=1, source_target_pairs={{0,1},{1,2},{2,3},{4,5},{5,6},{6,7},{8,9},{9,10},{10,11},{12,13},{... | collective-permute-start | bytes 73736 | tf_op jit(solution)/shard_map/ppermute | solution.py:18
  19.2 7.6 %collective-permute-start.3 = (bf16[86,3,128]{2,1,0:T(4,128)(2,1)S(1)}, bf16[86,3,128]{2,1,0:T(4,128)(2,1)S(1)}, u32[]{:S(2)}, u32[]{:S(2)}) collective-permute-start(bf16[86,3,128]{2,1,0:T(4,128)(2,1)S(1)} %get-tuple-element.8), channel_id=1, source_target_pairs={{124,0},{0,4},{4,8},{8,12},{12,16},{16,20},{20,24},{24,28},{28,32}... | collective-permute-start | bytes 198152 | tf_op jit(solution)/shard_map/ppermute | solution.py:12
  19.3 7.6 %collective-permute-start.4 = (bf16[86,3,128]{2,1,0:T(4,128)(2,1)S(1)}, bf16[86,3,128]{2,1,0:T(4,128)(2,1)S(1)}, u32[]{:S(2)}, u32[]{:S(2)}) collective-permute-start(bf16[86,3,128]{2,1,0:T(4,128)(2,1)S(1)} %get-tuple-element.9), channel_id=1, source_target_pairs={{4,0},{8,4},{12,8},{16,12},{20,16},{24,20},{28,24},{32,28},{36,32}... | collective-permute-start | bytes 198152 | tf_op jit(solution)/shard_map/ppermute | solution.py:12
  36.7 1.9 %copy-start.1 = (f32[80,32,128]{2,1,0:T(8,128)S(1)}, f32[80,32,128]{2,1,0:T(8,128)}, u32[]{:S(2)}) copy-start(f32[80,32,128]{2,1,0:T(8,128)} %shard_map.131) | copy-start | bytes 3932164
  36.7 2.8 %copy-start.7 = (f32[128]{0:T(128)S(1)}, f32[128]{0:T(128)}, u32[]{:S(2)}) copy-start(f32[128]{0:T(128)} %param.17) | copy-start | bytes 1540
  36.7 2.8 %copy-start.8 = (f32[128]{0:T(128)S(1)}, f32[128]{0:T(128)}, u32[]{:S(2)}) copy-start(f32[128]{0:T(128)} %param.16) | copy-start | bytes 1540
  39.4 1.7 %copy-start.6 = (f32[512]{0:T(512)S(1)}, f32[512]{0:T(512)}, u32[]{:S(2)}) copy-start(f32[512]{0:T(512)} %param.19) | copy-start | bytes 6148
  41.0 3.1 %copy-start.10 = (bf16[512,128]{1,0:T(8,128)(2,1)S(1)}, bf16[512,128]{1,0:T(8,128)(2,1)}, u32[]{:S(2)}) copy-start(bf16[512,128]{1,0:T(8,128)(2,1)} %param.20) | copy-start | bytes 393220
  53.9 8.8 %collective-permute-start.5 = (f32[3,32,128]{2,1,0:T(8,128)S(1)}, f32[3,32,128]{2,1,0:T(8,128)S(1)}, u32[]{:S(2)}, u32[]{:S(2)}) collective-permute-start(f32[3,32,128]{2,1,0:T(8,128)S(1)} %bitcast.31), channel_id=1, source_target_pairs={{0,1},{1,2},{2,3},{4,5},{5,6},{6,7},{8,9},{9,10},{10,11},{12,13},{... | collective-permute-start | bytes 147464 | tf_op jit(solution)/shard_map/ppermute | solution.py:18
  60.7 6.9 %collective-permute-start.6 = (f32[3,32,128]{2,1,0:T(8,128)S(1)}, f32[3,32,128]{2,1,0:T(8,128)S(1)}, u32[]{:S(2)}, u32[]{:S(2)}) collective-permute-start(f32[3,32,128]{2,1,0:T(8,128)S(1)} %bitcast.30), channel_id=1, source_target_pairs={{1,0},{2,1},{3,2},{5,4},{6,5},{7,6},{9,8},{10,9},{11,10},{13,12},{... | collective-permute-start | bytes 147464 | tf_op jit(solution)/shard_map/ppermute | solution.py:18
  67.7 8.7 %collective-permute-start.7 = (f32[89,3,128]{2,1,0:T(4,128)S(1)}, f32[89,3,128]{2,1,0:T(4,128)S(1)}, u32[]{:S(2)}, u32[]{:S(2)}) collective-permute-start(f32[89,3,128]{2,1,0:T(4,128)S(1)} %get-tuple-element.4), channel_id=1, source_target_pairs={{124,0},{0,4},{4,8},{8,12},{12,16},{16,20},{20,24},{24,28},{28,32}... | collective-permute-start | bytes 410120 | tf_op jit(solution)/shard_map/ppermute | solution.py:12
  67.8 8.6 %collective-permute-start.8 = (f32[89,3,128]{2,1,0:T(4,128)S(1)}, f32[89,3,128]{2,1,0:T(4,128)S(1)}, u32[]{:S(2)}, u32[]{:S(2)}) collective-permute-start(f32[89,3,128]{2,1,0:T(4,128)S(1)} %get-tuple-element.5), channel_id=1, source_target_pairs={{4,0},{8,4},{12,8},{16,12},{20,16},{24,20},{28,24},{32,28},{36,32}... | collective-permute-start | bytes 410120 | tf_op jit(solution)/shard_map/ppermute | solution.py:12
  78.5 15.3 %copy-start.4 = (bf16[80,32,128]{2,1,0:T(8,128)(2,1)S(1)}, bf16[80,32,128]{2,1,0:T(8,128)(2,1)}, u32[]{:S(2)}) copy-start(bf16[80,32,128]{2,1,0:T(8,128)(2,1)} %param.12) | copy-start | bytes 1966084
  78.5 15.3 %copy-start.11 = (bf16[512,128]{1,0:T(8,128)(2,1)S(1)}, bf16[512,128]{1,0:T(8,128)(2,1)}, u32[]{:S(2)}) copy-start(bf16[512,128]{1,0:T(8,128)(2,1)} %param.20) | copy-start | bytes 393220
  78.5 15.3 %copy-start.12 = (f32[128]{0:T(128)S(1)}, f32[128]{0:T(128)}, u32[]{:S(2)}) copy-start(f32[128]{0:T(128)} %param.21) | copy-start | bytes 1540
  88.0 9.9 %collective-permute-start.9 = (f32[3,32,128]{2,1,0:T(8,128)S(1)}, f32[3,32,128]{2,1,0:T(8,128)S(1)}, u32[]{:S(2)}, u32[]{:S(2)}) collective-permute-start(f32[3,32,128]{2,1,0:T(8,128)S(1)} %rev.11), channel_id=1, source_target_pairs={{0,124},{4,120},{8,116},{12,112},{16,108},{20,104},{24,100},{28,96... | collective-permute-start | bytes 147464 | tf_op jit(solution)/shard_map/ppermute | solution.py:23
  93.8 4.1 %copy-start.2 = (f32[83,32,128]{2,1,0:T(8,128)S(1)}, f32[83,32,128]{2,1,0:T(8,128)}, u32[]{:S(2)}) copy-start(f32[83,32,128]{2,1,0:T(8,128)} %shard_map.132) | copy-start | bytes 4079620

commit v3 on v1

v3 whole, which is shorter than its diff:
```python
import jax
import jax.numpy as jnp
from jax import lax
from jax.sharding import PartitionSpec as P
from jax.experimental import pallas as pl
from jax.experimental.pallas import tpu as pltpu


MESH = pl.DeviceIdType.MESH


def correlate_into(src, taps, bias, o_ref, out_rows, out_cols, chans, block=4):
    block = min(block, out_rows)
    steps = -(-out_rows // block)

    def step(i, carry):
        r0 = jnp.minimum(i * block, out_rows - block)
        acc = jnp.broadcast_to(bias, (block, out_cols, chans))
        for row_tap in range(7):
            for col_tap in range(7):
                window = src[pl.ds(r0 + row_tap, block), pl.ds(col_tap, out_cols), :]
                acc = acc + taps[row_tap * 7 + col_tap] * window
        o_ref[pl.ds(r0, block)] = acc
        return carry

    lax.fori_loop(0, steps, step, 0)


def halo_correlate(block, fold_src, taps, fold_taps, bias, north_fold, collective):
    rows, cols, chans = block.shape
    nlat, nlon = lax.axis_size("lat"), lax.axis_size("lon")
    fold_back = fold_taps is not None

    def run(x_ref, f_ref, k_ref, kf_ref, b_ref, o_ref, pad, gf, send, recv, local, folds):
        band = lax.axis_index("lat")
        lon = lax.axis_index("lon")
        has_south = band > 0
        has_north = band < nlat - 1
        top = band == nlat - 1
        west = lax.rem(lon + nlon - 1, nlon)
        east = lax.rem(lon + 1, nlon)
        fold_dst = gf if fold_back else pad
        fold_row = 6 if fold_back else rows + 3
        hi = pl.ds(rows - 3, 3)
        lo = pl.ds(0, 3)
        allr = pl.ds(0, rows)
        c_lo, c_hi, c_all = pl.ds(0, 3), pl.ds(cols - 3, 3), pl.ds(0, cols)
        d_w, d_mid, d_e = pl.ds(0, 3), pl.ds(3, cols), pl.ds(cols + 3, 3)
        messages = [
            (x_ref.at[hi, c_all], pad.at[pl.ds(0, 3), d_mid], (lon, band + 1), has_north, has_south),
            (x_ref.at[hi, c_hi], pad.at[pl.ds(0, 3), d_w], (east, band + 1), has_north, has_south),
            (x_ref.at[hi, c_lo], pad.at[pl.ds(0, 3), d_e], (west, band + 1), has_north, has_south),
            (x_ref.at[lo, c_all], pad.at[pl.ds(rows + 3, 3), d_mid], (lon, band - 1), has_south, has_north),
            (x_ref.at[lo, c_hi], pad.at[pl.ds(rows + 3, 3), d_w], (east, band - 1), has_south, has_north),
            (x_ref.at[lo, c_lo], pad.at[pl.ds(rows + 3, 3), d_e], (west, band - 1), has_south, has_north),
            (x_ref.at[allr, c_hi], pad.at[pl.ds(3, rows), d_w], (east, band), None, None),
            (x_ref.at[allr, c_lo], pad.at[pl.ds(3, rows), d_e], (west, band), None, None),
            (f_ref.at[:, c_all], fold_dst.at[pl.ds(fold_row, 3), d_mid], (nlon - 1 - lon, band), top, top),
            (f_ref.at[:, c_hi], fold_dst.at[pl.ds(fold_row, 3), d_w], (lax.rem(2 * nlon - lon, nlon), band), top, top),
            (f_ref.at[:, c_lo], fold_dst.at[pl.ds(fold_row, 3), d_e], (lax.rem(2 * nlon - 2 - lon, nlon), band), top, top),
        ]
        sources = [
            (lon, band - 1), (west, band - 1), (east, band - 1),
            (lon, band + 1), (west, band + 1), (east, band + 1),
            (west, band), (east, band),
        ]
        for i in (9, 10):
            src, dst, target, _, _ = messages[i]
            apart = jnp.logical_and(top, target[0] != lon)
            messages[i] = (src, dst, target, apart, apart)
        sources += [messages[8][2], messages[9][2], messages[10][2]]
        own = [
            (pltpu.make_async_copy(messages[i][0], messages[i][1], folds.at[j]),
             jnp.logical_and(top, messages[i][2][0] == lon))
            for j, i in enumerate((9, 10))
        ]
        for copy, cond in own:
            pl.when(cond)(copy.start)

        interior = pltpu.make_async_copy(x_ref, pad.at[pl.ds(3, rows), pl.ds(3, cols)], local)
        interior.start()

        @pl.when(band == 0)
        def _():
            pad[pl.ds(0, 3)] = jnp.zeros((3, cols + 6, chans), jnp.float32)

        if not north_fold:
            @pl.when(top)
            def _():
                pad[pl.ds(rows + 3, 3)] = jnp.zeros((3, cols + 6, chans), jnp.float32)

        if fold_back:
            gf[pl.ds(0, 6)] = jnp.zeros((6, cols + 6, chans), jnp.float32)

            @pl.when(jnp.logical_not(top))
            def _():
                gf[pl.ds(6, 3)] = jnp.zeros((3, cols + 6, chans), jnp.float32)

        barrier = pltpu.get_barrier_semaphore()

        def when(cond, fn):
            if cond is None:
                fn()
            else:
                pl.when(cond)(fn)

        for (src, dst, target, s_cond, r_cond), source in zip(messages, sources):
            def greet_target(target=target):
                pl.semaphore_signal(barrier, 1, device_id=target, device_id_type=MESH)

            def greet_source(source=source):
                pl.semaphore_signal(barrier, 1, device_id=source, device_id_type=MESH)

            when(s_cond, greet_target)
            when(r_cond, greet_source)
        edge = has_north.astype(jnp.int32) + has_south.astype(jnp.int32)
        folded = top.astype(jnp.int32) + sum(messages[i][3].astype(jnp.int32) for i in (9, 10))
        expected = 2 * (3 * edge + 2 + folded)
        pl.semaphore_wait(barrier, expected)

        copies = []
        for i, (src, dst, target, s_cond, r_cond) in enumerate(messages):
            copy = pltpu.make_async_remote_copy(
                src_ref=src,
                dst_ref=dst,
                send_sem=send.at[i],
                recv_sem=recv.at[i],
                device_id=target,
                device_id_type=MESH,
            )
            copies.append(copy)
            when(s_cond, copy.start)
        for copy, (src, dst, target, s_cond, r_cond) in zip(copies, messages):
            when(s_cond, copy.wait_send)
            when(r_cond, copy.wait_recv)
        interior.wait()
        for copy, cond in own:
            pl.when(cond)(copy.wait)

        correlate_into(pad, k_ref, b_ref[...], o_ref, rows, cols, chans)
        if fold_back:
            extra = jnp.zeros((3, cols, chans), jnp.float32)
            for row_tap in range(7):
                for col_tap in range(7):
                    window = gf[pl.ds(row_tap, 3), pl.ds(col_tap, cols), :]
                    extra = extra + kf_ref[row_tap * 7 + col_tap] * window
            o_ref[pl.ds(rows - 3, 3)] = o_ref[pl.ds(rows - 3, 3)] + extra

    taps = taps.astype(jnp.float32).reshape(49, 1, chans)
    if fold_taps is None:
        fold_taps = taps
    else:
        fold_taps = fold_taps.astype(jnp.float32).reshape(49, 1, chans)
    return pl.pallas_call(
        run,
        out_shape=jax.ShapeDtypeStruct((rows, cols, chans), jnp.float32),
        in_specs=[pl.BlockSpec(memory_space=pltpu.VMEM)] * 5,
        out_specs=pl.BlockSpec(memory_space=pltpu.VMEM),
        scratch_shapes=[
            pltpu.VMEM((rows + 6, cols + 6, chans), jnp.float32),
            pltpu.VMEM((9, cols + 6, chans), jnp.float32),
            pltpu.SemaphoreType.DMA((11,)),
            pltpu.SemaphoreType.DMA((11,)),
            pltpu.SemaphoreType.DMA,
            pltpu.SemaphoreType.DMA((2,)),
        ],
        compiler_params=pltpu.CompilerParams(collective_id=collective, has_side_effects=True),
    )(block, fold_src, taps, fold_taps, bias.reshape(1, chans))


def gelu_value(values):
    return 0.5 * values * (1.0 + lax.erf(values * 0.7071067811865476))


def gelu_slope(values):
    cumulative = 0.5 * (1.0 + lax.erf(values * 0.7071067811865476))
    return cumulative + values * jnp.exp(-0.5 * values * values) * 0.3989422804014327


def pointwise(
    conv_out,
    ocean_state,
    keep_mask,
    cotangent,
    norm_gain,
    norm_bias,
    w_expand,
    b_expand,
    w_reduce,
    b_reduce,
    layer_scale,
):
    row_mean = jnp.mean(conv_out, axis=-1, keepdims=True)
    centered = conv_out - row_mean
    inv_std = lax.rsqrt(jnp.mean(centered * centered, axis=-1, keepdims=True) + 1e-06)
    normal_hat = centered * inv_std
    normed = (normal_hat * norm_gain + norm_bias).astype(jnp.bfloat16)
    hidden = jnp.dot(normed, w_expand, preferred_element_type=jnp.float32) + b_expand
    activated = gelu_value(hidden).astype(jnp.bfloat16)
    projected = jnp.dot(activated, w_reduce, preferred_element_type=jnp.float32) + b_reduce
    result = (keep_mask * (ocean_state.astype(jnp.float32) + layer_scale * projected)).astype(
        jnp.bfloat16
    )
    grad_out = (keep_mask * layer_scale * cotangent.astype(jnp.float32)).astype(jnp.bfloat16)
    grad_act = jnp.dot(grad_out, w_reduce.T, preferred_element_type=jnp.float32)
    grad_hidden = (grad_act * gelu_slope(hidden)).astype(jnp.bfloat16)
    grad_normed = jnp.dot(grad_hidden, w_expand.T, preferred_element_type=jnp.float32)
    grad_scaled = grad_normed * norm_gain
    conv_grad = inv_std * (
        grad_scaled
        - jnp.mean(grad_scaled, axis=-1, keepdims=True)
        - normal_hat * jnp.mean(grad_scaled * normal_hat, axis=-1, keepdims=True)
    )
    return (result, conv_grad)


def body(
    ocean_state,
    land_sea,
    kernel,
    conv_bias,
    norm_gain,
    norm_bias,
    w_expand,
    b_expand,
    w_reduce,
    b_reduce,
    layer_scale,
    cotangent,
):
    band_rows, band_cols, channels = ocean_state.shape
    keep_mask = land_sea.astype(jnp.float32)[:, :, None]
    masked = (ocean_state.astype(jnp.float32) * keep_mask).astype(jnp.bfloat16)

    masked32 = masked.astype(jnp.float32)
    top_rows = masked32[band_rows - 3 :][::-1, ::-1]
    conv_out = halo_correlate(masked32, top_rows, kernel, None, conv_bias, True, 0)
    cell_count = band_rows * band_cols
    result, conv_grad = pointwise(
        conv_out.reshape(cell_count, channels),
        ocean_state.reshape(cell_count, channels),
        keep_mask.reshape(cell_count, 1),
        cotangent.reshape(cell_count, channels),
        norm_gain,
        norm_bias,
        w_expand,
        b_expand,
        w_reduce,
        b_reduce,
        layer_scale,
    )
    conv_grad = conv_grad.reshape(band_rows, band_cols, channels)

    grad_top = conv_grad[band_rows - 3 :][::-1, ::-1]
    zero_bias = jnp.zeros((channels,), jnp.float32)
    masked_grad = halo_correlate(
        conv_grad, grad_top, kernel[::-1, ::-1], kernel, zero_bias, False, 1
    )
    state_grad = (keep_mask * (cotangent.astype(jnp.float32) + masked_grad)).astype(jnp.bfloat16)
    return (result.reshape(band_rows, band_cols, channels), state_grad)


def solution(mesh):
    placed = (
        P("lat", "lon", None),
        P("lat", "lon"),
        P(),
        P(),
        P(),
        P(),
        P(),
        P(),
        P(),
        P(),
        P(),
        P("lat", "lon", None),
    )
    return jax.shard_map(
        body,
        mesh=mesh,
        in_specs=placed,
        out_specs=(P("lat", "lon", None), P("lat", "lon", None)),
        check_vma=False,
    )
```

time: 117 us -> 73.2 us (0.63); the launches traced: 114 us -> 72.9 us
  Pallas kernels: 0 us -> 42.2 us
  starting transfers between devices: 39.5 us -> 0 us
  other arithmetic: 51.8 us -> 12.8 us
  waiting for transfers between devices: 6.87 us -> 0 us
  local copies, waits for them, and re-layouts: 1.3 us -> 3.67 us
    pallas_call x0 -> x2, Pallas kernels: none -> 42.2 us  [halo_correlate(): pl.pallas_call(run, out_shape=jax.ShapeDtypeStruct((rows, cols, chans), j...]
    ppermute x10 -> x0, starting transfers between devices: 39.5 us -> none  [the longest x4 15 us: from_behind(): lax.ppermute(value, axis, [(source, source + steps) for source in range(l...]
    add x1 -> x0, other arithmetic: 27.7 us -> none  [correlate(): summed = summed + kernel[row_tap, col_tap].astype(jnp.float32) * window]
    reduce_sum x1, other arithmetic: 9.48 us -> 1.82 us  [pointwise(): row_mean = jnp.mean(conv_out, axis=-1, keepdims=True)]
    ppermute x10 -> x0, waiting for transfers between devices: 6.87 us -> none  [the longest x4 4.44 us: from_behind(): lax.ppermute(value, axis, [(source, source + steps) for source in range(l...]
    concatenate x2 -> x0, other arithmetic: 3.56 us -> none  [the longest x1 1.98 us: body(): jnp.concatenate([grad_below, conv_grad, grad_above, jnp.zeros_like(grad_a...]
    reshape x0 -> x3, local copies, waits for them, and re-layouts: none -> 1.84 us  [the longest x2 1.27 us: halo_correlate(): taps = taps.astype(jnp.float32).reshape(49, 1, chans)]
    rev x2 -> x3, local copies, waits for them, and re-layouts: 0.04 us -> 1.43 us  [the longest x1 0.7 us: body(): grad_top = conv_grad[band_rows - 3:][::-1, ::-1]]
  transfers between devices with their start and end apart: 10 -> 0, of which waited for: 4 -> 0; matrix products, arithmetic and copies ran while one was open for 7% -> 0% of each run, Pallas kernels for 0% -> 0%
where the time goes in v3:
time: 73.2 us; the launch traced here: 72.9 us
  Pallas kernels  42.2 us (58%)
  matrix products  13.4 us (18%)
  other arithmetic  12.8 us (17%)
  local copies, waits for them, and re-layouts  3.67 us (5%)
  between operations  0.9 us (1%)
    pallas_call x2, Pallas kernels, halo_correlate(): pl.pallas_call(run, out_shape=jax.ShapeDtypeStruct((rows, cols, chans), j...  42.2 us
    dot_general x1, matrix products, pointwise(): jnp.dot(grad_hidden, w_expand.T, preferred_element_type=jnp.float32)  6.18 us
    dot_general x1, matrix products, pointwise(): jnp.dot(activated, w_reduce, preferred_element_type=jnp.float32) + b_reduce  4.08 us
    mul x1, other arithmetic, pointwise(): inv_std * (grad_scaled - jnp.mean(grad_scaled, axis=-1, keepdims=True) -...  3.47 us
    dot_general x1, matrix products, pointwise(): jnp.dot(normed, w_expand, preferred_element_type=jnp.float32) + b_expand  3.12 us
    convert_element_type x1, other arithmetic, body(): (keep_mask * (cotangent.astype(jnp.float32) + masked_grad)).astype(jnp.bf...  2.56 us
    reduce_sum x1, other arithmetic, pointwise(): row_mean = jnp.mean(conv_out, axis=-1, keepdims=True)  1.82 us
    convert_element_type x1, other arithmetic, body(): masked32 = masked.astype(jnp.float32)  1.49 us

profile of v3, /device:TPU:1, one launch (start us, length us, event | category | flops | bytes accessed | tf_op | source)
XLA Modules:
  0.0 72.9 jit_solution(1437721597984095240)
XLA Ops:
  0.6 0.0 copy-start
  0.7 0.8 %convert_element_type.48 = f32[80,32]{0,1:T(8,128)S(1)} convert(s32[80,32]{0,1:T(8,128)} %param.13) | non-fusion elementwise | flops 2560 | bytes 20480 | tf_op jit(solution)/shard_map/convert_element_type | solution.py:232
  1.4 0.1 copy.15
  1.5 1.5 %fusion.13.x_ref = f32[80,32,128]{2,1,0:T(8,128)S(1)} fusion(f32[80,32]{1,0:T(8,128)S(1)} %copy.15, bf16[80,32,128]{2,1,0:T(8,128)(2,1)} %param.12), kind=kLoop, calls=%fused_computation.27 | loop fusion | flops 1310720 | bytes 1976320 | tf_op jit(solution)/shard_map/convert_element_type | solution.py:235
  3.0 0.7 rev.9.f_ref
  3.7 0.6 reshape.95.k_ref.kf_ref
  4.4 22.3 %shard_map.131 = f32[80,32,128]{2,1,0:T(8,128)} custom-call(f32[80,32,128]{2,1,0:T(8,128)} %copy-done.3, f32[3,32,128]{2,1,0:T(8,128)} %rev.9.f_ref, f32[49,1,128]{2,1,0:T(1,128)} %reshape.95.k_ref.kf_ref, f32[49,1,128]{2,1,0:T(1,128)} %reshape.95.k_ref.kf_ref, f32[1,128]{1,0:T(1,128)} %bitcast.29), custom_call_target="tpu_custom_call" | custom-call | tf_op jit(solution)/shard_map/pallas_call | solution.py:154
  26.6 0.0 copy-start.8
  26.7 0.0 copy-start.10
  26.7 1.8 %reduce_sum.36 = f32[80,32]{1,0:T(8,128)S(1)} reduce(f32[80,32,128]{2,1,0:T(8,128)} %shard_map.131, f32[]{:T(128)} %constant.8.clone.1), dimensions={2}, to_apply=%region_0.0 | reduce | flops 325120 | bytes 1320964 | tf_op jit(solution)/shard_map/reduce_sum | solution.py:193
  28.5 0.0 copy-done.1
  28.5 0.8 %multiply_reduce_fusion.1 = f32[80,32]{1,0:T(8,128)S(1)} fusion(f32[80,32,128]{2,1,0:T(8,128)S(1)} %copy-done.1, f32[80,32]{1,0:T(8,128)S(1)} %broadcast_multiply_fusion), kind=kLoop, calls=%fused_computation.25 | loop fusion | flops 980480 | bytes 1331200 | tf_op jit(solution)/shard_map/reduce_sum | solution.py:195
  29.3 0.0 copy-start.7
  29.3 0.1 rsqrt.12
  29.4 0.1 div.15
  29.5 1.5 %add_convert_fusion = bf16[2560,128]{1,0:T(8,128)(2,1)S(1)} fusion(f32[80,32,128]{2,1,0:T(8,128)S(1)} %copy-done.1, f32[128]{0:T(128)S(1)} %copy-done.8, f32[128]{0:T(128)S(1)} %copy-done.10, f32[2560]{0:T(1024)S(1)} %rsqrt.12, f32[2560]{0:T(1024)S(1)} %div.15), kind=kLoop, calls=%fused_computation.24 | loop fusion | flops 1638400 | bytes 1987584 | tf_op jit(solution)/shard_map/convert_element_type | solution.py:197
  31.0 0.0 copy-start.5
  31.0 0.0 copy-start.9
  31.0 0.0 copy-start.11
  31.0 0.0 copy-start.12
  31.0 3.1 %convolution_add_fusion = f32[2560,512]{1,0:T(8,128)} fusion(bf16[2560,128]{1,0:T(8,128)(2,1)S(1)} %add_convert_fusion, bf16[128,512]{1,0:T(8,128)(2,1)S(1)} %copy-done, f32[512]{0:T(512)S(1)} %copy-done.7), kind=kOutput, calls=%fused_computation.9 | convolution fusion | flops 336855040 | bytes 6031360 | tf_op jit(solution)/shard_map/dot_general | solution.py:198
  34.2 0.1 mul.121
  34.3 0.0 copy-start.4
  34.3 4.1 %fusion.9 = bf16[2560,128]{1,0:T(8,128)(2,1)} fusion(bf16[512,128]{1,0:T(8,128)(2,1)S(1)} %copy-done.11, f32[2560,512]{1,0:T(8,128)} %convolution_add_fusion, f32[128]{0:T(128)S(1)} %copy-done.12, f32[128]{0:T(128)S(1)} %copy-done.9, f32[2560]{0:T(1024)S(1)} %mul.121, bf16[2560,128]{1,0:T(8,128)(2,1)S(1)} %bitcast.27), kind=kOutput, calls=%fused_computation.15 | convolution fusion | flops 344064000 | bytes 6695936 | tf_op jit(solution)/shard_map/dot_general | solution.py:200
  38.4 0.4 fusion.11
  38.8 6.2 %fusion.18 = (f32[2560]{0:T(1024)S(1)}, f32[2560]{0:T(1024)S(1)}, f32[2560,128]{1,0:T(8,128)}) fusion(f32[2560]{0:T(1024)S(1)} %rsqrt.12, f32[2560]{0:T(1024)S(1)} %div.15, f32[80,32,128]{2,1,0:T(8,128)S(1)} %copy-done.1, f32[128]{0:T(128)S(1)} %copy-done.10, bf16[128,512]{1,0:T(8,128)(2,1)S(1)} %copy-done, f32[2560,512]{1,0:T(8,128)} %convolution_add_fusion, ...), kind=kOutput, calls=%fused_computation.36 | convolution fusion | flops 686156800 | bytes 8823296 | tf_op jit(solution)/shard_map/dot_general | solution.py:207
  45.0 3.5 %subtract_multiply_fusion = f32[2560,128]{1,0:T(8,128)S(1)} fusion(f32[2560,128]{1,0:T(8,128)} %get-tuple-element.4, f32[80,32,128]{2,1,0:T(8,128)S(1)} %copy-done.1, f32[2560]{0:T(1024)S(1)} %get-tuple-element.5, f32[2560]{0:T(1024)S(1)} %get-tuple-element.6, f32[2560]{0:T(1024)S(1)} %rsqrt.12, f32[2560]{0:T(1024)S(1)} %div.15), kind=kLoop, calls=%fused_computation.22 | loop fusion | flops 1966080 | bytes 3973120 | tf_op jit(solution)/shard_map/mul | solution.py:209
  48.5 0.7 rev.10.f_ref
  49.2 0.6 reshape.98.k_ref
  49.8 0.6 reshape.92.b_ref
  50.4 19.9 %shard_map.132 = f32[80,32,128]{2,1,0:T(8,128)} custom-call(f32[80,32,128]{2,1,0:T(8,128)} %bitcast.26, f32[3,32,128]{2,1,0:T(8,128)} %rev.10.f_ref, f32[49,1,128]{2,1,0:T(1,128)} %reshape.98.k_ref, f32[49,1,128]{2,1,0:T(1,128)} %reshape.95.k_ref.kf_ref, f32[1,128]{1,0:T(1,128)} %reshape.92.b_ref), custom_call_target="tpu_custom_call" | custom-call | tf_op jit(solution)/shard_map/pallas_call | solution.py:154
  70.3 2.6 %multiply_convert_fusion.2 = bf16[80,32,128]{2,1,0:T(8,128)(2,1)} fusion(f32[80,32,128]{2,1,0:T(8,128)} %shard_map.132, f32[80,32]{1,0:T(8,128)S(1)} %copy.15, bf16[80,32,128]{2,1,0:T(8,128)(2,1)S(1)} %copy-done.4), kind=kLoop, calls=%fused_computation.21 | loop fusion | flops 1310720 | bytes 2631680 | tf_op jit(solution)/shard_map/convert_element_type | solution.py:259
  (22 shorter events, 0.1 us)
Async XLA Ops:
  0.6 30.3 %copy-start = (bf16[128,512]{1,0:T(8,128)(2,1)S(1)}, bf16[128,512]{1,0:T(8,128)(2,1)}, u32[]{:S(2)}) copy-start(bf16[128,512]{1,0:T(8,128)(2,1)} %param.18) | copy-start | bytes 393220
  0.6 3.1 %copy-start.6 = (bf16[7,7,128]{2,1,0:T(8,128)(2,1)S(1)}, bf16[7,7,128]{2,1,0:T(8,128)(2,1)}, u32[]{:S(2)}) copy-start(bf16[7,7,128]{2,1,0:T(8,128)(2,1)} %param.14) | copy-start | bytes 37636
  3.0 1.4 %copy-start.3 = (f32[80,32,128]{2,1,0:T(8,128)}, f32[80,32,128]{2,1,0:T(8,128)S(1)}, u32[]{:S(2)}) copy-start(f32[80,32,128]{2,1,0:T(8,128)S(1)} %fusion.13.x_ref) | copy-start | bytes 3932164
  26.6 1.9 %copy-start.1 = (f32[80,32,128]{2,1,0:T(8,128)S(1)}, f32[80,32,128]{2,1,0:T(8,128)}, u32[]{:S(2)}) copy-start(f32[80,32,128]{2,1,0:T(8,128)} %shard_map.131) | copy-start | bytes 3932164
  26.6 2.8 %copy-start.8 = (f32[128]{0:T(128)S(1)}, f32[128]{0:T(128)}, u32[]{:S(2)}) copy-start(f32[128]{0:T(128)} %param.17) | copy-start | bytes 1540
  26.7 2.8 %copy-start.10 = (f32[128]{0:T(128)S(1)}, f32[128]{0:T(128)}, u32[]{:S(2)}) copy-start(f32[128]{0:T(128)} %param.16) | copy-start | bytes 1540
  29.3 1.7 %copy-start.7 = (f32[512]{0:T(512)S(1)}, f32[512]{0:T(512)}, u32[]{:S(2)}) copy-start(f32[512]{0:T(512)} %param.19) | copy-start | bytes 6148
  31.0 3.2 %copy-start.5 = (bf16[80,32,128]{2,1,0:T(8,128)(2,1)S(1)}, bf16[80,32,128]{2,1,0:T(8,128)(2,1)}, u32[]{:S(2)}) copy-start(bf16[80,32,128]{2,1,0:T(8,128)(2,1)} %param.12) | copy-start | bytes 1966084
  31.0 3.2 %copy-start.9 = (f32[128]{0:T(128)S(1)}, f32[128]{0:T(128)}, u32[]{:S(2)}) copy-start(f32[128]{0:T(128)} %param.22) | copy-start | bytes 1540
  31.0 3.2 %copy-start.11 = (bf16[512,128]{1,0:T(8,128)(2,1)S(1)}, bf16[512,128]{1,0:T(8,128)(2,1)}, u32[]{:S(2)}) copy-start(bf16[512,128]{1,0:T(8,128)(2,1)} %param.20) | copy-start | bytes 393220
  31.0 3.2 %copy-start.12 = (f32[128]{0:T(128)S(1)}, f32[128]{0:T(128)}, u32[]{:S(2)}) copy-start(f32[128]{0:T(128)} %param.21) | copy-start | bytes 1540
  34.3 4.1 %copy-start.4 = (bf16[80,32,128]{2,1,0:T(8,128)(2,1)S(1)}, bf16[80,32,128]{2,1,0:T(8,128)(2,1)}, u32[]{:S(2)}) copy-start(bf16[80,32,128]{2,1,0:T(8,128)(2,1)} %param.23) | copy-start | bytes 1966084
  48.4 2.0 %copy-start.2 = (f32[2560,128]{1,0:T(8,128)}, f32[2560,128]{1,0:T(8,128)S(1)}, u32[]{:S(2)}) copy-start(f32[2560,128]{1,0:T(8,128)S(1)} %subtract_multiply_fusion) | copy-start | bytes 3932164

commit v4 on v3

--- a/solution.py
+++ b/solution.py
@@ -189,29 +189,65 @@
     w_reduce,
     b_reduce,
     layer_scale,
+    tile=512,
 ):
-    row_mean = jnp.mean(conv_out, axis=-1, keepdims=True)
-    centered = conv_out - row_mean
-    inv_std = lax.rsqrt(jnp.mean(centered * centered, axis=-1, keepdims=True) + 1e-06)
-    normal_hat = centered * inv_std
-    normed = (normal_hat * norm_gain + norm_bias).astype(jnp.bfloat16)
-    hidden = jnp.dot(normed, w_expand, preferred_element_type=jnp.float32) + b_expand
-    activated = gelu_value(hidden).astype(jnp.bfloat16)
-    projected = jnp.dot(activated, w_reduce, preferred_element_type=jnp.float32) + b_reduce
-    result = (keep_mask * (ocean_state.astype(jnp.float32) + layer_scale * projected)).astype(
-        jnp.bfloat16
-    )
-    grad_out = (keep_mask * layer_scale * cotangent.astype(jnp.float32)).astype(jnp.bfloat16)
-    grad_act = jnp.dot(grad_out, w_reduce.T, preferred_element_type=jnp.float32)
-    grad_hidden = (grad_act * gelu_slope(hidden)).astype(jnp.bfloat16)
-    grad_normed = jnp.dot(grad_hidden, w_expand.T, preferred_element_type=jnp.float32)
-    grad_scaled = grad_normed * norm_gain
-    conv_grad = inv_std * (
-        grad_scaled
-        - jnp.mean(grad_scaled, axis=-1, keepdims=True)
-        - normal_hat * jnp.mean(grad_scaled * normal_hat, axis=-1, keepdims=True)
-    )
-    return (result, conv_grad)
+    cells, chans = conv_out.shape
+    hidden_size = w_expand.shape[1]
+    tile = min(tile, cells)
+    contract_last = (((1,), (1,)), ((), ()))
+
+    def run(c_ref, s_ref, m_ref, t_ref, g_ref, nb_ref, we_ref, be_ref, wr_ref, br_ref, ls_ref, r_ref, o_ref):
+        conv = c_ref[...]
+        keep = m_ref[...]
+        gain = g_ref[...]
+        scale = ls_ref[...]
+        row_mean = jnp.mean(conv, axis=-1, keepdims=True)
+        centered = conv - row_mean
+        inv_std = lax.rsqrt(jnp.mean(centered * centered, axis=-1, keepdims=True) + 1e-06)
+        normal_hat = centered * inv_std
+        normed = (normal_hat * gain + nb_ref[...]).astype(jnp.bfloat16)
+        hidden = jnp.dot(normed, we_ref[...], preferred_element_type=jnp.float32) + be_ref[...]
+        erf_term = lax.erf(hidden * 0.7071067811865476)
+        activated = (0.5 * hidden * (1.0 + erf_term)).astype(jnp.bfloat16)
+        projected = jnp.dot(activated, wr_ref[...], preferred_element_type=jnp.float32) + br_ref[...]
+        r_ref[...] = (keep * (s_ref[...].astype(jnp.float32) + scale * projected)).astype(r_ref.dtype)
+        grad_out = (keep * scale * t_ref[...].astype(jnp.float32)).astype(jnp.bfloat16)
+        grad_act = lax.dot_general(
+            grad_out, wr_ref[...], contract_last, preferred_element_type=jnp.float32
+        )
+        slope = 0.5 * (1.0 + erf_term) + hidden * jnp.exp(-0.5 * hidden * hidden) * 0.3989422804014327
+        grad_hidden = (grad_act * slope).astype(jnp.bfloat16)
+        grad_normed = lax.dot_general(
+            grad_hidden, we_ref[...], contract_last, preferred_element_type=jnp.float32
+        )
+        grad_scaled = grad_normed * gain
+        o_ref[...] = inv_std * (
+            grad_scaled
+            - jnp.mean(grad_scaled, axis=-1, keepdims=True)
+            - normal_hat * jnp.mean(grad_scaled * normal_hat, axis=-1, keepdims=True)
+        )
+
+    rows = lambda width: pl.BlockSpec((tile, width), lambda i: (i, 0))
+    whole = lambda shape: pl.BlockSpec(shape, lambda i: (0, 0))
+    vec = lambda v: v.reshape(1, -1)
+    return pl.pallas_call(
+        run,
+        grid=(cells // tile,),
+        out_shape=(
+            jax.ShapeDtypeStruct((cells, chans), jnp.bfloat16),
+            jax.ShapeDtypeStruct((cells, chans), jnp.float32),
+        ),
+        in_specs=[
+            rows(chans), rows(chans), rows(1), rows(chans),
+            whole((1, chans)), whole((1, chans)),
+            whole((chans, hidden_size)), whole((1, hidden_size)),
+            whole((hidden_size, chans)), whole((1, chans)), whole((1, chans)),
+        ],
+        out_specs=(rows(chans), rows(chans)),
+    )(
+        conv_out, ocean_state, keep_mask, cotangent, vec(norm_gain), vec(norm_bias),
+        w_expand, vec(b_expand), w_reduce, vec(b_reduce), vec(layer_scale),
+    )
 
 
 def body(

time: 73.2 us -> 63.8 us (0.87)
  matrix products: 13.4 us -> 0 us
  Pallas kernels: 42.2 us -> 51.5 us
  other arithmetic: 12.8 us -> 4.78 us
  local copies, waits for them, and re-layouts: 3.67 us -> 6.51 us
    dot_general x3 -> x0, matrix products: 13.4 us -> none  [the longest x1 6.18 us: pointwise(): jnp.dot(grad_hidden, w_expand.T, preferred_element_type=jnp.float32)]
    pallas_call x0 -> x1, Pallas kernels: none -> 9.24 us  [pointwise(): pl.pallas_call(run, grid=(cells // tile,), out_shape=(jax.ShapeDtypeStruc...]
    mul x1 -> x0, other arithmetic: 3.47 us -> none  [pointwise(): inv_std * (grad_scaled - jnp.mean(grad_scaled, axis=-1, keepdims=True) -...]
    reduce_sum x2 -> x0, other arithmetic: 2.59 us -> none  [the longest x1 1.82 us: pointwise(): row_mean = jnp.mean(conv_out, axis=-1, keepdims=True)]
    another operation x0 -> x1, local copies, waits for them, and re-layouts: none -> 2.41 us  [body(): keep_mask.reshape(cell_count, 1)]
    convert_element_type x2 -> x0, other arithmetic: 1.86 us -> none  [the longest x1 1.46 us: pointwise(): normed = (normal_hat * norm_gain + norm_bias).astype(jnp.bfloat16)]
    slice x1, local copies, waits for them, and re-layouts: 0.01 us -> 0.8 us  [body(): grad_top = conv_grad[band_rows - 3:][::-1, ::-1]]
where the time goes in v4:
time: 63.8 us; the launch traced here: 63.4 us
  Pallas kernels  51.5 us (81%)
  local copies, waits for them, and re-layouts  6.51 us (10%)
  other arithmetic  4.78 us (7%)
  between operations  0.69 us (1%)
    pallas_call x2, Pallas kernels, halo_correlate(): pl.pallas_call(run, out_shape=jax.ShapeDtypeStruct((rows, cols, chans), j...  42.2 us
    pallas_call x1, Pallas kernels, pointwise(): pl.pallas_call(run, grid=(cells // tile,), out_shape=(jax.ShapeDtypeStruc...  9.24 us
    convert_element_type x1, other arithmetic, body(): (keep_mask * (cotangent.astype(jnp.float32) + masked_grad)).astype(jnp.bf...  2.56 us
    another operation x1, local copies, waits for them, and re-layouts, body(): keep_mask.reshape(cell_count, 1)  2.41 us
    convert_element_type x1, other arithmetic, body(): masked32 = masked.astype(jnp.float32)  1.49 us

profile of v4, /device:TPU:1, one launch (start us, length us, event | category | flops | bytes accessed | tf_op | source)
XLA Modules:
  0.0 63.4 jit_solution(9714870210492833623)
XLA Ops:
  0.6 0.0 copy-start.2
  0.6 0.7 %convert_element_type.22 = f32[80,32]{0,1:T(8,128)S(1)} convert(s32[80,32]{0,1:T(8,128)} %param.13) | non-fusion elementwise | flops 2560 | bytes 20480 | tf_op jit(solution)/shard_map/convert_element_type | solution.py:268
  1.4 0.1 copy.16
  1.5 1.5 %fusion.x_ref = f32[80,32,128]{2,1,0:T(8,128)S(1)} fusion(bf16[80,32,128]{2,1,0:T(8,128)(2,1)} %param.12, f32[80,32]{1,0:T(8,128)S(1)} %copy.16), kind=kLoop, calls=%fused_computation.2 | loop fusion | flops 1310720 | bytes 1976320 | tf_op jit(solution)/shard_map/convert_element_type | solution.py:271
  2.9 0.0 copy-start
  3.0 0.7 %rev.9.f_ref = f32[3,32,128]{2,1,0:T(8,128)} reverse(f32[3,32,128]{2,1,0:T(8,128)S(1)} %slice.12), dimensions={0,1} | reverse | bytes 98304 | tf_op jit(solution)/shard_map/rev | solution.py:272
  3.7 0.0 copy-done.2
  3.7 0.6 reshape.70.k_ref.kf_ref
  4.3 0.0 copy-done
  4.3 22.3 %shard_map.131 = f32[80,32,128]{2,1,0:T(8,128)} custom-call(f32[80,32,128]{2,1,0:T(8,128)} %copy-done, f32[3,32,128]{2,1,0:T(8,128)} %rev.9.f_ref, f32[49,1,128]{2,1,0:T(1,128)} %reshape.70.k_ref.kf_ref, f32[49,1,128]{2,1,0:T(1,128)} %reshape.70.k_ref.kf_ref, f32[1,128]{1,0:T(1,128)} %bitcast.22), custom_call_target="tpu_custom_call" | custom-call | tf_op jit(solution)/shard_map/pallas_call | solution.py:154
  26.6 2.4 %reshape_broadcast_in_dim.4.m_ref = f32[2560,1]{1,0:T(8,128)} reshape(f32[80,32]{1,0:T(8,128)S(1)} %copy.16) | data formatting | bytes 20480 | tf_op jit(solution)/shard_map/reshape;broadcast_in_dim | solution.py:278
  29.0 9.2 %shard_map.132 = (bf16[2560,128]{1,0:T(8,128)(2,1)}, f32[2560,128]{1,0:T(8,128)}) custom-call(f32[2560,128]{1,0:T(8,128)} %bitcast.12, bf16[2560,128]{1,0:T(8,128)(2,1)} %bitcast.13, f32[2560,1]{1,0:T(8,128)} %reshape_broadcast_in_dim.4.m_ref, bf16[2560,128]{1,0:T(8,128)(2,1)} %bitcast.14, f32[1,128]{1,0:T(1,128)} %bitcast.18, f32[1,128]{1,0:T(1,128)} %bitcast.19, ...), custom_call_target="tpu_custom_call" | custom-call | tf_op jit(solution)/shard_map/pallas_call | solution.py:233
  38.2 0.8 %slice.10 = f32[96,128]{1,0:T(8,128)S(1)} slice(f32[2560,128]{1,0:T(8,128)} %get-tuple-element.5), slice={[2464:2560], [0:128]} | slice | bytes 98304 | tf_op jit(solution)/shard_map/slice | solution.py:290
  39.0 0.6 rev.10.f_ref
  39.7 0.6 %reshape.72.k_ref = f32[49,1,128]{2,1,0:T(1,128)} reshape(bf16[7,7,128]{2,1,0:T(8,128)(2,1)S(1)} %rev.11) | data formatting | bytes 37632 | tf_op jit(solution)/shard_map/reshape | solution.py:149
  40.3 0.6 reshape.68.b_ref
  40.9 0.0 copy-start.1
  40.9 20.0 %shard_map.133 = f32[80,32,128]{2,1,0:T(8,128)} custom-call(f32[80,32,128]{2,1,0:T(8,128)} %bitcast.15, f32[3,32,128]{2,1,0:T(8,128)} %rev.10.f_ref, f32[49,1,128]{2,1,0:T(1,128)} %reshape.72.k_ref, f32[49,1,128]{2,1,0:T(1,128)} %reshape.70.k_ref.kf_ref, f32[1,128]{1,0:T(1,128)} %reshape.68.b_ref), custom_call_target="tpu_custom_call" | custom-call | tf_op jit(solution)/shard_map/pallas_call | solution.py:154
  60.9 0.0 copy-done.1
  60.9 2.6 %multiply_convert_fusion = bf16[80,32,128]{2,1,0:T(8,128)(2,1)} fusion(f32[80,32,128]{2,1,0:T(8,128)} %shard_map.133, bf16[80,32,128]{2,1,0:T(8,128)(2,1)S(1)} %copy-done.1, f32[80,32]{1,0:T(8,128)S(1)} %copy.16), kind=kLoop, calls=%fused_computation | loop fusion | flops 1310720 | bytes 2631680 | tf_op jit(solution)/shard_map/convert_element_type | solution.py:295
  (2 shorter events, 0.0 us)
Async XLA Ops:
  0.6 3.0 %copy-start.2 = (bf16[7,7,128]{2,1,0:T(8,128)(2,1)S(1)}, bf16[7,7,128]{2,1,0:T(8,128)(2,1)}, u32[]{:S(2)}) copy-start(bf16[7,7,128]{2,1,0:T(8,128)(2,1)} %param.14) | copy-start | bytes 37636
  2.9 1.3 %copy-start = (f32[80,32,128]{2,1,0:T(8,128)}, f32[80,32,128]{2,1,0:T(8,128)S(1)}, u32[]{:S(2)}) copy-start(f32[80,32,128]{2,1,0:T(8,128)S(1)} %fusion.x_ref) | copy-start | bytes 3932164
  40.9 20.0 %copy-start.1 = (bf16[80,32,128]{2,1,0:T(8,128)(2,1)S(1)}, bf16[80,32,128]{2,1,0:T(8,128)(2,1)}, u32[]{:S(2)}) copy-start(bf16[80,32,128]{2,1,0:T(8,128)(2,1)} %param.23) | copy-start | bytes 1966084

commit v5 on v4

--- a/solution.py
+++ b/solution.py
@@ -9,18 +9,20 @@
 MESH = pl.DeviceIdType.MESH
 
 
-def correlate_into(src, taps, bias, o_ref, out_rows, out_cols, chans, block=4):
-    block = min(block, out_rows)
-    steps = -(-out_rows // block)
+def correlate_into(src, taps, bias, o_ref, first_row, count, col_tiles, block=8):
+    block = min(block, count)
+    steps = -(-count // block)
+    chans = o_ref.shape[-1]
 
     def step(i, carry):
-        r0 = jnp.minimum(i * block, out_rows - block)
-        acc = jnp.broadcast_to(bias, (block, out_cols, chans))
-        for row_tap in range(7):
+        r0 = first_row + jnp.minimum(i * block, count - block)
+        for c0 in col_tiles:
+            acc = jnp.broadcast_to(bias, (block, 8, chans))
             for col_tap in range(7):
-                window = src[pl.ds(r0 + row_tap, block), pl.ds(col_tap, out_cols), :]
-                acc = acc + taps[row_tap * 7 + col_tap] * window
-        o_ref[pl.ds(r0, block)] = acc
+                window = src[pl.ds(r0, block + 6), pl.ds(c0 + col_tap, 8), :]
+                for row_tap in range(7):
+                    acc = acc + taps[row_tap * 7 + col_tap] * window[row_tap : row_tap + block]
+            o_ref[pl.ds(r0, block), pl.ds(c0, 8), :] = acc
         return carry
 
     lax.fori_loop(0, steps, step, 0)
@@ -113,6 +115,11 @@
 
             when(s_cond, greet_target)
             when(r_cond, greet_source)
+        interior.wait()
+        inner_tiles = tuple(range(8, cols - 8, 8))
+        bias_row = b_ref[...]
+        correlate_into(pad, k_ref, bias_row, o_ref, 3, rows - 6, inner_tiles)
+
         edge = has_north.astype(jnp.int32) + has_south.astype(jnp.int32)
         folded = top.astype(jnp.int32) + sum(messages[i][3].astype(jnp.int32) for i in (9, 10))
         expected = 2 * (3 * edge + 2 + folded)
@@ -133,11 +140,13 @@
         for copy, (src, dst, target, s_cond, r_cond) in zip(copies, messages):
             when(s_cond, copy.wait_send)
             when(r_cond, copy.wait_recv)
-        interior.wait()
         for copy, cond in own:
             pl.when(cond)(copy.wait)
 
-        correlate_into(pad, k_ref, b_ref[...], o_ref, rows, cols, chans)
+        outer_tiles = (0, cols - 8)
+        correlate_into(pad, k_ref, bias_row, o_ref, 0, rows, outer_tiles)
+        correlate_into(pad, k_ref, bias_row, o_ref, 0, 3, inner_tiles)
+        correlate_into(pad, k_ref, bias_row, o_ref, rows - 3, 3, inner_tiles)
         if fold_back:
             extra = jnp.zeros((3, cols, chans), jnp.float32)
             for row_tap in range(7):

time: 63.8 us -> 59.1 us (0.926)
  Pallas kernels: 51.5 us -> 46.7 us
    pallas_call x2, Pallas kernels: 42.2 us -> 37.5 us  [halo_correlate(): pl.pallas_call(run, out_shape=jax.ShapeDtypeStruct((rows, cols, chans), j...]
where the time goes in v5:
time: 59.1 us; the launch traced here: 58.7 us
  Pallas kernels  46.7 us (79%)
  local copies, waits for them, and re-layouts  6.51 us (11%)
  other arithmetic  4.78 us (8%)
  between operations  0.69 us (1%)
    pallas_call x2, Pallas kernels, halo_correlate(): pl.pallas_call(run, out_shape=jax.ShapeDtypeStruct((rows, cols, chans), j...  37.5 us
    pallas_call x1, Pallas kernels, pointwise(): pl.pallas_call(run, grid=(cells // tile,), out_shape=(jax.ShapeDtypeStruc...  9.24 us
    convert_element_type x1, other arithmetic, body(): (keep_mask * (cotangent.astype(jnp.float32) + masked_grad)).astype(jnp.bf...  2.56 us
    another operation x1, local copies, waits for them, and re-layouts, body(): keep_mask.reshape(cell_count, 1)  2.41 us
    convert_element_type x1, other arithmetic, body(): masked32 = masked.astype(jnp.float32)  1.49 us
    reshape x2, local copies, waits for them, and re-layouts, halo_correlate(): taps = taps.astype(jnp.float32).reshape(49, 1, chans)  1.27 us

profile of v5, /device:TPU:1, one launch (start us, length us, event | category | flops | bytes accessed | tf_op | source)
XLA Modules:
  0.0 58.7 jit_solution(13557767954506149658)
XLA Ops:
  0.6 0.0 copy-start.2
  0.6 0.7 %convert_element_type.22 = f32[80,32]{0,1:T(8,128)S(1)} convert(s32[80,32]{0,1:T(8,128)} %param.13) | non-fusion elementwise | flops 2560 | bytes 20480 | tf_op jit(solution)/shard_map/convert_element_type | solution.py:277
  1.4 0.1 copy.16
  1.5 1.5 %fusion.x_ref = f32[80,32,128]{2,1,0:T(8,128)S(1)} fusion(bf16[80,32,128]{2,1,0:T(8,128)(2,1)} %param.12, f32[80,32]{1,0:T(8,128)S(1)} %copy.16), kind=kLoop, calls=%fused_computation.2 | loop fusion | flops 1310720 | bytes 1976320 | tf_op jit(solution)/shard_map/convert_element_type | solution.py:280
  2.9 0.0 copy-start
  3.0 0.7 %rev.9.f_ref = f32[3,32,128]{2,1,0:T(8,128)} reverse(f32[3,32,128]{2,1,0:T(8,128)S(1)} %slice.12), dimensions={0,1} | reverse | bytes 98304 | tf_op jit(solution)/shard_map/rev | solution.py:281
  3.7 0.0 copy-done.2
  3.7 0.6 %reshape.70.k_ref.kf_ref = f32[49,1,128]{2,1,0:T(1,128)} reshape(bf16[7,7,128]{2,1,0:T(8,128)(2,1)S(1)} %copy-done.2) | data formatting | bytes 37632 | tf_op jit(solution)/shard_map/reshape | solution.py:158
  4.3 0.0 copy-done
  4.3 20.5 %shard_map.131 = f32[80,32,128]{2,1,0:T(8,128)} custom-call(f32[80,32,128]{2,1,0:T(8,128)} %copy-done, f32[3,32,128]{2,1,0:T(8,128)} %rev.9.f_ref, f32[49,1,128]{2,1,0:T(1,128)} %reshape.70.k_ref.kf_ref, f32[49,1,128]{2,1,0:T(1,128)} %reshape.70.k_ref.kf_ref, f32[1,128]{1,0:T(1,128)} %bitcast.22), custom_call_target="tpu_custom_call" | custom-call | tf_op jit(solution)/shard_map/pallas_call | solution.py:163
  24.8 2.4 %reshape_broadcast_in_dim.4.m_ref = f32[2560,1]{1,0:T(8,128)} reshape(f32[80,32]{1,0:T(8,128)S(1)} %copy.16) | data formatting | bytes 20480 | tf_op jit(solution)/shard_map/reshape;broadcast_in_dim | solution.py:287
  27.2 9.2 %shard_map.132 = (bf16[2560,128]{1,0:T(8,128)(2,1)}, f32[2560,128]{1,0:T(8,128)}) custom-call(f32[2560,128]{1,0:T(8,128)} %bitcast.12, bf16[2560,128]{1,0:T(8,128)(2,1)} %bitcast.13, f32[2560,1]{1,0:T(8,128)} %reshape_broadcast_in_dim.4.m_ref, bf16[2560,128]{1,0:T(8,128)(2,1)} %bitcast.14, f32[1,128]{1,0:T(1,128)} %bitcast.18, f32[1,128]{1,0:T(1,128)} %bitcast.19, ...), custom_call_target="tpu_custom_call" | custom-call | tf_op jit(solution)/shard_map/pallas_call | solution.py:242
  36.4 0.8 %slice.10 = f32[96,128]{1,0:T(8,128)S(1)} slice(f32[2560,128]{1,0:T(8,128)} %get-tuple-element.5), slice={[2464:2560], [0:128]} | slice | bytes 98304 | tf_op jit(solution)/shard_map/slice | solution.py:299
  37.2 0.6 %rev.10.f_ref = f32[3,32,128]{2,1,0:T(8,128)} reverse(f32[3,32,128]{2,1,0:T(8,128)S(1)} %bitcast.16), dimensions={0,1} | reverse | bytes 98304 | tf_op jit(solution)/shard_map/rev | solution.py:299
  37.9 0.6 %reshape.72.k_ref = f32[49,1,128]{2,1,0:T(1,128)} reshape(bf16[7,7,128]{2,1,0:T(8,128)(2,1)S(1)} %rev.11) | data formatting | bytes 37632 | tf_op jit(solution)/shard_map/reshape | solution.py:158
  38.5 0.6 reshape.68.b_ref
  39.1 0.0 copy-start.1
  39.1 17.0 %shard_map.133 = f32[80,32,128]{2,1,0:T(8,128)} custom-call(f32[80,32,128]{2,1,0:T(8,128)} %bitcast.15, f32[3,32,128]{2,1,0:T(8,128)} %rev.10.f_ref, f32[49,1,128]{2,1,0:T(1,128)} %reshape.72.k_ref, f32[49,1,128]{2,1,0:T(1,128)} %reshape.70.k_ref.kf_ref, f32[1,128]{1,0:T(1,128)} %reshape.68.b_ref), custom_call_target="tpu_custom_call" | custom-call | tf_op jit(solution)/shard_map/pallas_call | solution.py:163
  56.2 0.0 copy-done.1
  56.2 2.6 %multiply_convert_fusion = bf16[80,32,128]{2,1,0:T(8,128)(2,1)} fusion(f32[80,32,128]{2,1,0:T(8,128)} %shard_map.133, bf16[80,32,128]{2,1,0:T(8,128)(2,1)S(1)} %copy-done.1, f32[80,32]{1,0:T(8,128)S(1)} %copy.16), kind=kLoop, calls=%fused_computation | loop fusion | flops 1310720 | bytes 2631680 | tf_op jit(solution)/shard_map/convert_element_type | solution.py:304
  (2 shorter events, 0.0 us)
Async XLA Ops:
  0.6 3.0 %copy-start.2 = (bf16[7,7,128]{2,1,0:T(8,128)(2,1)S(1)}, bf16[7,7,128]{2,1,0:T(8,128)(2,1)}, u32[]{:S(2)}) copy-start(bf16[7,7,128]{2,1,0:T(8,128)(2,1)} %param.14) | copy-start | bytes 37636
  2.9 1.3 %copy-start = (f32[80,32,128]{2,1,0:T(8,128)}, f32[80,32,128]{2,1,0:T(8,128)S(1)}, u32[]{:S(2)}) copy-start(f32[80,32,128]{2,1,0:T(8,128)S(1)} %fusion.x_ref) | copy-start | bytes 3932164
  39.1 17.0 %copy-start.1 = (bf16[80,32,128]{2,1,0:T(8,128)(2,1)S(1)}, bf16[80,32,128]{2,1,0:T(8,128)(2,1)}, u32[]{:S(2)}) copy-start(bf16[80,32,128]{2,1,0:T(8,128)(2,1)} %param.23) | copy-start | bytes 1966084

commit v6 on v5

--- a/solution.py
+++ b/solution.py
@@ -28,12 +28,17 @@
     lax.fori_loop(0, steps, step, 0)
 
 
-def halo_correlate(block, fold_src, taps, fold_taps, bias, north_fold, collective):
+def halo_correlate(block, fold_src, kernel, bias, north_fold, collective, tail=None):
     rows, cols, chans = block.shape
     nlat, nlon = lax.axis_size("lat"), lax.axis_size("lon")
-    fold_back = fold_taps is not None
-
-    def run(x_ref, f_ref, k_ref, kf_ref, b_ref, o_ref, pad, gf, send, recv, local, folds):
+    fold_back = tail is not None
+
+    def run(*refs):
+        if fold_back:
+            x_ref, f_ref, kw_ref, t_ref, m_ref, o_ref, pad, gf, k_ref, acc_ref, send, recv, local, folds = refs
+        else:
+            x_ref, f_ref, kw_ref, b_ref, o_ref, pad, gf, k_ref, acc_ref, send, recv, local, folds = refs
+            acc_ref = o_ref
         band = lax.axis_index("lat")
         lon = lax.axis_index("lon")
         has_south = band > 0
@@ -115,10 +120,18 @@
 
             when(s_cond, greet_target)
             when(r_cond, greet_source)
+        for row_tap in range(7):
+            for col_tap in range(7):
+                a, b = (6 - row_tap, 6 - col_tap) if fold_back else (row_tap, col_tap)
+                k_ref[row_tap * 7 + col_tap] = kw_ref[a, pl.ds(b, 1), :].astype(jnp.float32)
+        if fold_back:
+            bias_row = jnp.zeros((1, chans), jnp.float32)
+        else:
+            bias_row = b_ref[...]
+
         interior.wait()
         inner_tiles = tuple(range(8, cols - 8, 8))
-        bias_row = b_ref[...]
-        correlate_into(pad, k_ref, bias_row, o_ref, 3, rows - 6, inner_tiles)
+        correlate_into(pad, k_ref, bias_row, acc_ref, 3, rows - 6, inner_tiles)
 
         edge = has_north.astype(jnp.int32) + has_south.astype(jnp.int32)
         folded = top.astype(jnp.int32) + sum(messages[i][3].astype(jnp.int32) for i in (9, 10))
@@ -144,37 +157,51 @@
             pl.when(cond)(copy.wait)
 
         outer_tiles = (0, cols - 8)
-        correlate_into(pad, k_ref, bias_row, o_ref, 0, rows, outer_tiles)
-        correlate_into(pad, k_ref, bias_row, o_ref, 0, 3, inner_tiles)
-        correlate_into(pad, k_ref, bias_row, o_ref, rows - 3, 3, inner_tiles)
+        correlate_into(pad, k_ref, bias_row, acc_ref, 0, rows, outer_tiles)
+        correlate_into(pad, k_ref, bias_row, acc_ref, 0, 3, inner_tiles)
+        correlate_into(pad, k_ref, bias_row, acc_ref, rows - 3, 3, inner_tiles)
         if fold_back:
             extra = jnp.zeros((3, cols, chans), jnp.float32)
             for row_tap in range(7):
                 for col_tap in range(7):
                     window = gf[pl.ds(row_tap, 3), pl.ds(col_tap, cols), :]
-                    extra = extra + kf_ref[row_tap * 7 + col_tap] * window
-            o_ref[pl.ds(rows - 3, 3)] = o_ref[pl.ds(rows - 3, 3)] + extra
-
-    taps = taps.astype(jnp.float32).reshape(49, 1, chans)
-    if fold_taps is None:
-        fold_taps = taps
+                    tap = kw_ref[row_tap, pl.ds(col_tap, 1), :].astype(jnp.float32)
+                    extra = extra + tap * window
+            acc_ref[pl.ds(rows - 3, 3)] = acc_ref[pl.ds(rows - 3, 3)] + extra
+            step = 8 if rows % 8 == 0 else rows
+
+            def finish(i, carry):
+                at = pl.ds(i * step, step)
+                total = t_ref[at].astype(jnp.float32) + acc_ref[at]
+                o_ref[at] = (m_ref[at].astype(jnp.float32) * total).astype(o_ref.dtype)
+                return carry
+
+            lax.fori_loop(0, rows // step, finish, 0)
+
+    if fold_back:
+        cotangent, keep = tail
+        operands = (block, fold_src, kernel, cotangent, keep)
     else:
-        fold_taps = fold_taps.astype(jnp.float32).reshape(49, 1, chans)
+        operands = (block, fold_src, kernel, bias.reshape(1, chans))
     return pl.pallas_call(
         run,
-        out_shape=jax.ShapeDtypeStruct((rows, cols, chans), jnp.float32),
-        in_specs=[pl.BlockSpec(memory_space=pltpu.VMEM)] * 5,
+        out_shape=jax.ShapeDtypeStruct(
+            (rows, cols, chans), jnp.bfloat16 if fold_back else jnp.float32
+        ),
+        in_specs=[pl.BlockSpec(memory_space=pltpu.VMEM)] * len(operands),
         out_specs=pl.BlockSpec(memory_space=pltpu.VMEM),
         scratch_shapes=[
             pltpu.VMEM((rows + 6, cols + 6, chans), jnp.float32),
             pltpu.VMEM((9, cols + 6, chans), jnp.float32),
+            pltpu.VMEM((49, 1, chans), jnp.float32),
+            pltpu.VMEM((rows, cols, chans) if fold_back else (8, 128), jnp.float32),
             pltpu.SemaphoreType.DMA((11,)),
             pltpu.SemaphoreType.DMA((11,)),
             pltpu.SemaphoreType.DMA,
             pltpu.SemaphoreType.DMA((2,)),
         ],
         compiler_params=pltpu.CompilerParams(collective_id=collective, has_side_effects=True),
-    )(block, fold_src, taps, fold_taps, bias.reshape(1, chans))
+    )(*operands)
 
 
 def gelu_value(values):
@@ -207,7 +234,7 @@
 
     def run(c_ref, s_ref, m_ref, t_ref, g_ref, nb_ref, we_ref, be_ref, wr_ref, br_ref, ls_ref, r_ref, o_ref):
         conv = c_ref[...]
-        keep = m_ref[...]
+        keep = m_ref[...].astype(jnp.float32)
         gain = g_ref[...]
         scale = ls_ref[...]
         row_mean = jnp.mean(conv, axis=-1, keepdims=True)
@@ -247,7 +274,7 @@
             jax.ShapeDtypeStruct((cells, chans), jnp.float32),
         ),
         in_specs=[
-            rows(chans), rows(chans), rows(1), rows(chans),
+            rows(chans), rows(chans), rows(chans), rows(chans),
             whole((1, chans)), whole((1, chans)),
             whole((chans, hidden_size)), whole((1, hidden_size)),
             whole((hidden_size, chans)), whole((1, chans)), whole((1, chans)),
@@ -275,16 +302,15 @@
 ):
     band_rows, band_cols, channels = ocean_state.shape
     keep_mask = land_sea.astype(jnp.float32)[:, :, None]
-    masked = (ocean_state.astype(jnp.float32) * keep_mask).astype(jnp.bfloat16)
-
-    masked32 = masked.astype(jnp.float32)
+    masked32 = ocean_state.astype(jnp.float32) * keep_mask
+    keep_wide = jnp.broadcast_to(keep_mask, ocean_state.shape).astype(jnp.bfloat16)
     top_rows = masked32[band_rows - 3 :][::-1, ::-1]
-    conv_out = halo_correlate(masked32, top_rows, kernel, None, conv_bias, True, 0)
+    conv_out = halo_correlate(masked32, top_rows, kernel, conv_bias, True, 0)
     cell_count = band_rows * band_cols
     result, conv_grad = pointwise(
         conv_out.reshape(cell_count, channels),
         ocean_state.reshape(cell_count, channels),
-        keep_mask.reshape(cell_count, 1),
+        keep_wide.reshape(cell_count, channels),
         cotangent.reshape(cell_count, channels),
         norm_gain,
         norm_bias,
@@ -297,11 +323,9 @@
     conv_grad = conv_grad.reshape(band_rows, band_cols, channels)
 
     grad_top = conv_grad[band_rows - 3 :][::-1, ::-1]
-    zero_bias = jnp.zeros((channels,), jnp.float32)
-    masked_grad = halo_correlate(
-        conv_grad, grad_top, kernel[::-1, ::-1], kernel, zero_bias, False, 1
-    )
-    state_grad = (keep_mask * (cotangent.astype(jnp.float32) + masked_grad)).astype(jnp.bfloat16)
+    state_grad = halo_correlate(
+        conv_grad, grad_top, kernel, None, False, 1, (cotangent, keep_wide)
+    )
     return (result.reshape(band_rows, band_cols, channels), state_grad)
 
 

time: 59.1 us -> 57 us (0.964)
  other arithmetic: 4.78 us -> 2.21 us
  local copies, waits for them, and re-layouts: 6.51 us -> 7.24 us
    convert_element_type x3 -> x1, other arithmetic: 4.78 us -> 0.72 us  [body(): jnp.broadcast_to(keep_mask, ocean_state.shape).astype(jnp.bfloat16)]
    mul x0 -> x3, local copies, waits for them, and re-layouts: none -> 2.59 us  [body(): masked32 = ocean_state.astype(jnp.float32) * keep_mask]
    another operation x1 -> x0, local copies, waits for them, and re-layouts: 2.41 us -> none  [body(): keep_mask.reshape(cell_count, 1)]
    unnamed x6 -> x3, local copies, waits for them, and re-layouts: 0.01 us -> 2.35 us
    reshape x3 -> x0, local copies, waits for them, and re-layouts: 1.84 us -> none  [the longest x2 1.27 us: halo_correlate(): taps = taps.astype(jnp.float32).reshape(49, 1, chans)]
    mul x0 -> x1, other arithmetic: none -> 1.49 us  [body(): masked32 = ocean_state.astype(jnp.float32) * keep_mask]
where the time goes in v6:
time: 57 us; the launch traced here: 56.6 us
  Pallas kernels  46.4 us (81%)
  local copies, waits for them, and re-layouts  7.24 us (13%)
  other arithmetic  2.21 us (4%)
  between operations  0.67 us (1%)
    pallas_call x2, Pallas kernels, halo_correlate(): pl.pallas_call(run, out_shape=jax.ShapeDtypeStruct((rows, cols, chans), j...  37.7 us
    pallas_call x1, Pallas kernels, pointwise(): pl.pallas_call(run, grid=(cells // tile,), out_shape=(jax.ShapeDtypeStruc...  8.78 us
    mul x3, local copies, waits for them, and re-layouts, body(): masked32 = ocean_state.astype(jnp.float32) * keep_mask  2.59 us
    unnamed x3, local copies, waits for them, and re-layouts  2.35 us
    mul x1, other arithmetic, body(): masked32 = ocean_state.astype(jnp.float32) * keep_mask  1.49 us

profile of v6, /device:TPU:1, one launch (start us, length us, event | category | flops | bytes accessed | tf_op | source)
XLA Modules:
  0.0 56.6 jit_solution(853228029662258366)
XLA Ops:
  0.6 0.7 %convert_convert_fusion = (bf16[80,32]{0,1:T(8,128)(2,1)S(1)}, f32[80,32]{0,1:T(8,128)S(1)}) fusion(s32[80,32]{0,1:T(8,128)} %param.13), kind=kLoop, calls=%fused_computation.1 | loop fusion | flops 5120 | bytes 25600 | tf_op jit(solution)/shard_map/convert_element_type | solution.py:306
  1.4 0.1 copy.16
  1.4 1.5 %convert_multiply_fusion.refs_0_ = f32[80,32,128]{2,1,0:T(8,128)S(1)} fusion(bf16[80,32,128]{2,1,0:T(8,128)(2,1)} %param.12, f32[80,32]{1,0:T(8,128)S(1)} %copy.16), kind=kLoop, calls=%fused_computation | loop fusion | flops 655360 | bytes 1976320 | tf_op jit(solution)/shard_map/mul | solution.py:305
  2.9 0.0 copy-start
  3.0 0.7 %rev.6.refs_1_ = f32[3,32,128]{2,1,0:T(8,128)} reverse(f32[3,32,128]{2,1,0:T(8,128)S(1)} %slice.12), dimensions={0,1} | reverse | bytes 98304 | tf_op jit(solution)/shard_map/rev | solution.py:307
  3.6 0.4 copy-done
  4.0 20.4 %shard_map.131 = f32[80,32,128]{2,1,0:T(8,128)} custom-call(f32[80,32,128]{2,1,0:T(8,128)} %copy-done, f32[3,32,128]{2,1,0:T(8,128)} %rev.6.refs_1_, bf16[7,7,128]{2,1,0:T(8,128)(2,1)} %refs_2_.3, f32[1,128]{1,0:T(1,128)} %bitcast.18), custom_call_target="tpu_custom_call" | custom-call | tf_op jit(solution)/shard_map/pallas_call | solution.py:186
  24.4 0.1 copy.17
  24.5 0.1 mul.16
  24.6 1.3 %mul.17.m_ref = bf16[2560,128]{1,0:T(8,128)(2,1)} broadcast(bf16[2560]{0:T(1024)(128)(2,1)S(1)} %mul.16), dimensions={0} | broadcast | bytes 660480 | tf_op jit(solution)/shard_map/mul | solution.py:305
  25.8 8.8 %shard_map.132 = (bf16[2560,128]{1,0:T(8,128)(2,1)}, f32[2560,128]{1,0:T(8,128)}) custom-call(f32[2560,128]{1,0:T(8,128)} %bitcast.12, bf16[2560,128]{1,0:T(8,128)(2,1)} %bitcast.13, bf16[2560,128]{1,0:T(8,128)(2,1)} %mul.17.m_ref, bf16[2560,128]{1,0:T(8,128)(2,1)} %bitcast.14, f32[1,128]{1,0:T(1,128)} %bitcast.19, f32[1,128]{1,0:T(1,128)} %bitcast.20, ...), custom_call_target="tpu_custom_call" | custom-call | tf_op jit(solution)/shard_map/pallas_call | solution.py:269
  34.6 0.8 %slice.10 = f32[96,128]{1,0:T(8,128)S(1)} slice(f32[2560,128]{1,0:T(8,128)} %get-tuple-element.5), slice={[2464:2560], [0:128]} | slice | bytes 98304 | tf_op jit(solution)/shard_map/slice | solution.py:325
  35.4 0.6 %rev.7.refs_1_ = f32[3,32,128]{2,1,0:T(8,128)} reverse(f32[3,32,128]{2,1,0:T(8,128)S(1)} %bitcast.16), dimensions={0,1} | reverse | bytes 98304 | tf_op jit(solution)/shard_map/rev | solution.py:325
  36.0 1.2 %mul.18.refs_4_ = bf16[80,32,128]{2,1,0:T(8,128)(2,1)} broadcast(bf16[80,32]{1,0:T(8,128)(2,1)S(1)} %copy.17), dimensions={0,1} | broadcast | bytes 660480 | tf_op jit(solution)/shard_map/mul | solution.py:305
  37.3 17.3 %shard_map.133 = bf16[80,32,128]{2,1,0:T(8,128)(2,1)} custom-call(f32[80,32,128]{2,1,0:T(8,128)} %bitcast.15, f32[3,32,128]{2,1,0:T(8,128)} %rev.7.refs_1_, bf16[7,7,128]{2,1,0:T(8,128)(2,1)} %refs_2_.3, bf16[80,32,128]{2,1,0:T(8,128)(2,1)} %refs_3_.1, bf16[80,32,128]{2,1,0:T(8,128)(2,1)} %mul.18.refs_4_), custom_call_target="tpu_custom_call" | custom-call | tf_op jit(solution)/shard_map/pallas_call | solution.py:186
  54.6 2.0 %copy.20 = bf16[80,32,128]{2,1,0:T(8,128)(2,1)} copy(bf16[80,32,128]{2,1,0:T(8,128)(2,1)} %shard_map.133) | data formatting | bytes 1310720
  (1 shorter events, 0.0 us)
Async XLA Ops:
  2.9 1.1 %copy-start = (f32[80,32,128]{2,1,0:T(8,128)}, f32[80,32,128]{2,1,0:T(8,128)S(1)}, u32[]{:S(2)}) copy-start(f32[80,32,128]{2,1,0:T(8,128)S(1)} %convert_multiply_fusion.refs_0_) | copy-start | bytes 3932164

commit v7 on v6

--- a/solution.py
+++ b/solution.py
@@ -225,16 +225,19 @@
     w_reduce,
     b_reduce,
     layer_scale,
-    tile=512,
+    tile=16,
 ):
-    cells, chans = conv_out.shape
+    band_rows, band_cols, chans = conv_out.shape
+    cells = tile * band_cols
     hidden_size = w_expand.shape[1]
-    tile = min(tile, cells)
+    tile = tile if band_rows % tile == 0 else band_rows
+    cells = tile * band_cols
     contract_last = (((1,), (1,)), ((), ()))
 
     def run(c_ref, s_ref, m_ref, t_ref, g_ref, nb_ref, we_ref, be_ref, wr_ref, br_ref, ls_ref, r_ref, o_ref):
-        conv = c_ref[...]
-        keep = m_ref[...].astype(jnp.float32)
+        flat = lambda ref: ref[...].reshape(cells, chans)
+        conv = flat(c_ref)
+        keep = flat(m_ref).astype(jnp.float32)
         gain = g_ref[...]
         scale = ls_ref[...]
         row_mean = jnp.mean(conv, axis=-1, keepdims=True)
@@ -246,8 +249,9 @@
         erf_term = lax.erf(hidden * 0.7071067811865476)
         activated = (0.5 * hidden * (1.0 + erf_term)).astype(jnp.bfloat16)
         projected = jnp.dot(activated, wr_ref[...], preferred_element_type=jnp.float32) + br_ref[...]
-        r_ref[...] = (keep * (s_ref[...].astype(jnp.float32) + scale * projected)).astype(r_ref.dtype)
-        grad_out = (keep * scale * t_ref[...].astype(jnp.float32)).astype(jnp.bfloat16)
+        result = keep * (flat(s_ref).astype(jnp.float32) + scale * projected)
+        r_ref[...] = result.astype(r_ref.dtype).reshape(tile, band_cols, chans)
+        grad_out = (keep * scale * flat(t_ref).astype(jnp.float32)).astype(jnp.bfloat16)
         grad_act = lax.dot_general(
             grad_out, wr_ref[...], contract_last, preferred_element_type=jnp.float32
         )
@@ -257,21 +261,22 @@
             grad_hidden, we_ref[...], contract_last, preferred_element_type=jnp.float32
         )
         grad_scaled = grad_normed * gain
-        o_ref[...] = inv_std * (
+        conv_grad = inv_std * (
             grad_scaled
             - jnp.mean(grad_scaled, axis=-1, keepdims=True)
             - normal_hat * jnp.mean(grad_scaled * normal_hat, axis=-1, keepdims=True)
         )
-
-    rows = lambda width: pl.BlockSpec((tile, width), lambda i: (i, 0))
+        o_ref[...] = conv_grad.reshape(tile, band_cols, chans)
+
+    rows = lambda width: pl.BlockSpec((tile, band_cols, width), lambda i: (i, 0, 0))
     whole = lambda shape: pl.BlockSpec(shape, lambda i: (0, 0))
     vec = lambda v: v.reshape(1, -1)
     return pl.pallas_call(
         run,
-        grid=(cells // tile,),
+        grid=(band_rows // tile,),
         out_shape=(
-            jax.ShapeDtypeStruct((cells, chans), jnp.bfloat16),
-            jax.ShapeDtypeStruct((cells, chans), jnp.float32),
+            jax.ShapeDtypeStruct(conv_out.shape, jnp.bfloat16),
+            jax.ShapeDtypeStruct(conv_out.shape, jnp.float32),
         ),
         in_specs=[
             rows(chans), rows(chans), rows(chans), rows(chans),
@@ -306,12 +311,11 @@
     keep_wide = jnp.broadcast_to(keep_mask, ocean_state.shape).astype(jnp.bfloat16)
     top_rows = masked32[band_rows - 3 :][::-1, ::-1]
     conv_out = halo_correlate(masked32, top_rows, kernel, conv_bias, True, 0)
-    cell_count = band_rows * band_cols
     result, conv_grad = pointwise(
-        conv_out.reshape(cell_count, channels),
-        ocean_state.reshape(cell_count, channels),
-        keep_wide.reshape(cell_count, channels),
-        cotangent.reshape(cell_count, channels),
+        conv_out,
+        ocean_state,
+        keep_wide,
+        cotangent,
         norm_gain,
         norm_bias,
         w_expand,
@@ -320,13 +324,12 @@
         b_reduce,
         layer_scale,
     )
-    conv_grad = conv_grad.reshape(band_rows, band_cols, channels)
 
     grad_top = conv_grad[band_rows - 3 :][::-1, ::-1]
     state_grad = halo_correlate(
         conv_grad, grad_top, kernel, None, False, 1, (cotangent, keep_wide)
     )
-    return (result.reshape(band_rows, band_cols, channels), state_grad)
+    return (result, state_grad)
 
 
 def solution(mesh):

time: 57 us -> 55.7 us (0.977)
  local copies, waits for them, and re-layouts: 7.24 us -> 5.89 us
    mul x3 -> x1, local copies, waits for them, and re-layouts: 2.59 us -> 1.25 us  [body(): masked32 = ocean_state.astype(jnp.float32) * keep_mask]
where the time goes in v7:
time: 55.7 us; the launch traced here: 55.3 us
  Pallas kernels  46.5 us (83%)
  local copies, waits for them, and re-layouts  5.89 us (11%)
  other arithmetic  2.21 us (4%)
  between operations  0.68 us (1%)
    pallas_call x2, Pallas kernels, halo_correlate(): pl.pallas_call(run, out_shape=jax.ShapeDtypeStruct((rows, cols, chans), j...  37.7 us
    pallas_call x1, Pallas kernels, pointwise(): pl.pallas_call(run, grid=(band_rows // tile,), out_shape=(jax.ShapeDtypeS...  8.82 us
    unnamed x3, local copies, waits for them, and re-layouts  2.34 us
    mul x1, other arithmetic, body(): masked32 = ocean_state.astype(jnp.float32) * keep_mask  1.49 us
    mul x1, local copies, waits for them, and re-layouts, body(): masked32 = ocean_state.astype(jnp.float32) * keep_mask  1.25 us

profile of v7, /device:TPU:1, one launch (start us, length us, event | category | flops | bytes accessed | tf_op | source)
XLA Modules:
  0.0 55.3 jit_solution(17973041648150733793)
XLA Ops:
  0.6 0.7 %convert_convert_fusion = (bf16[80,32]{0,1:T(8,128)(2,1)S(1)}, f32[80,32]{0,1:T(8,128)S(1)}) fusion(s32[80,32]{0,1:T(8,128)} %param.13), kind=kLoop, calls=%fused_computation.1 | loop fusion | flops 5120 | bytes 25600 | tf_op jit(solution)/shard_map/convert_element_type | solution.py:311
  1.4 0.1 copy.15
  1.5 0.1 copy.14
  1.5 1.2 %mul.12.m_ref.refs_4_ = bf16[80,32,128]{2,1,0:T(8,128)(2,1)} broadcast(bf16[80,32]{1,0:T(8,128)(2,1)S(1)} %copy.15), dimensions={0,1} | broadcast | bytes 660480 | tf_op jit(solution)/shard_map/mul | solution.py:310
  2.8 1.5 %convert_multiply_fusion.refs_0_ = f32[80,32,128]{2,1,0:T(8,128)S(1)} fusion(bf16[80,32,128]{2,1,0:T(8,128)(2,1)} %s_ref.1, f32[80,32]{1,0:T(8,128)S(1)} %copy.14), kind=kLoop, calls=%fused_computation | loop fusion | flops 655360 | bytes 1976320 | tf_op jit(solution)/shard_map/mul | solution.py:310
  4.3 0.0 copy-start
  4.3 0.7 %rev.6.refs_1_ = f32[3,32,128]{2,1,0:T(8,128)} reverse(f32[3,32,128]{2,1,0:T(8,128)S(1)} %slice.8), dimensions={0,1} | reverse | bytes 98304 | tf_op jit(solution)/shard_map/rev | solution.py:312
  5.0 0.4 copy-done
  5.4 20.4 %shard_map.131.c_ref = f32[80,32,128]{2,1,0:T(8,128)} custom-call(f32[80,32,128]{2,1,0:T(8,128)} %copy-done, f32[3,32,128]{2,1,0:T(8,128)} %rev.6.refs_1_, bf16[7,7,128]{2,1,0:T(8,128)(2,1)} %refs_2_.3, f32[1,128]{1,0:T(1,128)} %bitcast.7), custom_call_target="tpu_custom_call" | custom-call | tf_op jit(solution)/shard_map/pallas_call | solution.py:186
  25.7 8.8 %shard_map.132 = (bf16[80,32,128]{2,1,0:T(8,128)(2,1)}, f32[80,32,128]{2,1,0:T(8,128)}) custom-call(f32[80,32,128]{2,1,0:T(8,128)} %shard_map.131.c_ref, bf16[80,32,128]{2,1,0:T(8,128)(2,1)} %s_ref.1, bf16[80,32,128]{2,1,0:T(8,128)(2,1)} %mul.12.m_ref.refs_4_, bf16[80,32,128]{2,1,0:T(8,128)(2,1)} %refs_3_.1, f32[1,128]{1,0:T(1,128)} %bitcast.8, ...), custom_call_target="tpu_custom_call" | custom-call | tf_op jit(solution)/shard_map/pallas_call | solution.py:274
  34.5 0.8 %slice.7 = f32[3,32,128]{2,1,0:T(8,128)S(1)} slice(f32[80,32,128]{2,1,0:T(8,128)} %get-tuple-element.5.refs_0_), slice={[77:80], [0:32], [0:128]} | slice | bytes 98304 | tf_op jit(solution)/shard_map/slice | solution.py:328
  35.3 0.6 %rev.7.refs_1_ = f32[3,32,128]{2,1,0:T(8,128)} reverse(f32[3,32,128]{2,1,0:T(8,128)S(1)} %slice.7), dimensions={0,1} | reverse | bytes 98304 | tf_op jit(solution)/shard_map/rev | solution.py:328
  36.0 17.3 %shard_map.133 = bf16[80,32,128]{2,1,0:T(8,128)(2,1)} custom-call(f32[80,32,128]{2,1,0:T(8,128)} %get-tuple-element.5.refs_0_, f32[3,32,128]{2,1,0:T(8,128)} %rev.7.refs_1_, bf16[7,7,128]{2,1,0:T(8,128)(2,1)} %refs_2_.3, bf16[80,32,128]{2,1,0:T(8,128)(2,1)} %refs_3_.1, bf16[80,32,128]{2,1,0:T(8,128)(2,1)} %mul.12.m_ref.refs_4_), custom_call_target="tpu_custom_call" | custom-call | tf_op jit(solution)/shard_map/pallas_call | solution.py:186
  53.3 2.0 %copy.17 = bf16[80,32,128]{2,1,0:T(8,128)(2,1)} copy(bf16[80,32,128]{2,1,0:T(8,128)(2,1)} %shard_map.133) | data formatting | bytes 1310720
  (1 shorter events, 0.0 us)
Async XLA Ops:
  4.3 1.1 %copy-start = (f32[80,32,128]{2,1,0:T(8,128)}, f32[80,32,128]{2,1,0:T(8,128)S(1)}, u32[]{:S(2)}) copy-start(f32[80,32,128]{2,1,0:T(8,128)S(1)} %convert_multiply_fusion.refs_0_) | copy-start | bytes 3932164

commit v8 on v7

--- a/solution.py
+++ b/solution.py
@@ -28,16 +28,16 @@
     lax.fori_loop(0, steps, step, 0)
 
 
-def halo_correlate(block, fold_src, kernel, bias, north_fold, collective, tail=None):
+def halo_correlate(block, kernel, bias, north_fold, collective, tail=None):
     rows, cols, chans = block.shape
     nlat, nlon = lax.axis_size("lat"), lax.axis_size("lon")
     fold_back = tail is not None
 
     def run(*refs):
         if fold_back:
-            x_ref, f_ref, kw_ref, t_ref, m_ref, o_ref, pad, gf, k_ref, acc_ref, send, recv, local, folds = refs
+            x_ref, kw_ref, t_ref, m_ref, o_ref, pad, gf, k_ref, acc_ref, stage, send, recv, local, folds = refs
         else:
-            x_ref, f_ref, kw_ref, b_ref, o_ref, pad, gf, k_ref, acc_ref, send, recv, local, folds = refs
+            x_ref, kw_ref, b_ref, o_ref, pad, gf, k_ref, acc_ref, stage, send, recv, local, folds = refs
             acc_ref = o_ref
         band = lax.axis_index("lat")
         lon = lax.axis_index("lon")
@@ -62,9 +62,9 @@
             (x_ref.at[lo, c_lo], pad.at[pl.ds(rows + 3, 3), d_e], (west, band - 1), has_south, has_north),
             (x_ref.at[allr, c_hi], pad.at[pl.ds(3, rows), d_w], (east, band), None, None),
             (x_ref.at[allr, c_lo], pad.at[pl.ds(3, rows), d_e], (west, band), None, None),
-            (f_ref.at[:, c_all], fold_dst.at[pl.ds(fold_row, 3), d_mid], (nlon - 1 - lon, band), top, top),
-            (f_ref.at[:, c_hi], fold_dst.at[pl.ds(fold_row, 3), d_w], (lax.rem(2 * nlon - lon, nlon), band), top, top),
-            (f_ref.at[:, c_lo], fold_dst.at[pl.ds(fold_row, 3), d_e], (lax.rem(2 * nlon - 2 - lon, nlon), band), top, top),
+            (x_ref.at[hi, c_all], stage.at[:, d_mid], (nlon - 1 - lon, band), top, top),
+            (x_ref.at[hi, c_lo], stage.at[:, d_e], (lax.rem(2 * nlon - lon, nlon), band), top, top),
+            (x_ref.at[hi, c_hi], stage.at[:, d_w], (lax.rem(2 * nlon - 2 - lon, nlon), band), top, top),
         ]
         sources = [
             (lon, band - 1), (west, band - 1), (east, band - 1),
@@ -156,6 +156,12 @@
         for copy, cond in own:
             pl.when(cond)(copy.wait)
 
+        @pl.when(top)
+        def _():
+            for t in range(3):
+                for j in range(cols + 6):
+                    fold_dst[fold_row + t, pl.ds(j, 1), :] = stage[2 - t, pl.ds(cols + 5 - j, 1), :]
+
         outer_tiles = (0, cols - 8)
         correlate_into(pad, k_ref, bias_row, acc_ref, 0, rows, outer_tiles)
         correlate_into(pad, k_ref, bias_row, acc_ref, 0, 3, inner_tiles)
@@ -180,9 +186,9 @@
 
     if fold_back:
         cotangent, keep = tail
-        operands = (block, fold_src, kernel, cotangent, keep)
+        operands = (block, kernel, cotangent, keep)
     else:
-        operands = (block, fold_src, kernel, bias.reshape(1, chans))
+        operands = (block, kernel, bias.reshape(1, chans))
     return pl.pallas_call(
         run,
         out_shape=jax.ShapeDtypeStruct(
@@ -195,6 +201,7 @@
             pltpu.VMEM((9, cols + 6, chans), jnp.float32),
             pltpu.VMEM((49, 1, chans), jnp.float32),
             pltpu.VMEM((rows, cols, chans) if fold_back else (8, 128), jnp.float32),
+            pltpu.VMEM((3, cols + 6, chans), jnp.float32),
             pltpu.SemaphoreType.DMA((11,)),
             pltpu.SemaphoreType.DMA((11,)),
             pltpu.SemaphoreType.DMA,
@@ -309,8 +316,7 @@
     keep_mask = land_sea.astype(jnp.float32)[:, :, None]
     masked32 = ocean_state.astype(jnp.float32) * keep_mask
     keep_wide = jnp.broadcast_to(keep_mask, ocean_state.shape).astype(jnp.bfloat16)
-    top_rows = masked32[band_rows - 3 :][::-1, ::-1]
-    conv_out = halo_correlate(masked32, top_rows, kernel, conv_bias, True, 0)
+    conv_out = halo_correlate(masked32, kernel, conv_bias, True, 0)
     result, conv_grad = pointwise(
         conv_out,
         ocean_state,
@@ -325,9 +331,8 @@
         layer_scale,
     )
 
-    grad_top = conv_grad[band_rows - 3 :][::-1, ::-1]
     state_grad = halo_correlate(
-        conv_grad, grad_top, kernel, None, False, 1, (cotangent, keep_wide)
+        conv_grad, kernel, None, False, 1, (cotangent, keep_wide)
     )
     return (result, state_grad)
 

time: 55.7 us -> 54.1 us (0.971)
  local copies, waits for them, and re-layouts: 5.89 us -> 3.4 us
  other arithmetic: 2.21 us -> 3.3 us
    rev x2 -> x0, local copies, waits for them, and re-layouts: 1.31 us -> none  [the longest x1 0.69 us: body(): top_rows = masked32[band_rows - 3:][::-1, ::-1]]
    mul x1, other arithmetic: 1.49 us -> 2.58 us  [body(): masked32 = ocean_state.astype(jnp.float32) * keep_mask]
    slice x2 -> x0, local copies, waits for them, and re-layouts: 0.81 us -> none  [the longest x1 0.8 us: body(): grad_top = conv_grad[band_rows - 3:][::-1, ::-1]]
    unnamed x3 -> x1, local copies, waits for them, and re-layouts: 2.34 us -> 1.97 us
where the time goes in v8:
time: 54.1 us; the launch traced here: 53.8 us
  Pallas kernels  46.4 us (86%)
  local copies, waits for them, and re-layouts  3.4 us (6%)
  other arithmetic  3.3 us (6%)
  between operations  0.65 us (1%)
    pallas_call x2, Pallas kernels, halo_correlate(): pl.pallas_call(run, out_shape=jax.ShapeDtypeStruct((rows, cols, chans), j...  37.6 us
    pallas_call x1, Pallas kernels, pointwise(): pl.pallas_call(run, grid=(band_rows // tile,), out_shape=(jax.ShapeDtypeS...  8.82 us
    mul x1, other arithmetic, body(): masked32 = ocean_state.astype(jnp.float32) * keep_mask  2.58 us
    unnamed x1, local copies, waits for them, and re-layouts  1.97 us
    mul x1, local copies, waits for them, and re-layouts, body(): masked32 = ocean_state.astype(jnp.float32) * keep_mask  1.25 us

profile of v8, /device:TPU:1, one launch (start us, length us, event | category | flops | bytes accessed | tf_op | source)
XLA Modules:
  0.0 53.8 jit_solution(3943313378832063436)
XLA Ops:
  0.6 0.7 %convert_convert_fusion = (bf16[80,32]{0,1:T(8,128)(2,1)S(1)}, f32[80,32]{0,1:T(8,128)S(1)}) fusion(s32[80,32]{0,1:T(8,128)} %param.13), kind=kLoop, calls=%fused_computation.1 | loop fusion | flops 5120 | bytes 25600 | tf_op jit(solution)/shard_map/convert_element_type | solution.py:318
  1.4 0.1 copy.15
  1.5 0.1 copy.14
  1.5 1.2 %mul.12.m_ref.refs_3_ = bf16[80,32,128]{2,1,0:T(8,128)(2,1)} broadcast(bf16[80,32]{1,0:T(8,128)(2,1)S(1)} %copy.15), dimensions={0,1} | broadcast | bytes 660480 | tf_op jit(solution)/shard_map/mul | solution.py:317
  2.8 2.6 %convert_multiply_fusion.refs_0_ = f32[80,32,128]{2,1,0:T(8,128)} fusion(bf16[80,32,128]{2,1,0:T(8,128)(2,1)} %s_ref.1, f32[80,32]{1,0:T(8,128)S(1)} %copy.14), kind=kLoop, calls=%fused_computation | loop fusion | flops 655360 | bytes 1976320 | tf_op jit(solution)/shard_map/mul | solution.py:317
  5.4 20.3 %shard_map.131.c_ref = f32[80,32,128]{2,1,0:T(8,128)} custom-call(f32[80,32,128]{2,1,0:T(8,128)} %convert_multiply_fusion.refs_0_, bf16[7,7,128]{2,1,0:T(8,128)(2,1)} %refs_1_.3, f32[1,128]{1,0:T(1,128)} %bitcast.7), custom_call_target="tpu_custom_call" | custom-call | tf_op jit(solution)/shard_map/pallas_call | solution.py:192
  25.7 8.8 %shard_map.132 = (bf16[80,32,128]{2,1,0:T(8,128)(2,1)}, f32[80,32,128]{2,1,0:T(8,128)}) custom-call(f32[80,32,128]{2,1,0:T(8,128)} %shard_map.131.c_ref, bf16[80,32,128]{2,1,0:T(8,128)(2,1)} %s_ref.1, bf16[80,32,128]{2,1,0:T(8,128)(2,1)} %mul.12.m_ref.refs_3_, bf16[80,32,128]{2,1,0:T(8,128)(2,1)} %refs_2_.1, f32[1,128]{1,0:T(1,128)} %bitcast.8, ...), custom_call_target="tpu_custom_call" | custom-call | tf_op jit(solution)/shard_map/pallas_call | solution.py:281
  34.5 17.3 %shard_map.133 = bf16[80,32,128]{2,1,0:T(8,128)(2,1)} custom-call(f32[80,32,128]{2,1,0:T(8,128)} %get-tuple-element.5.refs_0_, bf16[7,7,128]{2,1,0:T(8,128)(2,1)} %refs_1_.3, bf16[80,32,128]{2,1,0:T(8,128)(2,1)} %refs_2_.1, bf16[80,32,128]{2,1,0:T(8,128)(2,1)} %mul.12.m_ref.refs_3_), custom_call_target="tpu_custom_call" | custom-call | tf_op jit(solution)/shard_map/pallas_call | solution.py:192
  51.8 2.0 %copy.17 = bf16[80,32,128]{2,1,0:T(8,128)(2,1)} copy(bf16[80,32,128]{2,1,0:T(8,128)(2,1)} %shard_map.133) | data formatting | bytes 1310720

commit v9 on v8

--- a/solution.py
+++ b/solution.py
@@ -9,7 +9,7 @@
 MESH = pl.DeviceIdType.MESH
 
 
-def correlate_into(src, taps, bias, o_ref, first_row, count, col_tiles, block=8):
+def correlate_into(src, taps, bias, o_ref, first_row, count, col_tiles, block=16):
     block = min(block, count)
     steps = -(-count // block)
     chans = o_ref.shape[-1]

time: 54.1 us -> 53.6 us (level)
  no operation moved by 1% of the time
where the time goes in v9:
time: 53.6 us; the launch traced here: 53.2 us
  Pallas kernels  45.9 us (86%)
  local copies, waits for them, and re-layouts  3.4 us (6%)
  other arithmetic  3.3 us (6%)
  between operations  0.65 us (1%)
    pallas_call x2, Pallas kernels, halo_correlate(): pl.pallas_call(run, out_shape=jax.ShapeDtypeStruct((rows, cols, chans), j...  37.1 us
    pallas_call x1, Pallas kernels, pointwise(): pl.pallas_call(run, grid=(band_rows // tile,), out_shape=(jax.ShapeDtypeS...  8.82 us
    mul x1, other arithmetic, body(): masked32 = ocean_state.astype(jnp.float32) * keep_mask  2.58 us
    unnamed x1, local copies, waits for them, and re-layouts  1.97 us
    mul x1, local copies, waits for them, and re-layouts, body(): masked32 = ocean_state.astype(jnp.float32) * keep_mask  1.25 us

profile of v9, /device:TPU:1, one launch (start us, length us, event | category | flops | bytes accessed | tf_op | source)
XLA Modules:
  0.0 53.2 jit_solution(12117504996379553527)
XLA Ops:
  0.6 0.7 %convert_convert_fusion = (bf16[80,32]{0,1:T(8,128)(2,1)S(1)}, f32[80,32]{0,1:T(8,128)S(1)}) fusion(s32[80,32]{0,1:T(8,128)} %param.13), kind=kLoop, calls=%fused_computation.1 | loop fusion | flops 5120 | bytes 25600 | tf_op jit(solution)/shard_map/convert_element_type | solution.py:318
  1.4 0.1 copy.15
  1.5 0.1 copy.14
  1.5 1.2 %mul.12.m_ref.refs_3_ = bf16[80,32,128]{2,1,0:T(8,128)(2,1)} broadcast(bf16[80,32]{1,0:T(8,128)(2,1)S(1)} %copy.15), dimensions={0,1} | broadcast | bytes 660480 | tf_op jit(solution)/shard_map/mul | solution.py:317
  2.8 2.6 %convert_multiply_fusion.refs_0_ = f32[80,32,128]{2,1,0:T(8,128)} fusion(bf16[80,32,128]{2,1,0:T(8,128)(2,1)} %s_ref.1, f32[80,32]{1,0:T(8,128)S(1)} %copy.14), kind=kLoop, calls=%fused_computation | loop fusion | flops 655360 | bytes 1976320 | tf_op jit(solution)/shard_map/mul | solution.py:317
  5.4 20.0 %shard_map.131.c_ref = f32[80,32,128]{2,1,0:T(8,128)} custom-call(f32[80,32,128]{2,1,0:T(8,128)} %convert_multiply_fusion.refs_0_, bf16[7,7,128]{2,1,0:T(8,128)(2,1)} %refs_1_.3, f32[1,128]{1,0:T(1,128)} %bitcast.7), custom_call_target="tpu_custom_call" | custom-call | tf_op jit(solution)/shard_map/pallas_call | solution.py:192
  25.4 8.8 %shard_map.132 = (bf16[80,32,128]{2,1,0:T(8,128)(2,1)}, f32[80,32,128]{2,1,0:T(8,128)}) custom-call(f32[80,32,128]{2,1,0:T(8,128)} %shard_map.131.c_ref, bf16[80,32,128]{2,1,0:T(8,128)(2,1)} %s_ref.1, bf16[80,32,128]{2,1,0:T(8,128)(2,1)} %mul.12.m_ref.refs_3_, bf16[80,32,128]{2,1,0:T(8,128)(2,1)} %refs_2_.1, f32[1,128]{1,0:T(1,128)} %bitcast.8, ...), custom_call_target="tpu_custom_call" | custom-call | tf_op jit(solution)/shard_map/pallas_call | solution.py:281
  34.2 17.1 %shard_map.133 = bf16[80,32,128]{2,1,0:T(8,128)(2,1)} custom-call(f32[80,32,128]{2,1,0:T(8,128)} %get-tuple-element.5.refs_0_, bf16[7,7,128]{2,1,0:T(8,128)(2,1)} %refs_1_.3, bf16[80,32,128]{2,1,0:T(8,128)(2,1)} %refs_2_.1, bf16[80,32,128]{2,1,0:T(8,128)(2,1)} %mul.12.m_ref.refs_3_), custom_call_target="tpu_custom_call" | custom-call | tf_op jit(solution)/shard_map/pallas_call | solution.py:192
  51.3 2.0 %copy.17 = bf16[80,32,128]{2,1,0:T(8,128)(2,1)} copy(bf16[80,32,128]{2,1,0:T(8,128)(2,1)} %shard_map.133) | data formatting | bytes 1310720

commit v10 on v9

--- a/solution.py
+++ b/solution.py
@@ -232,7 +232,7 @@
     w_reduce,
     b_reduce,
     layer_scale,
-    tile=16,
+    tile=40,
 ):
     band_rows, band_cols, chans = conv_out.shape
     cells = tile * band_cols

time: 53.6 us -> 52.7 us (0.983)
  Pallas kernels: 45.9 us -> 45 us
    pallas_call x1, Pallas kernels: 8.82 us -> 7.95 us  [pointwise(): pl.pallas_call(run, grid=(band_rows // tile,), out_shape=(jax.ShapeDtypeS...]
where the time goes in v10:
time: 52.7 us; the launch traced here: 52.4 us
  Pallas kernels  45 us (85%)
  local copies, waits for them, and re-layouts  3.4 us (6%)
  other arithmetic  3.3 us (6%)
  between operations  0.65 us (1%)
    pallas_call x2, Pallas kernels, halo_correlate(): pl.pallas_call(run, out_shape=jax.ShapeDtypeStruct((rows, cols, chans), j...  37.1 us
    pallas_call x1, Pallas kernels, pointwise(): pl.pallas_call(run, grid=(band_rows // tile,), out_shape=(jax.ShapeDtypeS...  7.95 us
    mul x1, other arithmetic, body(): masked32 = ocean_state.astype(jnp.float32) * keep_mask  2.58 us
    unnamed x1, local copies, waits for them, and re-layouts  1.97 us
    mul x1, local copies, waits for them, and re-layouts, body(): masked32 = ocean_state.astype(jnp.float32) * keep_mask  1.25 us

profile of v10, /device:TPU:1, one launch (start us, length us, event | category | flops | bytes accessed | tf_op | source)
XLA Modules:
  0.0 52.4 jit_solution(14002215799833369742)
XLA Ops:
  0.6 0.7 %convert_convert_fusion = (bf16[80,32]{0,1:T(8,128)(2,1)S(1)}, f32[80,32]{0,1:T(8,128)S(1)}) fusion(s32[80,32]{0,1:T(8,128)} %param.13), kind=kLoop, calls=%fused_computation.1 | loop fusion | flops 5120 | bytes 25600 | tf_op jit(solution)/shard_map/convert_element_type | solution.py:318
  1.4 0.1 copy.15
  1.5 0.1 copy.14
  1.5 1.2 %mul.12.m_ref.refs_3_ = bf16[80,32,128]{2,1,0:T(8,128)(2,1)} broadcast(bf16[80,32]{1,0:T(8,128)(2,1)S(1)} %copy.15), dimensions={0,1} | broadcast | bytes 660480 | tf_op jit(solution)/shard_map/mul | solution.py:317
  2.8 2.6 %convert_multiply_fusion.refs_0_ = f32[80,32,128]{2,1,0:T(8,128)} fusion(bf16[80,32,128]{2,1,0:T(8,128)(2,1)} %s_ref.1, f32[80,32]{1,0:T(8,128)S(1)} %copy.14), kind=kLoop, calls=%fused_computation | loop fusion | flops 655360 | bytes 1976320 | tf_op jit(solution)/shard_map/mul | solution.py:317
  5.4 20.0 %shard_map.131.c_ref = f32[80,32,128]{2,1,0:T(8,128)} custom-call(f32[80,32,128]{2,1,0:T(8,128)} %convert_multiply_fusion.refs_0_, bf16[7,7,128]{2,1,0:T(8,128)(2,1)} %refs_1_.3, f32[1,128]{1,0:T(1,128)} %bitcast.7), custom_call_target="tpu_custom_call" | custom-call | tf_op jit(solution)/shard_map/pallas_call | solution.py:192
  25.4 7.9 %shard_map.132 = (bf16[80,32,128]{2,1,0:T(8,128)(2,1)}, f32[80,32,128]{2,1,0:T(8,128)}) custom-call(f32[80,32,128]{2,1,0:T(8,128)} %shard_map.131.c_ref, bf16[80,32,128]{2,1,0:T(8,128)(2,1)} %s_ref.1, bf16[80,32,128]{2,1,0:T(8,128)(2,1)} %mul.12.m_ref.refs_3_, bf16[80,32,128]{2,1,0:T(8,128)(2,1)} %refs_2_.1, f32[1,128]{1,0:T(1,128)} %bitcast.8, ...), custom_call_target="tpu_custom_call" | custom-call | tf_op jit(solution)/shard_map/pallas_call | solution.py:281
  33.3 17.1 %shard_map.133 = bf16[80,32,128]{2,1,0:T(8,128)(2,1)} custom-call(f32[80,32,128]{2,1,0:T(8,128)} %get-tuple-element.5.refs_0_, bf16[7,7,128]{2,1,0:T(8,128)(2,1)} %refs_1_.3, bf16[80,32,128]{2,1,0:T(8,128)(2,1)} %refs_2_.1, bf16[80,32,128]{2,1,0:T(8,128)(2,1)} %mul.12.m_ref.refs_3_), custom_call_target="tpu_custom_call" | custom-call | tf_op jit(solution)/shard_map/pallas_call | solution.py:192
  50.4 2.0 %copy.17 = bf16[80,32,128]{2,1,0:T(8,128)(2,1)} copy(bf16[80,32,128]{2,1,0:T(8,128)(2,1)} %shard_map.133) | data formatting | bytes 1310720

commit v11 on v10

--- a/solution.py
+++ b/solution.py
@@ -232,7 +232,7 @@
     w_reduce,
     b_reduce,
     layer_scale,
-    tile=40,
+    tile=80,
 ):
     band_rows, band_cols, chans = conv_out.shape
     cells = tile * band_cols

time: 52.7 us -> 52.9 us (level)
  no operation moved by 1% of the time
where the time goes in v11:
time: 52.9 us; the launch traced here: 52.5 us
  Pallas kernels  45.2 us (85%)
  local copies, waits for them, and re-layouts  3.4 us (6%)
  other arithmetic  3.3 us (6%)
  between operations  0.65 us (1%)
    pallas_call x2, Pallas kernels, halo_correlate(): pl.pallas_call(run, out_shape=jax.ShapeDtypeStruct((rows, cols, chans), j...  37.1 us
    pallas_call x1, Pallas kernels, pointwise(): pl.pallas_call(run, grid=(band_rows // tile,), out_shape=(jax.ShapeDtypeS...  8.13 us
    mul x1, other arithmetic, body(): masked32 = ocean_state.astype(jnp.float32) * keep_mask  2.58 us
    unnamed x1, local copies, waits for them, and re-layouts  1.97 us
    mul x1, local copies, waits for them, and re-layouts, body(): masked32 = ocean_state.astype(jnp.float32) * keep_mask  1.25 us

profile of v11, /device:TPU:1, one launch (start us, length us, event | category | flops | bytes accessed | tf_op | source)
XLA Modules:
  0.0 52.5 jit_solution(5346130617403969666)
XLA Ops:
  0.6 0.7 %convert_convert_fusion = (bf16[80,32]{0,1:T(8,128)(2,1)S(1)}, f32[80,32]{0,1:T(8,128)S(1)}) fusion(s32[80,32]{0,1:T(8,128)} %param.13), kind=kLoop, calls=%fused_computation.1 | loop fusion | flops 5120 | bytes 25600 | tf_op jit(solution)/shard_map/convert_element_type | solution.py:318
  1.4 0.1 copy.15
  1.5 0.1 copy.14
  1.5 1.2 %mul.12.m_ref.refs_3_ = bf16[80,32,128]{2,1,0:T(8,128)(2,1)} broadcast(bf16[80,32]{1,0:T(8,128)(2,1)S(1)} %copy.15), dimensions={0,1} | broadcast | bytes 660480 | tf_op jit(solution)/shard_map/mul | solution.py:317
  2.8 2.6 %convert_multiply_fusion.refs_0_ = f32[80,32,128]{2,1,0:T(8,128)} fusion(bf16[80,32,128]{2,1,0:T(8,128)(2,1)} %s_ref.1, f32[80,32]{1,0:T(8,128)S(1)} %copy.14), kind=kLoop, calls=%fused_computation | loop fusion | flops 655360 | bytes 1976320 | tf_op jit(solution)/shard_map/mul | solution.py:317
  5.4 20.0 %shard_map.131.c_ref = f32[80,32,128]{2,1,0:T(8,128)} custom-call(f32[80,32,128]{2,1,0:T(8,128)} %convert_multiply_fusion.refs_0_, bf16[7,7,128]{2,1,0:T(8,128)(2,1)} %refs_1_.3, f32[1,128]{1,0:T(1,128)} %bitcast.7), custom_call_target="tpu_custom_call" | custom-call | tf_op jit(solution)/shard_map/pallas_call | solution.py:192
  25.4 8.1 %shard_map.132 = (bf16[80,32,128]{2,1,0:T(8,128)(2,1)}, f32[80,32,128]{2,1,0:T(8,128)}) custom-call(f32[80,32,128]{2,1,0:T(8,128)} %shard_map.131.c_ref, bf16[80,32,128]{2,1,0:T(8,128)(2,1)} %s_ref.1, bf16[80,32,128]{2,1,0:T(8,128)(2,1)} %mul.12.m_ref.refs_3_, bf16[80,32,128]{2,1,0:T(8,128)(2,1)} %refs_2_.1, f32[1,128]{1,0:T(1,128)} %bitcast.8, ...), custom_call_target="tpu_custom_call" | custom-call | tf_op jit(solution)/shard_map/pallas_call | solution.py:281
  33.5 17.1 %shard_map.133 = bf16[80,32,128]{2,1,0:T(8,128)(2,1)} custom-call(f32[80,32,128]{2,1,0:T(8,128)} %get-tuple-element.5.refs_0_, bf16[7,7,128]{2,1,0:T(8,128)(2,1)} %refs_1_.3, bf16[80,32,128]{2,1,0:T(8,128)(2,1)} %refs_2_.1, bf16[80,32,128]{2,1,0:T(8,128)(2,1)} %mul.12.m_ref.refs_3_), custom_call_target="tpu_custom_call" | custom-call | tf_op jit(solution)/shard_map/pallas_call | solution.py:192
  50.6 2.0 %copy.17 = bf16[80,32,128]{2,1,0:T(8,128)(2,1)} copy(bf16[80,32,128]{2,1,0:T(8,128)(2,1)} %shard_map.133) | data formatting | bytes 1310720

commit v12 on v10

--- a/solution.py
+++ b/solution.py
@@ -9,23 +9,29 @@
 MESH = pl.DeviceIdType.MESH
 
 
-def correlate_into(src, taps, bias, o_ref, first_row, count, col_tiles, block=16):
+def correlate_into(src, taps, bias, o_ref, first_row, count, col_tiles, block=16,
+                   col_taps=tuple(range(7)), accumulate=False):
+    chans = o_ref.shape[-1]
     block = min(block, count)
-    steps = -(-count // block)
-    chans = o_ref.shape[-1]
+    steps, left = divmod(count, block)
+
+    def one(r0, size):
+        for c0 in col_tiles:
+            at = (pl.ds(r0, size), pl.ds(c0, 8), slice(None))
+            acc = o_ref[at] if accumulate else jnp.broadcast_to(bias, (size, 8, chans))
+            for col_tap in col_taps:
+                window = src[pl.ds(r0, size + 6), pl.ds(c0 + col_tap, 8), :]
+                for row_tap in range(7):
+                    acc = acc + taps[row_tap * 7 + col_tap] * window[row_tap : row_tap + size]
+            o_ref[at] = acc
 
     def step(i, carry):
-        r0 = first_row + jnp.minimum(i * block, count - block)
-        for c0 in col_tiles:
-            acc = jnp.broadcast_to(bias, (block, 8, chans))
-            for col_tap in range(7):
-                window = src[pl.ds(r0, block + 6), pl.ds(c0 + col_tap, 8), :]
-                for row_tap in range(7):
-                    acc = acc + taps[row_tap * 7 + col_tap] * window[row_tap : row_tap + block]
-            o_ref[pl.ds(r0, block), pl.ds(c0, 8), :] = acc
+        one(first_row + i * block, block)
         return carry
 
     lax.fori_loop(0, steps, step, 0)
+    if left:
+        one(first_row + steps * block, left)
 
 
 def halo_correlate(block, kernel, bias, north_fold, collective, tail=None):
@@ -132,6 +138,8 @@
         interior.wait()
         inner_tiles = tuple(range(8, cols - 8, 8))
         correlate_into(pad, k_ref, bias_row, acc_ref, 3, rows - 6, inner_tiles)
+        correlate_into(pad, k_ref, bias_row, acc_ref, 3, rows - 6, (0,), col_taps=(3, 4, 5, 6))
+        correlate_into(pad, k_ref, bias_row, acc_ref, 3, rows - 6, (cols - 8,), col_taps=(0, 1, 2, 3))
 
         edge = has_north.astype(jnp.int32) + has_south.astype(jnp.int32)
         folded = top.astype(jnp.int32) + sum(messages[i][3].astype(jnp.int32) for i in (9, 10))
@@ -162,10 +170,13 @@
                 for j in range(cols + 6):
                     fold_dst[fold_row + t, pl.ds(j, 1), :] = stage[2 - t, pl.ds(cols + 5 - j, 1), :]
 
-        outer_tiles = (0, cols - 8)
-        correlate_into(pad, k_ref, bias_row, acc_ref, 0, rows, outer_tiles)
-        correlate_into(pad, k_ref, bias_row, acc_ref, 0, 3, inner_tiles)
-        correlate_into(pad, k_ref, bias_row, acc_ref, rows - 3, 3, inner_tiles)
+        all_tiles = tuple(range(0, cols, 8))
+        correlate_into(pad, k_ref, bias_row, acc_ref, 3, rows - 6, (0,), col_taps=(0, 1, 2),
+                       accumulate=True)
+        correlate_into(pad, k_ref, bias_row, acc_ref, 3, rows - 6, (cols - 8,), col_taps=(4, 5, 6),
+                       accumulate=True)
+        correlate_into(pad, k_ref, bias_row, acc_ref, 0, 3, all_tiles)
+        correlate_into(pad, k_ref, bias_row, acc_ref, rows - 3, 3, all_tiles)
         if fold_back:
             extra = jnp.zeros((3, cols, chans), jnp.float32)
             for row_tap in range(7):

time: 52.7 us -> 51.5 us (0.977)
  Pallas kernels: 45 us -> 43.8 us
    pallas_call x2, Pallas kernels: 37.1 us -> 35.8 us  [halo_correlate(): pl.pallas_call(run, out_shape=jax.ShapeDtypeStruct((rows, cols, chans), j...]
where the time goes in v12:
time: 51.5 us; the launch traced here: 51.1 us
  Pallas kernels  43.8 us (85%)
  local copies, waits for them, and re-layouts  3.4 us (7%)
  other arithmetic  3.3 us (6%)
  between operations  0.65 us (1%)
    pallas_call x2, Pallas kernels, halo_correlate(): pl.pallas_call(run, out_shape=jax.ShapeDtypeStruct((rows, cols, chans), j...  35.8 us
    pallas_call x1, Pallas kernels, pointwise(): pl.pallas_call(run, grid=(band_rows // tile,), out_shape=(jax.ShapeDtypeS...  7.95 us
    mul x1, other arithmetic, body(): masked32 = ocean_state.astype(jnp.float32) * keep_mask  2.58 us
    unnamed x1, local copies, waits for them, and re-layouts  1.97 us
    mul x1, local copies, waits for them, and re-layouts, body(): masked32 = ocean_state.astype(jnp.float32) * keep_mask  1.25 us

profile of v12, /device:TPU:1, one launch (start us, length us, event | category | flops | bytes accessed | tf_op | source)
XLA Modules:
  0.0 51.1 jit_solution(16711724300286401469)
XLA Ops:
  0.6 0.7 %convert_convert_fusion = (bf16[80,32]{0,1:T(8,128)(2,1)S(1)}, f32[80,32]{0,1:T(8,128)S(1)}) fusion(s32[80,32]{0,1:T(8,128)} %param.13), kind=kLoop, calls=%fused_computation.1 | loop fusion | flops 5120 | bytes 25600 | tf_op jit(solution)/shard_map/convert_element_type | solution.py:329
  1.4 0.1 copy.15
  1.5 0.1 copy.14
  1.5 1.2 %mul.12.m_ref.refs_3_ = bf16[80,32,128]{2,1,0:T(8,128)(2,1)} broadcast(bf16[80,32]{1,0:T(8,128)(2,1)S(1)} %copy.15), dimensions={0,1} | broadcast | bytes 660480 | tf_op jit(solution)/shard_map/mul | solution.py:328
  2.8 2.6 %convert_multiply_fusion.refs_0_ = f32[80,32,128]{2,1,0:T(8,128)} fusion(bf16[80,32,128]{2,1,0:T(8,128)(2,1)} %s_ref.1, f32[80,32]{1,0:T(8,128)S(1)} %copy.14), kind=kLoop, calls=%fused_computation | loop fusion | flops 655360 | bytes 1976320 | tf_op jit(solution)/shard_map/mul | solution.py:328
  5.4 19.8 %shard_map.131.c_ref = f32[80,32,128]{2,1,0:T(8,128)} custom-call(f32[80,32,128]{2,1,0:T(8,128)} %convert_multiply_fusion.refs_0_, bf16[7,7,128]{2,1,0:T(8,128)(2,1)} %refs_1_.3, f32[1,128]{1,0:T(1,128)} %bitcast.7), custom_call_target="tpu_custom_call" | custom-call | tf_op jit(solution)/shard_map/pallas_call | solution.py:203
  25.2 7.9 %shard_map.132 = (bf16[80,32,128]{2,1,0:T(8,128)(2,1)}, f32[80,32,128]{2,1,0:T(8,128)}) custom-call(f32[80,32,128]{2,1,0:T(8,128)} %shard_map.131.c_ref, bf16[80,32,128]{2,1,0:T(8,128)(2,1)} %s_ref.1, bf16[80,32,128]{2,1,0:T(8,128)(2,1)} %mul.12.m_ref.refs_3_, bf16[80,32,128]{2,1,0:T(8,128)(2,1)} %refs_2_.1, f32[1,128]{1,0:T(1,128)} %bitcast.8, ...), custom_call_target="tpu_custom_call" | custom-call | tf_op jit(solution)/shard_map/pallas_call | solution.py:292
  33.2 16.0 %shard_map.133 = bf16[80,32,128]{2,1,0:T(8,128)(2,1)} custom-call(f32[80,32,128]{2,1,0:T(8,128)} %get-tuple-element.5.refs_0_, bf16[7,7,128]{2,1,0:T(8,128)(2,1)} %refs_1_.3, bf16[80,32,128]{2,1,0:T(8,128)(2,1)} %refs_2_.1, bf16[80,32,128]{2,1,0:T(8,128)(2,1)} %mul.12.m_ref.refs_3_), custom_call_target="tpu_custom_call" | custom-call | tf_op jit(solution)/shard_map/pallas_call | solution.py:203
  49.2 2.0 %copy.17 = bf16[80,32,128]{2,1,0:T(8,128)(2,1)} copy(bf16[80,32,128]{2,1,0:T(8,128)(2,1)} %shard_map.133) | data formatting | bytes 1310720

commit v13 on v12

--- a/solution.py
+++ b/solution.py
@@ -34,17 +34,23 @@
         one(first_row + steps * block, left)
 
 
-def halo_correlate(block, kernel, bias, north_fold, collective, tail=None):
+def halo_correlate(block, kernel, bias, north_fold, collective, tail=None, mask=None):
     rows, cols, chans = block.shape
     nlat, nlon = lax.axis_size("lat"), lax.axis_size("lon")
     fold_back = tail is not None
 
     def run(*refs):
         if fold_back:
-            x_ref, kw_ref, t_ref, m_ref, o_ref, pad, gf, k_ref, acc_ref, stage, send, recv, local, folds = refs
+            x_ref, kw_ref, t_ref, m_ref, o_ref, pad, gf, k_ref, acc_ref, stage, _, send, recv, local, folds = refs
         else:
-            x_ref, kw_ref, b_ref, o_ref, pad, gf, k_ref, acc_ref, stage, send, recv, local, folds = refs
+            s_ref, w_ref, kw_ref, b_ref, o_ref, pad, gf, k_ref, acc_ref, stage, x_ref, send, recv, local, folds = refs
             acc_ref = o_ref
+            def mask_rows(i, carry):
+                at = pl.ds(i * 8, 8)
+                x_ref[at] = s_ref[at].astype(jnp.float32) * w_ref[at].astype(jnp.float32)
+                return carry
+
+            lax.fori_loop(0, rows // 8, mask_rows, 0)
         band = lax.axis_index("lat")
         lon = lax.axis_index("lon")
         has_south = band > 0
@@ -199,7 +205,7 @@
         cotangent, keep = tail
         operands = (block, kernel, cotangent, keep)
     else:
-        operands = (block, kernel, bias.reshape(1, chans))
+        operands = (block, mask, kernel, bias.reshape(1, chans))
     return pl.pallas_call(
         run,
         out_shape=jax.ShapeDtypeStruct(
@@ -213,6 +219,7 @@
             pltpu.VMEM((49, 1, chans), jnp.float32),
             pltpu.VMEM((rows, cols, chans) if fold_back else (8, 128), jnp.float32),
             pltpu.VMEM((3, cols + 6, chans), jnp.float32),
+            pltpu.VMEM((8, 128) if fold_back else (rows, cols, chans), jnp.float32),
             pltpu.SemaphoreType.DMA((11,)),
             pltpu.SemaphoreType.DMA((11,)),
             pltpu.SemaphoreType.DMA,
@@ -325,9 +332,8 @@
 ):
     band_rows, band_cols, channels = ocean_state.shape
     keep_mask = land_sea.astype(jnp.float32)[:, :, None]
-    masked32 = ocean_state.astype(jnp.float32) * keep_mask
     keep_wide = jnp.broadcast_to(keep_mask, ocean_state.shape).astype(jnp.bfloat16)
-    conv_out = halo_correlate(masked32, kernel, conv_bias, True, 0)
+    conv_out = halo_correlate(ocean_state, kernel, conv_bias, True, 0, mask=keep_wide)
     result, conv_grad = pointwise(
         conv_out,
         ocean_state,

time: 51.5 us -> 49 us (0.951)
  other arithmetic: 3.3 us -> 0.72 us
    mul x1 -> x0, other arithmetic: 2.58 us -> none  [body(): masked32 = ocean_state.astype(jnp.float32) * keep_mask]
    broadcast_in_dim x0 -> x1, local copies, waits for them, and re-layouts: none -> 1.25 us  [body(): jnp.broadcast_to(keep_mask, ocean_state.shape).astype(jnp.bfloat16)]
    mul x1 -> x0, local copies, waits for them, and re-layouts: 1.25 us -> none  [body(): masked32 = ocean_state.astype(jnp.float32) * keep_mask]
where the time goes in v13:
time: 49 us; the launch traced here: 48.7 us
  Pallas kernels  44 us (90%)
  local copies, waits for them, and re-layouts  3.32 us (7%)
  other arithmetic  0.72 us (1%)
  between operations  0.65 us (1%)
    pallas_call x2, Pallas kernels, halo_correlate(): pl.pallas_call(run, out_shape=jax.ShapeDtypeStruct((rows, cols, chans), j...  36 us
    pallas_call x1, Pallas kernels, pointwise(): pl.pallas_call(run, grid=(band_rows // tile,), out_shape=(jax.ShapeDtypeS...  7.97 us
    unnamed x1, local copies, waits for them, and re-layouts  1.97 us
    broadcast_in_dim x1, local copies, waits for them, and re-layouts, body(): jnp.broadcast_to(keep_mask, ocean_state.shape).astype(jnp.bfloat16)  1.25 us

profile of v13, /device:TPU:1, one launch (start us, length us, event | category | flops | bytes accessed | tf_op | source)
XLA Modules:
  0.0 48.7 jit_solution(323387276061663889)
XLA Ops:
  0.6 0.7 %convert_convert_fusion = bf16[80,32]{0,1:T(8,128)(2,1)S(1)} fusion(s32[80,32]{0,1:T(8,128)} %param.13), kind=kLoop, calls=%fused_computation | loop fusion | flops 5120 | bytes 15360 | tf_op jit(solution)/shard_map/convert_element_type | solution.py:335
  1.4 0.1 copy.14
  1.5 1.2 %broadcast_in_dim.2.refs_1_.m_ref.refs_3_ = bf16[80,32,128]{2,1,0:T(8,128)(2,1)} broadcast(bf16[80,32]{1,0:T(8,128)(2,1)S(1)} %copy.14), dimensions={0,1} | broadcast | bytes 660480 | tf_op jit(solution)/shard_map/broadcast_in_dim | solution.py:335
  2.7 20.0 %shard_map.131.c_ref = f32[80,32,128]{2,1,0:T(8,128)} custom-call(bf16[80,32,128]{2,1,0:T(8,128)(2,1)} %s_ref.1, bf16[80,32,128]{2,1,0:T(8,128)(2,1)} %broadcast_in_dim.2.refs_1_.m_ref.refs_3_, bf16[7,7,128]{2,1,0:T(8,128)(2,1)} %refs_1_.1, f32[1,128]{1,0:T(1,128)} %bitcast.7), custom_call_target="tpu_custom_call" | custom-call | tf_op jit(solution)/shard_map/pallas_call | solution.py:209
  22.7 8.0 %shard_map.132 = (bf16[80,32,128]{2,1,0:T(8,128)(2,1)}, f32[80,32,128]{2,1,0:T(8,128)}) custom-call(f32[80,32,128]{2,1,0:T(8,128)} %shard_map.131.c_ref, bf16[80,32,128]{2,1,0:T(8,128)(2,1)} %s_ref.1, bf16[80,32,128]{2,1,0:T(8,128)(2,1)} %broadcast_in_dim.2.refs_1_.m_ref.refs_3_, bf16[80,32,128]{2,1,0:T(8,128)(2,1)} %refs_2_.3, f32[1,128]{1,0:T(1,128)} %bitcast.8, ...), custom_call_target="tpu_custom_call" | custom-call | tf_op jit(solution)/shard_map/pallas_call | solution.py:299
  30.7 16.0 %shard_map.133 = bf16[80,32,128]{2,1,0:T(8,128)(2,1)} custom-call(f32[80,32,128]{2,1,0:T(8,128)} %get-tuple-element.5.refs_0_, bf16[7,7,128]{2,1,0:T(8,128)(2,1)} %refs_1_.1, bf16[80,32,128]{2,1,0:T(8,128)(2,1)} %refs_2_.3, bf16[80,32,128]{2,1,0:T(8,128)(2,1)} %broadcast_in_dim.2.refs_1_.m_ref.refs_3_), custom_call_target="tpu_custom_call" | custom-call | tf_op jit(solution)/shard_map/pallas_call | solution.py:209
  46.7 2.0 %copy.16 = bf16[80,32,128]{2,1,0:T(8,128)(2,1)} copy(bf16[80,32,128]{2,1,0:T(8,128)(2,1)} %shard_map.133) | data formatting | bytes 1310720

commit v14 on v13

--- a/solution.py
+++ b/solution.py
@@ -250,7 +250,7 @@
     w_reduce,
     b_reduce,
     layer_scale,
-    tile=40,
+    tile=20,
 ):
     band_rows, band_cols, chans = conv_out.shape
     cells = tile * band_cols

time: 49 us -> 49.5 us (1.010)
  Pallas kernels: 44 us -> 44.5 us
where the time goes in v14:
time: 49.5 us; the launch traced here: 49.2 us
  Pallas kernels  44.5 us (90%)
  local copies, waits for them, and re-layouts  3.32 us (7%)
  other arithmetic  0.72 us (1%)
  between operations  0.65 us (1%)
    pallas_call x2, Pallas kernels, halo_correlate(): pl.pallas_call(run, out_shape=jax.ShapeDtypeStruct((rows, cols, chans), j...  36 us
    pallas_call x1, Pallas kernels, pointwise(): pl.pallas_call(run, grid=(band_rows // tile,), out_shape=(jax.ShapeDtypeS...  8.44 us
    unnamed x1, local copies, waits for them, and re-layouts  1.97 us
    broadcast_in_dim x1, local copies, waits for them, and re-layouts, body(): jnp.broadcast_to(keep_mask, ocean_state.shape).astype(jnp.bfloat16)  1.25 us

profile of v14, /device:TPU:1, one launch (start us, length us, event | category | flops | bytes accessed | tf_op | source)
XLA Modules:
  0.0 49.2 jit_solution(8048662121230493872)
XLA Ops:
  0.6 0.7 %convert_convert_fusion = bf16[80,32]{0,1:T(8,128)(2,1)S(1)} fusion(s32[80,32]{0,1:T(8,128)} %param.13), kind=kLoop, calls=%fused_computation | loop fusion | flops 5120 | bytes 15360 | tf_op jit(solution)/shard_map/convert_element_type | solution.py:335
  1.4 0.1 copy.14
  1.5 1.2 %broadcast_in_dim.2.refs_1_.m_ref.refs_3_ = bf16[80,32,128]{2,1,0:T(8,128)(2,1)} broadcast(bf16[80,32]{1,0:T(8,128)(2,1)S(1)} %copy.14), dimensions={0,1} | broadcast | bytes 660480 | tf_op jit(solution)/shard_map/broadcast_in_dim | solution.py:335
  2.7 20.0 %shard_map.131.c_ref = f32[80,32,128]{2,1,0:T(8,128)} custom-call(bf16[80,32,128]{2,1,0:T(8,128)(2,1)} %s_ref.1, bf16[80,32,128]{2,1,0:T(8,128)(2,1)} %broadcast_in_dim.2.refs_1_.m_ref.refs_3_, bf16[7,7,128]{2,1,0:T(8,128)(2,1)} %refs_1_.1, f32[1,128]{1,0:T(1,128)} %bitcast.7), custom_call_target="tpu_custom_call" | custom-call | tf_op jit(solution)/shard_map/pallas_call | solution.py:209
  22.7 8.4 %shard_map.132 = (bf16[80,32,128]{2,1,0:T(8,128)(2,1)}, f32[80,32,128]{2,1,0:T(8,128)}) custom-call(f32[80,32,128]{2,1,0:T(8,128)} %shard_map.131.c_ref, bf16[80,32,128]{2,1,0:T(8,128)(2,1)} %s_ref.1, bf16[80,32,128]{2,1,0:T(8,128)(2,1)} %broadcast_in_dim.2.refs_1_.m_ref.refs_3_, bf16[80,32,128]{2,1,0:T(8,128)(2,1)} %refs_2_.3, f32[1,128]{1,0:T(1,128)} %bitcast.8, ...), custom_call_target="tpu_custom_call" | custom-call | tf_op jit(solution)/shard_map/pallas_call | solution.py:299
  31.2 16.0 %shard_map.133 = bf16[80,32,128]{2,1,0:T(8,128)(2,1)} custom-call(f32[80,32,128]{2,1,0:T(8,128)} %get-tuple-element.5.refs_0_, bf16[7,7,128]{2,1,0:T(8,128)(2,1)} %refs_1_.1, bf16[80,32,128]{2,1,0:T(8,128)(2,1)} %refs_2_.3, bf16[80,32,128]{2,1,0:T(8,128)(2,1)} %broadcast_in_dim.2.refs_1_.m_ref.refs_3_), custom_call_target="tpu_custom_call" | custom-call | tf_op jit(solution)/shard_map/pallas_call | solution.py:209
  47.2 2.0 %copy.16 = bf16[80,32,128]{2,1,0:T(8,128)(2,1)} copy(bf16[80,32,128]{2,1,0:T(8,128)(2,1)} %shard_map.133) | data formatting | bytes 1310720

commit v15 on v13

--- a/solution.py
+++ b/solution.py
@@ -9,7 +9,7 @@
 MESH = pl.DeviceIdType.MESH
 
 
-def correlate_into(src, taps, bias, o_ref, first_row, count, col_tiles, block=16,
+def correlate_into(src, taps, bias, o_ref, first_row, count, col_tiles, block=24,
                    col_taps=tuple(range(7)), accumulate=False):
     chans = o_ref.shape[-1]
     block = min(block, count)

time: 49 us -> 48.8 us (level)
  no operation moved by 1% of the time
where the time goes in v15:
time: 48.8 us; the launch traced here: 48.5 us
  Pallas kernels  43.8 us (90%)
  local copies, waits for them, and re-layouts  3.32 us (7%)
  other arithmetic  0.72 us (1%)
  between operations  0.65 us (1%)
    pallas_call x2, Pallas kernels, halo_correlate(): pl.pallas_call(run, out_shape=jax.ShapeDtypeStruct((rows, cols, chans), j...  35.9 us
    pallas_call x1, Pallas kernels, pointwise(): pl.pallas_call(run, grid=(band_rows // tile,), out_shape=(jax.ShapeDtypeS...  7.97 us
    unnamed x1, local copies, waits for them, and re-layouts  1.97 us
    broadcast_in_dim x1, local copies, waits for them, and re-layouts, body(): jnp.broadcast_to(keep_mask, ocean_state.shape).astype(jnp.bfloat16)  1.25 us

profile of v15, /device:TPU:1, one launch (start us, length us, event | category | flops | bytes accessed | tf_op | source)
XLA Modules:
  0.0 48.5 jit_solution(5780232192300591162)
XLA Ops:
  0.6 0.7 %convert_convert_fusion = bf16[80,32]{0,1:T(8,128)(2,1)S(1)} fusion(s32[80,32]{0,1:T(8,128)} %param.13), kind=kLoop, calls=%fused_computation | loop fusion | flops 5120 | bytes 15360 | tf_op jit(solution)/shard_map/convert_element_type | solution.py:335
  1.4 0.1 copy.14
  1.5 1.2 %broadcast_in_dim.2.refs_1_.m_ref.refs_3_ = bf16[80,32,128]{2,1,0:T(8,128)(2,1)} broadcast(bf16[80,32]{1,0:T(8,128)(2,1)S(1)} %copy.14), dimensions={0,1} | broadcast | bytes 660480 | tf_op jit(solution)/shard_map/broadcast_in_dim | solution.py:335
  2.7 19.9 %shard_map.131.c_ref = f32[80,32,128]{2,1,0:T(8,128)} custom-call(bf16[80,32,128]{2,1,0:T(8,128)(2,1)} %s_ref.1, bf16[80,32,128]{2,1,0:T(8,128)(2,1)} %broadcast_in_dim.2.refs_1_.m_ref.refs_3_, bf16[7,7,128]{2,1,0:T(8,128)(2,1)} %refs_1_.1, f32[1,128]{1,0:T(1,128)} %bitcast.7), custom_call_target="tpu_custom_call" | custom-call | tf_op jit(solution)/shard_map/pallas_call | solution.py:209
  22.6 8.0 %shard_map.132 = (bf16[80,32,128]{2,1,0:T(8,128)(2,1)}, f32[80,32,128]{2,1,0:T(8,128)}) custom-call(f32[80,32,128]{2,1,0:T(8,128)} %shard_map.131.c_ref, bf16[80,32,128]{2,1,0:T(8,128)(2,1)} %s_ref.1, bf16[80,32,128]{2,1,0:T(8,128)(2,1)} %broadcast_in_dim.2.refs_1_.m_ref.refs_3_, bf16[80,32,128]{2,1,0:T(8,128)(2,1)} %refs_2_.3, f32[1,128]{1,0:T(1,128)} %bitcast.8, ...), custom_call_target="tpu_custom_call" | custom-call | tf_op jit(solution)/shard_map/pallas_call | solution.py:299
  30.6 16.0 %shard_map.133 = bf16[80,32,128]{2,1,0:T(8,128)(2,1)} custom-call(f32[80,32,128]{2,1,0:T(8,128)} %get-tuple-element.5.refs_0_, bf16[7,7,128]{2,1,0:T(8,128)(2,1)} %refs_1_.1, bf16[80,32,128]{2,1,0:T(8,128)(2,1)} %refs_2_.3, bf16[80,32,128]{2,1,0:T(8,128)(2,1)} %broadcast_in_dim.2.refs_1_.m_ref.refs_3_), custom_call_target="tpu_custom_call" | custom-call | tf_op jit(solution)/shard_map/pallas_call | solution.py:209
  46.6 2.0 %copy.16 = bf16[80,32,128]{2,1,0:T(8,128)(2,1)} copy(bf16[80,32,128]{2,1,0:T(8,128)(2,1)} %shard_map.133) | data formatting | bytes 1310720

commit v16 on v15

--- a/solution.py
+++ b/solution.py
@@ -9,7 +9,7 @@
 MESH = pl.DeviceIdType.MESH
 
 
-def correlate_into(src, taps, bias, o_ref, first_row, count, col_tiles, block=24,
+def correlate_into(src, taps, bias, o_ref, first_row, count, col_tiles, block=32,
                    col_taps=tuple(range(7)), accumulate=False):
     chans = o_ref.shape[-1]
     block = min(block, count)

time: 48.8 us -> 48.7 us (level)
  no operation moved by 1% of the time
where the time goes in v16:
time: 48.7 us; the launch traced here: 48.4 us
  Pallas kernels  43.7 us (90%)
  local copies, waits for them, and re-layouts  3.32 us (7%)
  other arithmetic  0.72 us (1%)
  between operations  0.65 us (1%)
    pallas_call x2, Pallas kernels, halo_correlate(): pl.pallas_call(run, out_shape=jax.ShapeDtypeStruct((rows, cols, chans), j...  35.7 us
    pallas_call x1, Pallas kernels, pointwise(): pl.pallas_call(run, grid=(band_rows // tile,), out_shape=(jax.ShapeDtypeS...  7.97 us
    unnamed x1, local copies, waits for them, and re-layouts  1.97 us
    broadcast_in_dim x1, local copies, waits for them, and re-layouts, body(): jnp.broadcast_to(keep_mask, ocean_state.shape).astype(jnp.bfloat16)  1.25 us

profile of v16, /device:TPU:1, one launch (start us, length us, event | category | flops | bytes accessed | tf_op | source)
XLA Modules:
  0.0 48.4 jit_solution(9914872884337158311)
XLA Ops:
  0.6 0.7 %convert_convert_fusion = bf16[80,32]{0,1:T(8,128)(2,1)S(1)} fusion(s32[80,32]{0,1:T(8,128)} %param.13), kind=kLoop, calls=%fused_computation | loop fusion | flops 5120 | bytes 15360 | tf_op jit(solution)/shard_map/convert_element_type | solution.py:335
  1.4 0.1 copy.14
  1.5 1.2 %broadcast_in_dim.2.refs_1_.m_ref.refs_3_ = bf16[80,32,128]{2,1,0:T(8,128)(2,1)} broadcast(bf16[80,32]{1,0:T(8,128)(2,1)S(1)} %copy.14), dimensions={0,1} | broadcast | bytes 660480 | tf_op jit(solution)/shard_map/broadcast_in_dim | solution.py:335
  2.7 19.8 %shard_map.131.c_ref = f32[80,32,128]{2,1,0:T(8,128)} custom-call(bf16[80,32,128]{2,1,0:T(8,128)(2,1)} %s_ref.1, bf16[80,32,128]{2,1,0:T(8,128)(2,1)} %broadcast_in_dim.2.refs_1_.m_ref.refs_3_, bf16[7,7,128]{2,1,0:T(8,128)(2,1)} %refs_1_.1, f32[1,128]{1,0:T(1,128)} %bitcast.7), custom_call_target="tpu_custom_call" | custom-call | tf_op jit(solution)/shard_map/pallas_call | solution.py:209
  22.5 8.0 %shard_map.132 = (bf16[80,32,128]{2,1,0:T(8,128)(2,1)}, f32[80,32,128]{2,1,0:T(8,128)}) custom-call(f32[80,32,128]{2,1,0:T(8,128)} %shard_map.131.c_ref, bf16[80,32,128]{2,1,0:T(8,128)(2,1)} %s_ref.1, bf16[80,32,128]{2,1,0:T(8,128)(2,1)} %broadcast_in_dim.2.refs_1_.m_ref.refs_3_, bf16[80,32,128]{2,1,0:T(8,128)(2,1)} %refs_2_.3, f32[1,128]{1,0:T(1,128)} %bitcast.8, ...), custom_call_target="tpu_custom_call" | custom-call | tf_op jit(solution)/shard_map/pallas_call | solution.py:299
  30.5 15.9 %shard_map.133 = bf16[80,32,128]{2,1,0:T(8,128)(2,1)} custom-call(f32[80,32,128]{2,1,0:T(8,128)} %get-tuple-element.5.refs_0_, bf16[7,7,128]{2,1,0:T(8,128)(2,1)} %refs_1_.1, bf16[80,32,128]{2,1,0:T(8,128)(2,1)} %refs_2_.3, bf16[80,32,128]{2,1,0:T(8,128)(2,1)} %broadcast_in_dim.2.refs_1_.m_ref.refs_3_), custom_call_target="tpu_custom_call" | custom-call | tf_op jit(solution)/shard_map/pallas_call | solution.py:209
  46.4 2.0 %copy.16 = bf16[80,32,128]{2,1,0:T(8,128)(2,1)} copy(bf16[80,32,128]{2,1,0:T(8,128)(2,1)} %shard_map.133) | data formatting | bytes 1310720
